TPU v7x, 32 devices: a whole 2x2x4 slice. The times are simulated.
32 devices in a mesh: tm: 8 (over z, x), pack: 4 (over y, core).
Axes of the slice: x: 2, y: 2, z: 4, core: 2. Of those that a mesh axis runs over, the one named last changes fastest.
Arguments:
- queries: bfloat16 [4, 4096, 1024], P('pack', 'tm'), may hold values from -8 to 8
- keys: bfloat16 [4, 4096, 1024], P('pack', 'tm'), may hold values from -8 to 8
- values: bfloat16 [4, 4096, 1024], P('pack', 'tm'), may hold values from -6 to 6
- w_out: bfloat16 [1024, 1024], replicated, may hold values from -0.1875 to 0.1875
- norm_gain: float32 [1024], replicated, may hold values from 0.1 to 1.9
- block_owner: int32 [4, 32, 1], P('pack', 'tm'), may hold values from 0 to 3; in each aligned block of 4 rows (0 to 3, 4 to 7, ..., all dimensions but the last counted through in order) at most 2 rows name the same one
- block_base: int32 [4, 32], P('pack', 'tm'), may hold values from 0 to 112
- frame_offset: int32 [4, 32, 128], P('pack', 'tm'), may hold values from 0 to 15, never falling along the last dimension, each value on 1 to 16 neighbouring positions
Outputs:
- encoded: bfloat16 [4, 4096, 1024], P('pack', 'tm')
- pooled: bfloat16 [4, 1024, 1024], P('pack', 'tm')
Inputs may be any that keep to these rules, and one draw needn't show every extreme that they name: `block_owner`: among the 4 blocks of one device (aligned runs of the list), at most 2 name the same owner. `frame_offset`: within each block of 128 frames the offsets never fall and each of 0 to 15 occurs.
All inputs are finite; a program needn't handle non-finite values.
Results may differ from a plain program's by a relative error of at most 0.008.
Values may be sent and summed in bfloat16 or wider, within the bound.
No kernel may reach another device: no remote copies, remote signals or barrier semaphores. Data moves between devices by JAX's collectives and lax.ppermute only.
A program may use at most 128 MiB of HBM per device.

v0:
```python
import functools
import math

import jax
import jax.numpy as jnp
from jax import lax
from jax.experimental import pallas as pl
from jax.experimental.pallas import tpu as pltpu
from jax.sharding import PartitionSpec as P


HEADS = 16
LANDMARKS = 256
BLOCK = 128
POOL_DEV = 128
WINDOW = 16
LANES = 128
ONES = 16
SLOTS = 2
META = 16
QUERY_BLOCK = 256
BF16 = jnp.bfloat16
F32 = jnp.float32


ANY = pl.BlockSpec(memory_space=pl.ANY)
HBM = pl.BlockSpec(memory_space=pltpu.HBM)
VMEM = pl.BlockSpec(memory_space=pltpu.VMEM)
SMEM = pl.BlockSpec(memory_space=pltpu.SMEM)


def dot(a, b):
    return jnp.dot(a, b, preferred_element_type=F32)


def marks_kernel(team, streams, head_dim, q_hbm, k_hbm, v_hbm, *refs):
    frames = q_hbm.shape[0]
    strips = team * streams
    near, far = refs[:strips], refs[strips : 2 * strips]
    packs, ins, score_a, score_b, in_sems, out_sems = refs[2 * strips :]
    me = lax.axis_index("tm") % team
    span = frames // LANDMARKS
    strip_heads = LANES // head_dim
    scale = head_dim**-0.5 * math.log2(math.e)
    loads = []
    for i in range(strips):
        stream, d = divmod(i, team)
        column = pl.multiple_of((jnp.bitwise_xor(me, d) * streams + stream) * LANES, LANES)
        columns = pl.ds(column, LANES)
        three = [
            pltpu.make_async_copy(q_hbm.at[:, columns], packs.at[i, pl.ds(0, frames)], in_sems.at[i, 0]),
            pltpu.make_async_copy(k_hbm.at[:, columns], ins.at[i, 0], in_sems.at[i, 1]),
            pltpu.make_async_copy(v_hbm.at[:, columns], ins.at[i, 1], in_sems.at[i, 2]),
        ]
        for load in three:
            load.start()
        loads.append(three)
    row = lax.broadcasted_iota(jnp.int32, (LANDMARKS, frames), 0)
    frame = lax.broadcasted_iota(jnp.int32, (LANDMARKS, frames), 1)
    member = ((frame >= row * span) & (frame < (row + 1) * span)).astype(BF16)
    lane_row = lax.broadcasted_iota(jnp.int32, (LANES, LANDMARKS), 0)
    ones = jnp.ones((ONES, frames), BF16)
    scores = (score_a, score_b)
    stores = []

    def prepare(i):
        for load in loads[i]:
            load.wait()
        mark_q = (dot(member, packs[i, pl.ds(0, frames)]) * (1.0 / span)).astype(BF16).astype(F32).T
        mark_k = (dot(member, ins[i, 0]) * (1.0 / span)).astype(BF16)
        packs[i, pl.ds(frames, LANDMARKS)] = mark_k
        return mark_q, ins[i, 1].astype(F32).T.astype(BF16)

    def score(i, h, slot, mark_q):
        low = h * head_dim
        own = jnp.where((lane_row >= low) & (lane_row < low + head_dim), mark_q, 0.0).astype(BF16)
        part = dot(ins[i, 0], own)
        scores[slot][...] = part
        return jnp.max(part, axis=0, keepdims=True)

    items = [(i, h) for i in range(strips) for h in range(strip_heads)]
    mark_q, v_next = prepare(0)
    top, heads = score(0, 0, 0, mark_q), []
    for n, (i, h) in enumerate(items):
        slot, most, v_t = n % 2, top, v_next
        if n + 1 < len(items):
            j, g = items[n + 1]
            if g == 0:
                mark_q, v_next = prepare(j)
            top = score(j, g, 1 - slot, mark_q)
        weights = jnp.exp2((scores[slot][...] - most) * scale).astype(BF16)
        mixed = dot(jnp.concatenate([v_t[h * head_dim : (h + 1) * head_dim], ones], axis=0), weights)
        heads.append(mixed[:head_dim] / mixed[head_dim : head_dim + 1])
        if h < strip_heads - 1:
            continue
        mark_v, heads = jnp.concatenate(heads, axis=0).astype(BF16), []
        for part in range(LANDMARKS // LANES):
            rows = pl.ds(frames + LANDMARKS + part * LANES, LANES)
            packs[i, rows] = mark_v[:, part * LANES : (part + 1) * LANES]
        two = [
            pltpu.make_async_copy(packs.at[i], near[i], out_sems.at[i, 0]),
            pltpu.make_async_copy(packs.at[i, pl.ds(frames, 2 * LANDMARKS)], far[i], out_sems.at[i, 1]),
        ]
        for store in two:
            store.start()
        stores += two
    for store in stores:
        store.wait()


def mark_strips(q, k, v, team, streams, head_dim):
    frames = q.shape[0]
    strips = team * streams
    near = jax.ShapeDtypeStruct((frames + 2 * LANDMARKS, LANES), BF16)
    far = jax.ShapeDtypeStruct((2 * LANDMARKS, LANES), BF16)
    out = pl.pallas_call(
        functools.partial(marks_kernel, team, streams, head_dim),
        out_shape=[near] * strips + [far] * strips,
        in_specs=[HBM] * 3,
        out_specs=[ANY] * (2 * strips),
        scratch_shapes=[
            pltpu.VMEM((strips, frames + 2 * LANDMARKS, LANES), BF16),
            pltpu.VMEM((strips, 2, frames, LANES), BF16),
            pltpu.VMEM((frames, LANDMARKS), F32),
            pltpu.VMEM((frames, LANDMARKS), F32),
            pltpu.SemaphoreType.DMA((strips, 3)),
            pltpu.SemaphoreType.DMA((strips, 2)),
        ],
        compiler_params=pltpu.CompilerParams(vmem_limit_bytes=60 << 20),
        name="marks",
    )(q, k, v)
    return out[:strips], out[strips:]


def mix_kernel(team, sources, frames, head_dim, *refs):
    near, far = refs[:team], refs[team:sources]
    outs = refs[sources : sources + team]
    queries, mark_keys, mark_values, mixed_all, weight_a, weight_b, scores, sems = refs[sources + team :]
    strip_heads = LANES // head_dim
    all_marks = sources * LANDMARKS
    scale = head_dim**-0.5 * math.log2(math.e)
    copies = []
    for s in range(sources):
        ref, base = (near[s], frames) if s < team else (far[s - team], 0)
        pairs = [(ref.at[pl.ds(base, LANDMARKS)], mark_keys.at[pl.ds(s * LANDMARKS, LANDMARKS)])]
        if s < team:
            pairs.append((ref.at[pl.ds(0, frames)], queries.at[s]))
        for part in range(LANDMARKS // LANES):
            for h in range(strip_heads):
                rows = pl.ds(base + LANDMARKS + part * LANES + h * head_dim, head_dim)
                columns = pl.ds(s * LANDMARKS + part * LANES, LANES)
                pairs.append((ref.at[rows], mark_values.at[h, pl.ds(0, head_dim), columns]))
        for source, target in pairs:
            copies.append(pltpu.make_async_copy(source, target, sems.at[len(copies)]))
            copies[-1].start()
    for h in range(strip_heads):
        mark_values[h, pl.ds(head_dim, ONES)] = jnp.ones((ONES, all_marks), BF16)
    for copy in copies:
        copy.wait()
    lane = lax.broadcasted_iota(jnp.int32, (QUERY_BLOCK, LANES), 1)
    chunk = math.gcd(all_marks, 512)
    chunks = all_marks // chunk
    blocks = frames // QUERY_BLOCK
    weights = (weight_a, weight_b)
    items = [(d, b, h) for d in range(team) for b in range(blocks) for h in range(strip_heads)]

    def own_queries(rows, h):
        own = (lane >= h * head_dim) & (lane < (h + 1) * head_dim)
        return jnp.where(own, rows.astype(F32), 0.0).T.astype(BF16)

    least, most = jnp.full((1, QUERY_BLOCK), 1.0, F32), jnp.full((1, QUERY_BLOCK), 1.0, F32)
    heads = []
    for i in range(len(items) + 1):
        if i < len(items):
            d, b, h = items[i]
            query = own_queries(queries[d, pl.ds(b * QUERY_BLOCK, QUERY_BLOCK)], h)
        for c in range(chunks):
            rows = pl.ds(c * chunk, chunk)
            if i < len(items):
                weights[i % 2][rows] = jnp.exp2(dot(mark_keys[rows], query) * scale).astype(BF16)
            if i > 0:
                part = dot(mark_values[items[i - 1][2], :, rows], weights[1 - i % 2][rows])
                mixed = part if c == 0 else mixed + part
        if i == 0:
            continue
        d, b, h = items[i - 1]
        total = mixed[head_dim : head_dim + 1]
        least, most = jnp.minimum(least, total), jnp.maximum(most, total)
        heads.append(mixed[:head_dim] / total)
        if h == strip_heads - 1:
            mixed_all[d, pl.ds(b * QUERY_BLOCK, QUERY_BLOCK)] = jnp.concatenate(heads, axis=0).T.astype(BF16)
            heads = []
    unsafe = jnp.sum(jnp.where((least > 2.0**-40) & (most < 2.0**100), 0, 1))

    @pl.when(unsafe > 0)
    def _():
        def exact(i, carry):
            d, b = i // blocks, i % blocks
            block = pl.ds(pl.multiple_of(b * QUERY_BLOCK, QUERY_BLOCK), QUERY_BLOCK)
            parts = []
            for h in range(strip_heads):
                query = own_queries(queries[d, block], h)

                def score(c, top):
                    rows = pl.ds(pl.multiple_of(c * chunk, chunk), chunk)
                    part = dot(mark_keys[rows], query)
                    scores[rows] = part
                    return jnp.maximum(top, jnp.max(part, axis=0, keepdims=True))

                top = lax.fori_loop(0, chunks, score, jnp.full((1, QUERY_BLOCK), -jnp.inf, F32))

                def weigh(c, total):
                    rows = pl.ds(pl.multiple_of(c * chunk, chunk), chunk)
                    weight_a[rows] = jnp.exp2((scores[rows] - top) * scale).astype(BF16)
                    return total

                lax.fori_loop(0, chunks, weigh, 0)
                mixed = dot(mark_values[h], weight_a[...])
                parts.append(mixed[:head_dim] / mixed[head_dim : head_dim + 1])
            mixed_all[d, block] = jnp.concatenate(parts, axis=0).T.astype(BF16)
            return carry

        lax.fori_loop(0, team * blocks, exact, 0)

    for d in range(team):
        outs[d][...] = mixed_all[d]


def mix_strips(near, far, frames, head_dim):
    team, sources = len(near), len(near) + len(far)
    all_marks, strip_heads = sources * LANDMARKS, LANES // head_dim
    copies = sources * (1 + strip_heads * LANDMARKS // LANES) + team
    return pl.pallas_call(
        functools.partial(mix_kernel, team, sources, frames, head_dim),
        out_shape=[jax.ShapeDtypeStruct((frames, LANES), BF16)] * team,
        in_specs=[ANY] * sources,
        out_specs=[VMEM] * team,
        scratch_shapes=[
            pltpu.VMEM((team, frames, LANES), BF16),
            pltpu.VMEM((all_marks, LANES), BF16),
            pltpu.VMEM((strip_heads, head_dim + ONES, all_marks), BF16),
            pltpu.VMEM((team, frames, LANES), BF16),
            pltpu.VMEM((all_marks, QUERY_BLOCK), BF16),
            pltpu.VMEM((all_marks, QUERY_BLOCK), BF16),
            pltpu.VMEM((all_marks, QUERY_BLOCK), F32),
            pltpu.SemaphoreType.DMA((copies,)),
        ],
        compiler_params=pltpu.CompilerParams(vmem_limit_bytes=32 << 20),
    )(*near, *far)


def finish_kernel(team, streams, packs, blocks, owners, bases, offsets, w_out, gain, *refs):
    strips = refs[: team * streams]
    encoded = refs[team * streams]
    sends = refs[team * streams + 1 :]
    me = lax.axis_index("tm") % team
    my_pack = lax.axis_index("pack")
    width = streams * LANES
    model = w_out.shape[1]
    slots = packs * SLOTS * WINDOW
    owner = [owners[b, 0] for b in range(blocks)]
    starts = []
    for b in range(blocks):
        rank = jnp.int32(0)
        for a in range(b):
            rank = rank + jnp.where(owner[a] == owner[b], 1, 0)
        starts.append((jnp.bitwise_xor(owner[b], my_pack) * SLOTS + rank) * WINDOW)
    slot_row = lax.broadcasted_iota(jnp.int32, (slots, BLOCK), 0)
    slot_lane = lax.broadcasted_iota(jnp.int32, (1, slots), 1)
    hits, rows_to = [], jnp.zeros((1, slots), jnp.int32)
    for b in range(blocks):
        hits.append((slot_row == offsets[pl.ds(b, 1)] + starts[b]).astype(F32).astype(BF16))
        step = slot_lane - starts[b]
        rows_to = rows_to + jnp.where((step >= 0) & (step < WINDOW), step + (bases[0, b] + 1), 0)
    hit = jnp.concatenate(hits, axis=1)
    frame_counts = lax.dot_general(
        jnp.ones((META, blocks * BLOCK), BF16), hit, (((1,), (1,)), ((), ())), preferred_element_type=F32
    )
    for b in range(blocks):
        rows = pl.ds(b * BLOCK, BLOCK)
        projected = None
        for d in range(team):
            strip = jnp.concatenate([strips[s * team + d][rows] for s in range(streams)], axis=1)
            first = pl.multiple_of(jnp.bitwise_xor(me, d) * width, LANES)
            part = dot(strip, w_out[pl.ds(first, width)])
            projected = part if projected is None else projected + part
        power = jnp.mean(projected * projected, axis=-1, keepdims=True)
        encoded[rows] = (projected * lax.rsqrt(power + 1e-06) * gain[...]).astype(BF16)
    sums = dot(hit, encoded[...]).astype(BF16)
    meta_row = lax.broadcasted_iota(jnp.int32, (META, slots), 0)
    meta = jnp.where(meta_row == 0, rows_to.astype(F32), jnp.where(meta_row == 1, frame_counts, 0.0))
    part = SLOTS * WINDOW
    for e in range(packs):
        sends[e][pl.ds(0, part)] = sums[e * part : (e + 1) * part]
        sends[e][pl.ds(part, META)] = jnp.zeros((META, model), BF16)
        sends[e][pl.ds(part, META), pl.ds(0, slots)] = meta.astype(BF16)


def finish(strips, w_out, gain, owners, bases, offsets, team, streams, packs):
    frames, model = strips[0].shape[0], w_out.shape[1]
    blocks = owners.shape[0]
    send = jax.ShapeDtypeStruct((SLOTS * WINDOW + META, model), BF16)
    out = pl.pallas_call(
        functools.partial(finish_kernel, team, streams, packs, blocks),
        out_shape=[jax.ShapeDtypeStruct((frames, model), BF16)] + [send] * packs,
        in_specs=[SMEM, SMEM] + [VMEM] * (3 + len(strips)),
        out_specs=[VMEM] * (1 + packs),
        compiler_params=pltpu.CompilerParams(vmem_limit_bytes=24 << 20),
        name="finish",
    )(owners, bases, offsets, w_out, gain, *strips)
    return out[0], out[1:]


def pool_kernel(packs, *refs):
    got, pooled = refs[:packs], refs[packs]
    part = SLOTS * WINDOW
    slots = packs * part
    lane = lax.broadcasted_iota(jnp.int32, (1, slots), 1)
    rows_to, counts = jnp.zeros((1, slots), F32), jnp.zeros((1, slots), F32)
    for e in range(packs):
        meta = got[e][pl.ds(part, META), pl.ds(0, slots)].astype(F32)
        mine = (lane >= e * part) & (lane < (e + 1) * part)
        rows_to = jnp.where(mine, meta[0:1], rows_to)
        counts = jnp.where(mine, meta[1:2], counts)
    row = lax.broadcasted_iota(jnp.int32, (POOL_DEV, slots), 0)
    place = row + 1 == rows_to.astype(jnp.int32)
    total = jnp.sum(jnp.where(place, counts, 0.0), axis=1, keepdims=True)
    rows = jnp.concatenate([got[e][pl.ds(0, part)] for e in range(packs)], axis=0)
    sums = dot(place.astype(F32).astype(BF16), rows)
    pooled[...] = (sums / jnp.maximum(total, 1.0)).astype(BF16)


def pool(got):
    return pl.pallas_call(
        functools.partial(pool_kernel, len(got)),
        out_shape=jax.ShapeDtypeStruct((POOL_DEV, got[0].shape[1]), BF16),
        in_specs=[VMEM] * len(got),
        out_specs=VMEM,
        compiler_params=pltpu.CompilerParams(vmem_limit_bytes=8 << 20),
        name="pool",
    )(*got)


def swap(array, axis, size, bits):
    return lax.ppermute(array, axis, [(i, i ^ bits) for i in range(size)])


def local(team, queries, keys, values, w_out, norm_gain, block_owner, block_base, frame_offset):
    q, k, v = queries[0], keys[0], values[0]
    frames, model = q.shape
    tm, packs = lax.axis_size("tm"), lax.axis_size("pack")
    head_dim = model // HEADS
    streams = model // team // LANES
    near_out, far_out = mark_strips(q, k, v, team, streams, head_dim)
    strips = []
    for s in range(streams):
        mine = range(s * team, (s + 1) * team)
        far = [
            swap(far_out[i], "tm", tm, other + d)
            for other in range(team, tm, team)
            for d, i in enumerate(mine)
        ]
        near = [near_out[s * team]]
        near += [swap(near_out[mine[d]], "tm", tm, d) for d in range(1, team)]
        mixed = mix_strips(near, far, frames, head_dim)
        strips += [mixed[0]] + [swap(mixed[d], "tm", tm, d) for d in range(1, team)]
    encoded, sends = finish(
        strips, w_out, norm_gain[None], block_owner[0], block_base, frame_offset[0], team, streams, packs
    )
    got = [sends[0]] + [swap(sends[e], "pack", packs, e) for e in range(1, packs)]
    return encoded[None], pool(got)[None]


def solution(mesh):
    tm = mesh.shape["tm"]
    team = tm // 2
    return jax.shard_map(
        functools.partial(local, team),
        mesh=mesh,
        in_specs=(
            P("pack", "tm", None),
            P("pack", "tm", None),
            P("pack", "tm", None),
            P(),
            P(),
            P("pack", "tm", None),
            P("pack", "tm"),
            P("pack", "tm", None),
        ),
        out_specs=(P("pack", "tm", None), P("pack", "tm", None)),
        check_vma=False,
    )
```

profile of v0, /device:TPU:0, one launch (start us, length us, event | category | flops | bytes accessed | tf_op | source)
XLA Modules:
  0.0 152.3 jit_solution(5816150237673419793)
XLA Ops:
  0.7 9.0 %marks.1 = (bf16[1024,128]{1,0:T(8,128)(2,1)}, bf16[1024,128]{1,0:T(8,128)(2,1)}, bf16[1024,128]{1,0:T(8,128)(2,1)}, bf16[1024,128]{1,0:T(8,128)(2,1)}, bf16[102...) custom-call(bf16[512,1024]{1,0:T(8,128)(2,1)} %bitcast.10, ...), custom_call_target="tpu_custom_call" | custom-call | tf_op jit(solution)/shard_map/marks/pallas_call | solution.py:116
  9.6 0.0 copy-start
  9.7 4.1 %collective-permute-start.13 = (bf16[512,128]{1,0:T(8,128)(2,1)}, bf16[512,128]{1,0:T(8,128)(2,1)S(1)}, u32[]{:S(2)}, u32[]{:S(2)}) collective-permute-start(bf16[512,128]{1,0:T(8,128)(2,1)} %get-tuple-element.47), channel_id=1, source_target_pairs={{0,16},{4,20},{8,24},{12,28},{16,0},{20,4},{24,8},{28,12},{1,17},{... | collective-permute-start | bytes 393224 | tf_op jit(solution)/shard_map/ppermute | solution.py:345
  13.8 1.3 collective-permute-start.14
  15.0 3.6 %collective-permute-start.15 = (bf16[512,128]{1,0:T(8,128)(2,1)}, bf16[512,128]{1,0:T(8,128)(2,1)S(1)}, u32[]{:S(2)}, u32[]{:S(2)}) collective-permute-start(bf16[512,128]{1,0:T(8,128)(2,1)} %get-tuple-element.49), channel_id=1, source_target_pairs={{0,24},{4,28},{8,16},{12,20},{16,8},{20,12},{24,0},{28,4},{1,25},{... | collective-permute-start | bytes 393224 | tf_op jit(solution)/shard_map/ppermute | solution.py:345
  18.6 0.0 collective-permute-start.16
  18.7 1.7 %collective-permute-start.10 = (bf16[1024,128]{1,0:T(8,128)(2,1)}, bf16[1024,128]{1,0:T(8,128)(2,1)S(1)}, u32[]{:S(2)}, u32[]{:S(2)}) collective-permute-start(bf16[1024,128]{1,0:T(8,128)(2,1)} %get-tuple-element.44), channel_id=1, source_target_pairs={{0,4},{4,0},{8,12},{12,8},{16,20},{20,16},{24,28},{28,24},{1,5},{5... | collective-permute-start | bytes 786440 | tf_op jit(solution)/shard_map/ppermute | solution.py:345
  20.3 9.3 %collective-permute-done.13.refs_4_ = bf16[512,128]{1,0:T(8,128)(2,1)S(1)} collective-permute-done((bf16[512,128]{1,0:T(8,128)(2,1)}, bf16[512,128]{1,0:T(8,128)(2,1)S(1)}, u32[]{:S(2)}, u32[]{:S(2)}) %collective-permute-start.13) | collective-permute-done | bytes 131104 | tf_op jit(solution)/shard_map/ppermute | solution.py:345
  29.6 0.0 collective-permute-start.11
  29.7 4.0 %collective-permute-done.14.refs_5_ = bf16[512,128]{1,0:T(8,128)(2,1)S(1)} collective-permute-done((bf16[512,128]{1,0:T(8,128)(2,1)}, bf16[512,128]{1,0:T(8,128)(2,1)S(1)}, u32[]{:S(2)}, u32[]{:S(2)}) %collective-permute-start.14) | collective-permute-done | bytes 131104 | tf_op jit(solution)/shard_map/ppermute | solution.py:345
  33.6 0.0 collective-permute-done.15.refs_6_
  33.6 3.5 %collective-permute-start.3 = (bf16[512,128]{1,0:T(8,128)(2,1)}, bf16[512,128]{1,0:T(8,128)(2,1)S(1)}, u32[]{:S(2)}, u32[]{:S(2)}) collective-permute-start(bf16[512,128]{1,0:T(8,128)(2,1)} %get-tuple-element.35), channel_id=1, source_target_pairs={{0,16},{4,20},{8,24},{12,28},{16,0},{20,4},{24,8},{28,12},{1,17},{... | collective-permute-start | bytes 393224 | tf_op jit(solution)/shard_map/ppermute | solution.py:345
  37.1 0.0 collective-permute-done.16.refs_7_
  37.1 4.2 %collective-permute-start.4 = (bf16[512,128]{1,0:T(8,128)(2,1)}, bf16[512,128]{1,0:T(8,128)(2,1)S(1)}, u32[]{:S(2)}, u32[]{:S(2)}) collective-permute-start(bf16[512,128]{1,0:T(8,128)(2,1)} %get-tuple-element.36), channel_id=1, source_target_pairs={{0,20},{4,16},{8,28},{12,24},{16,4},{20,0},{24,12},{28,8},{1,21},{... | collective-permute-start | bytes 393224 | tf_op jit(solution)/shard_map/ppermute | solution.py:345
  41.3 3.8 %collective-permute-done.3.refs_4_ = bf16[512,128]{1,0:T(8,128)(2,1)S(1)} collective-permute-done((bf16[512,128]{1,0:T(8,128)(2,1)}, bf16[512,128]{1,0:T(8,128)(2,1)S(1)}, u32[]{:S(2)}, u32[]{:S(2)}) %collective-permute-start.3) | collective-permute-done | bytes 131104 | tf_op jit(solution)/shard_map/ppermute | solution.py:345
  45.1 1.8 %collective-permute-start = (bf16[1024,128]{1,0:T(8,128)(2,1)}, bf16[1024,128]{1,0:T(8,128)(2,1)S(1)}, u32[]{:S(2)}, u32[]{:S(2)}) collective-permute-start(bf16[1024,128]{1,0:T(8,128)(2,1)} %get-tuple-element.32), channel_id=1, source_target_pairs={{0,4},{4,0},{8,12},{12,8},{16,20},{20,16},{24,28},{28,24},{1,5},{5... | collective-permute-start | bytes 786440 | tf_op jit(solution)/shard_map/ppermute | solution.py:345
  46.9 0.0 collective-permute-done.4.refs_5_
  46.9 5.1 %collective-permute-start.1 = (bf16[1024,128]{1,0:T(8,128)(2,1)}, bf16[1024,128]{1,0:T(8,128)(2,1)S(1)}, u32[]{:S(2)}, u32[]{:S(2)}) collective-permute-start(bf16[1024,128]{1,0:T(8,128)(2,1)} %get-tuple-element.33), channel_id=1, source_target_pairs={{0,8},{4,12},{8,0},{12,4},{16,24},{20,28},{24,16},{28,20},{1,9},{5... | collective-permute-start | bytes 786440 | tf_op jit(solution)/shard_map/ppermute | solution.py:345
  52.0 0.0 collective-permute-done.10.refs_1_
  52.0 0.0 collective-permute-start.2
  52.0 0.0 collective-permute-done.11.refs_2_
  52.0 3.0 %collective-permute-start.5 = (bf16[512,128]{1,0:T(8,128)(2,1)}, bf16[512,128]{1,0:T(8,128)(2,1)S(1)}, u32[]{:S(2)}, u32[]{:S(2)}) collective-permute-start(bf16[512,128]{1,0:T(8,128)(2,1)} %get-tuple-element.37), channel_id=1, source_target_pairs={{0,24},{4,28},{8,16},{12,20},{16,8},{20,12},{24,0},{28,4},{1,25},{... | collective-permute-start | bytes 393224 | tf_op jit(solution)/shard_map/ppermute | solution.py:345
  55.1 1.7 %collective-permute-start.6 = (bf16[512,128]{1,0:T(8,128)(2,1)}, bf16[512,128]{1,0:T(8,128)(2,1)S(1)}, u32[]{:S(2)}, u32[]{:S(2)}) collective-permute-start(bf16[512,128]{1,0:T(8,128)(2,1)} %get-tuple-element.38), channel_id=1, source_target_pairs={{0,28},{4,24},{8,20},{12,16},{16,12},{20,8},{24,4},{28,0},{1,29},{... | collective-permute-start | bytes 393224 | tf_op jit(solution)/shard_map/ppermute | solution.py:345
  56.7 0.9 copy-done.2
  57.7 35.1 %shard_map.96 = (bf16[512,128]{1,0:T(8,128)(2,1)S(1)}, bf16[512,128]{1,0:T(8,128)(2,1)S(1)}, bf16[512,128]{1,0:T(8,128)(2,1)S(1)}, bf16[512,128]{1,0:T(8,128)(2,1)S(1)}) custom-call(bf16[1024,128]{1,0:T(8,128)(2,1)S(1)} %copy-done.2, bf16[1024,128]{1,0:T(8,128)(2,1)S(1)} %collective-permute-done.10.refs_1_, ...), custom_call_target="tpu_custom_call" | custom-call | tf_op jit(solution)/shard_map/pallas_call | solution.py:233
  92.8 0.7 collective-permute-start.17
  93.5 0.2 collective-permute-start.18
  93.7 2.7 %collective-permute-start.19 = (bf16[512,128]{1,0:T(8,128)(2,1)S(1)}, bf16[512,128]{1,0:T(8,128)(2,1)S(1)}, u32[]{:S(2)}, u32[]{:S(2)}) collective-permute-start(bf16[512,128]{1,0:T(8,128)(2,1)S(1)} %get-tuple-element.54), channel_id=1, source_target_pairs={{0,12},{4,8},{8,4},{12,0},{16,28},{20,24},{24,20},{28,16},{1,13},{... | collective-permute-start | bytes 393224 | tf_op jit(solution)/shard_map/ppermute | solution.py:345
  96.4 0.0 collective-permute-done.1.refs_2_
  96.4 0.0 collective-permute-done.2.refs_3_
  96.4 0.9 copy-done.1
  97.4 35.8 %shard_map.95 = (bf16[512,128]{1,0:T(8,128)(2,1)S(1)}, bf16[512,128]{1,0:T(8,128)(2,1)}, bf16[512,128]{1,0:T(8,128)(2,1)}, bf16[512,128]{1,0:T(8,128)(2,1)S(1)}) custom-call(bf16[1024,128]{1,0:T(8,128)(2,1)S(1)} %copy-done.1, bf16[1024,128]{1,0:T(8,128)(2,1)S(1)} %collective-permute-done.refs_1_, bf16[1024,128]{1,0:T(8,128)(2,1)S(1)} %collective-permute-done.1.refs_2_, ...), custom_call_target="tpu_custom_call" | custom-call | tf_op jit(solution)/shard_map/pallas_call | solution.py:233
  133.2 0.7 collective-permute-start.7
  133.9 0.2 collective-permute-start.8
  134.0 0.0 collective-permute-done.17.refs_5_
  134.0 2.7 %collective-permute-start.9 = (bf16[512,128]{1,0:T(8,128)(2,1)S(1)}, bf16[512,128]{1,0:T(8,128)(2,1)S(1)}, u32[]{:S(2)}, u32[]{:S(2)}) collective-permute-start(bf16[512,128]{1,0:T(8,128)(2,1)S(1)} %get-tuple-element.42), channel_id=1, source_target_pairs={{0,12},{4,8},{8,4},{12,0},{16,28},{20,24},{24,20},{28,16},{1,13},{... | collective-permute-start | bytes 393224 | tf_op jit(solution)/shard_map/ppermute | solution.py:345
  136.7 0.7 copy.10.owners
  137.5 0.0 collective-permute-done.18.refs_6_
  137.5 0.0 collective-permute-done.19.refs_7_
  137.5 1.5 collective-permute-done.7.refs_1_
  139.0 0.1 collective-permute-done.8.refs_2_
  139.0 2.2 %collective-permute-done.9.refs_3_ = bf16[512,128]{1,0:T(8,128)(2,1)S(1)} collective-permute-done((bf16[512,128]{1,0:T(8,128)(2,1)S(1)}, bf16[512,128]{1,0:T(8,128)(2,1)S(1)}, u32[]{:S(2)}, u32[]{:S(2)}) %collective-permute-start.9) | collective-permute-done | bytes 131104 | tf_op jit(solution)/shard_map/ppermute | solution.py:345
  141.3 3.2 %finish.1 = (bf16[512,1024]{1,0:T(8,128)(2,1)}, bf16[48,1024]{1,0:T(8,128)(2,1)S(1)}, bf16[48,1024]{1,0:T(8,128)(2,1)S(1)}, bf16[48,1024]{1,0:T(8,128)(2,1)S(1)}, bf16[48,1024]{1,0:T(8,128)(2,1)S(1)}) custom-call(s32[4,1]{1,0:T(4,128)S(1)} %copy.10.owners, s32[1,4]{1,0:T(1,128)S(1)} %copy-done.5, s32[4,128]{1,0:T(4,128)S(1)} %bitcast.9, ...), custom_call_target="tpu_custom_call" | custom-call | tf_op jit(solution)/shard_map/finish/pallas_call | solution.py:303
  144.5 1.5 collective-permute-start.21
  146.0 0.3 collective-permute-start.22
  146.4 3.8 %collective-permute-done.21.refs_2_ = bf16[48,1024]{1,0:T(8,128)(2,1)S(1)} collective-permute-done((bf16[48,1024]{1,0:T(8,128)(2,1)S(1)}, bf16[48,1024]{1,0:T(8,128)(2,1)S(1)}, u32[]{:S(2)}, u32[]{:S(2)}) %collective-permute-start.21) | collective-permute-done | bytes 98336 | tf_op jit(solution)/shard_map/ppermute | solution.py:345
  150.2 1.2 collective-permute-done.22.refs_3_
  151.4 0.9 pool.1
  (16 shorter events, 0.0 us)
Async XLA Ops:
  0.6 140.7 %copy-start.3 = (f32[1024]{0:T(1024)S(1)}, f32[1024]{0:T(1024)}, u32[]{:S(2)}) copy-start(f32[1024]{0:T(1024)} %param.12) | copy-start | bytes 12292
  0.6 140.6 %copy-start.4 = (s32[1,4,128]{2,1,0:T(4,128)S(1)}, s32[1,4,128]{2,1,0:T(4,128)}, u32[]{:S(2)}) copy-start(s32[1,4,128]{2,1,0:T(4,128)} %param.15) | copy-start | bytes 6148
  0.7 140.6 %copy-start.5 = (s32[1,4]{1,0:T(1,128)S(1)}, s32[1,4]{1,0:T(1,128)}, u32[]{:S(2)}) copy-start(s32[1,4]{1,0:T(1,128)} %bases.1) | copy-start | bytes 52
  9.6 131.6 %copy-start = (bf16[1024,1024]{1,0:T(8,128)(2,1)S(1)}, bf16[1024,1024]{1,0:T(8,128)(2,1)}, u32[]{:S(2)}) copy-start(bf16[1024,1024]{1,0:T(8,128)(2,1)} %w_out.1) | copy-start | bytes 6291460
  9.7 20.0 %collective-permute-start.13 = (bf16[512,128]{1,0:T(8,128)(2,1)}, bf16[512,128]{1,0:T(8,128)(2,1)S(1)}, u32[]{:S(2)}, u32[]{:S(2)}) collective-permute-start(bf16[512,128]{1,0:T(8,128)(2,1)} %get-tuple-element.47), channel_id=1, source_target_pairs={{0,16},{4,20},{8,24},{12,28},{16,0},{20,4},{24,8},{28,12},{1,17},{... | collective-permute-start | bytes 393224 | tf_op jit(solution)/shard_map/ppermute | solution.py:345
  13.8 19.8 %collective-permute-start.14 = (bf16[512,128]{1,0:T(8,128)(2,1)}, bf16[512,128]{1,0:T(8,128)(2,1)S(1)}, u32[]{:S(2)}, u32[]{:S(2)}) collective-permute-start(bf16[512,128]{1,0:T(8,128)(2,1)} %get-tuple-element.48), channel_id=1, source_target_pairs={{0,20},{4,16},{8,28},{12,24},{16,4},{20,0},{24,12},{28,8},{1,21},{... | collective-permute-start | bytes 393224 | tf_op jit(solution)/shard_map/ppermute | solution.py:345
  15.0 18.6 %collective-permute-start.15 = (bf16[512,128]{1,0:T(8,128)(2,1)}, bf16[512,128]{1,0:T(8,128)(2,1)S(1)}, u32[]{:S(2)}, u32[]{:S(2)}) collective-permute-start(bf16[512,128]{1,0:T(8,128)(2,1)} %get-tuple-element.49), channel_id=1, source_target_pairs={{0,24},{4,28},{8,16},{12,20},{16,8},{20,12},{24,0},{28,4},{1,25},{... | collective-permute-start | bytes 393224 | tf_op jit(solution)/shard_map/ppermute | solution.py:345
  18.6 18.5 %collective-permute-start.16 = (bf16[512,128]{1,0:T(8,128)(2,1)}, bf16[512,128]{1,0:T(8,128)(2,1)S(1)}, u32[]{:S(2)}, u32[]{:S(2)}) collective-permute-start(bf16[512,128]{1,0:T(8,128)(2,1)} %get-tuple-element.50), channel_id=1, source_target_pairs={{0,28},{4,24},{8,20},{12,16},{16,12},{20,8},{24,4},{28,0},{1,29},{... | collective-permute-start | bytes 393224 | tf_op jit(solution)/shard_map/ppermute | solution.py:345
  18.7 33.3 %collective-permute-start.10 = (bf16[1024,128]{1,0:T(8,128)(2,1)}, bf16[1024,128]{1,0:T(8,128)(2,1)S(1)}, u32[]{:S(2)}, u32[]{:S(2)}) collective-permute-start(bf16[1024,128]{1,0:T(8,128)(2,1)} %get-tuple-element.44), channel_id=1, source_target_pairs={{0,4},{4,0},{8,12},{12,8},{16,20},{20,16},{24,28},{28,24},{1,5},{5... | collective-permute-start | bytes 786440 | tf_op jit(solution)/shard_map/ppermute | solution.py:345
  29.6 22.4 %collective-permute-start.11 = (bf16[1024,128]{1,0:T(8,128)(2,1)}, bf16[1024,128]{1,0:T(8,128)(2,1)S(1)}, u32[]{:S(2)}, u32[]{:S(2)}) collective-permute-start(bf16[1024,128]{1,0:T(8,128)(2,1)} %get-tuple-element.45), channel_id=1, source_target_pairs={{0,8},{4,12},{8,0},{12,4},{16,24},{20,28},{24,16},{28,20},{1,9},{5... | collective-permute-start | bytes 786440 | tf_op jit(solution)/shard_map/ppermute | solution.py:345
  33.6 21.4 %collective-permute-start.12 = (bf16[1024,128]{1,0:T(8,128)(2,1)}, bf16[1024,128]{1,0:T(8,128)(2,1)S(1)}, u32[]{:S(2)}, u32[]{:S(2)}) collective-permute-start(bf16[1024,128]{1,0:T(8,128)(2,1)} %get-tuple-element.46), channel_id=1, source_target_pairs={{0,12},{4,8},{8,4},{12,0},{16,28},{20,24},{24,20},{28,16},{1,13},{... | collective-permute-start | bytes 786440 | tf_op jit(solution)/shard_map/ppermute | solution.py:345
  33.6 11.5 %collective-permute-start.3 = (bf16[512,128]{1,0:T(8,128)(2,1)}, bf16[512,128]{1,0:T(8,128)(2,1)S(1)}, u32[]{:S(2)}, u32[]{:S(2)}) collective-permute-start(bf16[512,128]{1,0:T(8,128)(2,1)} %get-tuple-element.35), channel_id=1, source_target_pairs={{0,16},{4,20},{8,24},{12,28},{16,0},{20,4},{24,8},{28,12},{1,17},{... | collective-permute-start | bytes 393224 | tf_op jit(solution)/shard_map/ppermute | solution.py:345
  37.1 9.8 %collective-permute-start.4 = (bf16[512,128]{1,0:T(8,128)(2,1)}, bf16[512,128]{1,0:T(8,128)(2,1)S(1)}, u32[]{:S(2)}, u32[]{:S(2)}) collective-permute-start(bf16[512,128]{1,0:T(8,128)(2,1)} %get-tuple-element.36), channel_id=1, source_target_pairs={{0,20},{4,16},{8,28},{12,24},{16,4},{20,0},{24,12},{28,8},{1,21},{... | collective-permute-start | bytes 393224 | tf_op jit(solution)/shard_map/ppermute | solution.py:345
  45.1 48.6 %collective-permute-start = (bf16[1024,128]{1,0:T(8,128)(2,1)}, bf16[1024,128]{1,0:T(8,128)(2,1)S(1)}, u32[]{:S(2)}, u32[]{:S(2)}) collective-permute-start(bf16[1024,128]{1,0:T(8,128)(2,1)} %get-tuple-element.32), channel_id=1, source_target_pairs={{0,4},{4,0},{8,12},{12,8},{16,20},{20,16},{24,28},{28,24},{1,5},{5... | collective-permute-start | bytes 786440 | tf_op jit(solution)/shard_map/ppermute | solution.py:345
  46.9 49.5 %collective-permute-start.1 = (bf16[1024,128]{1,0:T(8,128)(2,1)}, bf16[1024,128]{1,0:T(8,128)(2,1)S(1)}, u32[]{:S(2)}, u32[]{:S(2)}) collective-permute-start(bf16[1024,128]{1,0:T(8,128)(2,1)} %get-tuple-element.33), channel_id=1, source_target_pairs={{0,8},{4,12},{8,0},{12,4},{16,24},{20,28},{24,16},{28,20},{1,9},{5... | collective-permute-start | bytes 786440 | tf_op jit(solution)/shard_map/ppermute | solution.py:345
  52.0 44.4 %collective-permute-start.2 = (bf16[1024,128]{1,0:T(8,128)(2,1)}, bf16[1024,128]{1,0:T(8,128)(2,1)S(1)}, u32[]{:S(2)}, u32[]{:S(2)}) collective-permute-start(bf16[1024,128]{1,0:T(8,128)(2,1)} %get-tuple-element.34), channel_id=1, source_target_pairs={{0,12},{4,8},{8,4},{12,0},{16,28},{20,24},{24,20},{28,16},{1,13},{... | collective-permute-start | bytes 786440 | tf_op jit(solution)/shard_map/ppermute | solution.py:345
  52.0 40.8 %collective-permute-start.5 = (bf16[512,128]{1,0:T(8,128)(2,1)}, bf16[512,128]{1,0:T(8,128)(2,1)S(1)}, u32[]{:S(2)}, u32[]{:S(2)}) collective-permute-start(bf16[512,128]{1,0:T(8,128)(2,1)} %get-tuple-element.37), channel_id=1, source_target_pairs={{0,24},{4,28},{8,16},{12,20},{16,8},{20,12},{24,0},{28,4},{1,25},{... | collective-permute-start | bytes 393224 | tf_op jit(solution)/shard_map/ppermute | solution.py:345
  55.1 38.5 %collective-permute-start.6 = (bf16[512,128]{1,0:T(8,128)(2,1)}, bf16[512,128]{1,0:T(8,128)(2,1)S(1)}, u32[]{:S(2)}, u32[]{:S(2)}) collective-permute-start(bf16[512,128]{1,0:T(8,128)(2,1)} %get-tuple-element.38), channel_id=1, source_target_pairs={{0,28},{4,24},{8,20},{12,16},{16,12},{20,8},{24,4},{28,0},{1,29},{... | collective-permute-start | bytes 393224 | tf_op jit(solution)/shard_map/ppermute | solution.py:345
  56.7 0.9 copy-start.2
  92.8 41.2 %collective-permute-start.17 = (bf16[512,128]{1,0:T(8,128)(2,1)S(1)}, bf16[512,128]{1,0:T(8,128)(2,1)S(1)}, u32[]{:S(2)}, u32[]{:S(2)}) collective-permute-start(bf16[512,128]{1,0:T(8,128)(2,1)S(1)} %get-tuple-element.52), channel_id=1, source_target_pairs={{0,4},{4,0},{8,12},{12,8},{16,20},{20,16},{24,28},{28,24},{1,5},{5... | collective-permute-start | bytes 393224 | tf_op jit(solution)/shard_map/ppermute | solution.py:345
  93.5 43.9 %collective-permute-start.18 = (bf16[512,128]{1,0:T(8,128)(2,1)S(1)}, bf16[512,128]{1,0:T(8,128)(2,1)S(1)}, u32[]{:S(2)}, u32[]{:S(2)}) collective-permute-start(bf16[512,128]{1,0:T(8,128)(2,1)S(1)} %get-tuple-element.53), channel_id=1, source_target_pairs={{0,8},{4,12},{8,0},{12,4},{16,24},{20,28},{24,16},{28,20},{1,9},{5... | collective-permute-start | bytes 393224 | tf_op jit(solution)/shard_map/ppermute | solution.py:345
  93.7 43.8 %collective-permute-start.19 = (bf16[512,128]{1,0:T(8,128)(2,1)S(1)}, bf16[512,128]{1,0:T(8,128)(2,1)S(1)}, u32[]{:S(2)}, u32[]{:S(2)}) collective-permute-start(bf16[512,128]{1,0:T(8,128)(2,1)S(1)} %get-tuple-element.54), channel_id=1, source_target_pairs={{0,12},{4,8},{8,4},{12,0},{16,28},{20,24},{24,20},{28,16},{1,13},{... | collective-permute-start | bytes 393224 | tf_op jit(solution)/shard_map/ppermute | solution.py:345
  96.4 1.0 copy-start.1
  133.2 5.8 %collective-permute-start.7 = (bf16[512,128]{1,0:T(8,128)(2,1)}, bf16[512,128]{1,0:T(8,128)(2,1)S(1)}, u32[]{:S(2)}, u32[]{:S(2)}) collective-permute-start(bf16[512,128]{1,0:T(8,128)(2,1)} %get-tuple-element.40), channel_id=1, source_target_pairs={{0,4},{4,0},{8,12},{12,8},{16,20},{20,16},{24,28},{28,24},{1,5},{5... | collective-permute-start | bytes 393224 | tf_op jit(solution)/shard_map/ppermute | solution.py:345
  133.9 5.2 %collective-permute-start.8 = (bf16[512,128]{1,0:T(8,128)(2,1)}, bf16[512,128]{1,0:T(8,128)(2,1)S(1)}, u32[]{:S(2)}, u32[]{:S(2)}) collective-permute-start(bf16[512,128]{1,0:T(8,128)(2,1)} %get-tuple-element.41), channel_id=1, source_target_pairs={{0,8},{4,12},{8,0},{12,4},{16,24},{20,28},{24,16},{28,20},{1,9},{5... | collective-permute-start | bytes 393224 | tf_op jit(solution)/shard_map/ppermute | solution.py:345
  134.0 7.2 %collective-permute-start.9 = (bf16[512,128]{1,0:T(8,128)(2,1)S(1)}, bf16[512,128]{1,0:T(8,128)(2,1)S(1)}, u32[]{:S(2)}, u32[]{:S(2)}) collective-permute-start(bf16[512,128]{1,0:T(8,128)(2,1)S(1)} %get-tuple-element.42), channel_id=1, source_target_pairs={{0,12},{4,8},{8,4},{12,0},{16,28},{20,24},{24,20},{28,16},{1,13},{... | collective-permute-start | bytes 393224 | tf_op jit(solution)/shard_map/ppermute | solution.py:345
  144.5 1.9 %collective-permute-start.20 = (bf16[48,1024]{1,0:T(8,128)(2,1)S(1)}, bf16[48,1024]{1,0:T(8,128)(2,1)S(1)}, u32[]{:S(2)}, u32[]{:S(2)}) collective-permute-start(bf16[48,1024]{1,0:T(8,128)(2,1)S(1)} %get-tuple-element.57), channel_id=1, source_target_pairs={{0,1},{1,0},{2,3},{3,2},{4,5},{5,4},{6,7},{7,6},{8,9},{9,8},{10,11... | collective-permute-start | bytes 294920 | tf_op jit(solution)/shard_map/ppermute | solution.py:345
  144.5 5.7 %collective-permute-start.21 = (bf16[48,1024]{1,0:T(8,128)(2,1)S(1)}, bf16[48,1024]{1,0:T(8,128)(2,1)S(1)}, u32[]{:S(2)}, u32[]{:S(2)}) collective-permute-start(bf16[48,1024]{1,0:T(8,128)(2,1)S(1)} %get-tuple-element.58), channel_id=1, source_target_pairs={{0,2},{1,3},{2,0},{3,1},{4,6},{5,7},{6,4},{7,5},{8,10},{9,11},{10,... | collective-permute-start | bytes 294920 | tf_op jit(solution)/shard_map/ppermute | solution.py:345
  146.0 5.3 %collective-permute-start.22 = (bf16[48,1024]{1,0:T(8,128)(2,1)S(1)}, bf16[48,1024]{1,0:T(8,128)(2,1)S(1)}, u32[]{:S(2)}, u32[]{:S(2)}) collective-permute-start(bf16[48,1024]{1,0:T(8,128)(2,1)S(1)} %get-tuple-element.59), channel_id=1, source_target_pairs={{0,3},{1,2},{2,1},{3,0},{4,7},{5,6},{6,5},{7,4},{8,11},{9,10},{10,... | collective-permute-start | bytes 294920 | tf_op jit(solution)/shard_map/ppermute | solution.py:345
where the time goes:
time: 152 us
  Pallas kernels  84 us (55%)
  starting transfers between devices  38.9 us (26%)
  waiting for transfers between devices  25.9 us (17%)
  local copies, waits for them, and re-layouts  2.66 us (2%)
    pallas_call x2, Pallas kernels, mix_strips(): pl.pallas_call(functools.partial(mix_kernel, team, sources, frames, head_...  70.9 us
    ppermute x23, starting transfers between devices, swap(): return lax.ppermute(array, axis, [(i, i ^ bits) for i in range(size)])  38.9 us
    ppermute x23, waiting for transfers between devices, swap(): return lax.ppermute(array, axis, [(i, i ^ bits) for i in range(size)])  25.9 us
    pallas_call x1, Pallas kernels, mark_strips(): pl.pallas_call(functools.partial(marks_kernel, team, streams, head_dim),...  8.97 us
    pallas_call x1, Pallas kernels, finish(): pl.pallas_call(functools.partial(finish_kernel, team, streams, packs, blo...  3.2 us
  transfers between devices with their start and end apart: 23, of which 8 were waited for; matrix products, arithmetic and copies ran while one was open for 0% of the time, Pallas kernels for 47%

commit v1 on v0

--- a/solution.py
+++ b/solution.py
@@ -33,9 +33,9 @@
     return jnp.dot(a, b, preferred_element_type=F32)
 
 
-def marks_kernel(team, streams, head_dim, q_hbm, k_hbm, v_hbm, *refs):
+def marks_kernel(team, streams, stream, head_dim, q_hbm, k_hbm, v_hbm, *refs):
     frames = q_hbm.shape[0]
-    strips = team * streams
+    strips = team
     near, far = refs[:strips], refs[strips : 2 * strips]
     packs, ins, score_a, score_b, in_sems, out_sems = refs[2 * strips :]
     me = lax.axis_index("tm") % team
@@ -44,8 +44,7 @@
     scale = head_dim**-0.5 * math.log2(math.e)
     loads = []
     for i in range(strips):
-        stream, d = divmod(i, team)
-        column = pl.multiple_of((jnp.bitwise_xor(me, d) * streams + stream) * LANES, LANES)
+        column = pl.multiple_of((jnp.bitwise_xor(me, i) * streams + stream) * LANES, LANES)
         columns = pl.ds(column, LANES)
         three = [
             pltpu.make_async_copy(q_hbm.at[:, columns], packs.at[i, pl.ds(0, frames)], in_sems.at[i, 0]),
@@ -108,13 +107,13 @@
         store.wait()
 
 
-def mark_strips(q, k, v, team, streams, head_dim):
+def mark_strips(q, k, v, team, streams, stream, head_dim):
     frames = q.shape[0]
-    strips = team * streams
+    strips = team
     near = jax.ShapeDtypeStruct((frames + 2 * LANDMARKS, LANES), BF16)
     far = jax.ShapeDtypeStruct((2 * LANDMARKS, LANES), BF16)
     out = pl.pallas_call(
-        functools.partial(marks_kernel, team, streams, head_dim),
+        functools.partial(marks_kernel, team, streams, stream, head_dim),
         out_shape=[near] * strips + [far] * strips,
         in_specs=[HBM] * 3,
         out_specs=[ANY] * (2 * strips),
@@ -127,126 +126,160 @@
             pltpu.SemaphoreType.DMA((strips, 2)),
         ],
         compiler_params=pltpu.CompilerParams(vmem_limit_bytes=60 << 20),
-        name="marks",
     )(q, k, v)
     return out[:strips], out[strips:]
 
 
-def mix_kernel(team, sources, frames, head_dim, *refs):
-    near, far = refs[:team], refs[team:sources]
-    outs = refs[sources : sources + team]
-    queries, mark_keys, mark_values, mixed_all, weight_a, weight_b, scores, sems = refs[sources + team :]
-    strip_heads = LANES // head_dim
-    all_marks = sources * LANDMARKS
+def head_queries(block, head_dim):
+    flat = block.astype(F32).T.astype(BF16)
+    parts = []
+    for low in range(0, LANES, head_dim):
+        pieces = [jnp.zeros((low, flat.shape[1]), BF16), flat[low : low + head_dim]]
+        pieces.append(jnp.zeros((LANES - low - head_dim, flat.shape[1]), BF16))
+        parts.append(jnp.concatenate([piece for piece in pieces if piece.shape[0]], axis=0))
+    return parts
+
+
+def mark_keys_of(ref, base):
+    return ref[pl.ds(base, LANDMARKS)]
+
+
+def mark_values_of(ref, base, h, head_dim):
+    parts = [
+        ref[pl.ds(base + LANDMARKS + part * LANES + h * head_dim, head_dim)] for part in range(LANDMARKS // LANES)
+    ]
+    return jnp.concatenate([jnp.concatenate(parts, axis=1), jnp.ones((ONES, LANDMARKS), BF16)], axis=0)
+
+
+def query_items(frames, head_dim, dests):
+    return [(n, b, h) for n in range(dests) for b in range(frames // QUERY_BLOCK) for h in range(LANES // head_dim)]
+
+
+def gather_sums(queries, sources, weights, head_dim, dests, frames, done):
     scale = head_dim**-0.5 * math.log2(math.e)
-    copies = []
-    for s in range(sources):
-        ref, base = (near[s], frames) if s < team else (far[s - team], 0)
-        pairs = [(ref.at[pl.ds(base, LANDMARKS)], mark_keys.at[pl.ds(s * LANDMARKS, LANDMARKS)])]
-        if s < team:
-            pairs.append((ref.at[pl.ds(0, frames)], queries.at[s]))
-        for part in range(LANDMARKS // LANES):
-            for h in range(strip_heads):
-                rows = pl.ds(base + LANDMARKS + part * LANES + h * head_dim, head_dim)
-                columns = pl.ds(s * LANDMARKS + part * LANES, LANES)
-                pairs.append((ref.at[rows], mark_values.at[h, pl.ds(0, head_dim), columns]))
-        for source, target in pairs:
-            copies.append(pltpu.make_async_copy(source, target, sems.at[len(copies)]))
-            copies[-1].start()
-    for h in range(strip_heads):
-        mark_values[h, pl.ds(head_dim, ONES)] = jnp.ones((ONES, all_marks), BF16)
-    for copy in copies:
-        copy.wait()
-    lane = lax.broadcasted_iota(jnp.int32, (QUERY_BLOCK, LANES), 1)
-    chunk = math.gcd(all_marks, 512)
-    chunks = all_marks // chunk
-    blocks = frames // QUERY_BLOCK
-    weights = (weight_a, weight_b)
-    items = [(d, b, h) for d in range(team) for b in range(blocks) for h in range(strip_heads)]
-
-    def own_queries(rows, h):
-        own = (lane >= h * head_dim) & (lane < (h + 1) * head_dim)
-        return jnp.where(own, rows.astype(F32), 0.0).T.astype(BF16)
-
-    least, most = jnp.full((1, QUERY_BLOCK), 1.0, F32), jnp.full((1, QUERY_BLOCK), 1.0, F32)
-    heads = []
+    items = query_items(frames, head_dim, dests)
     for i in range(len(items) + 1):
         if i < len(items):
-            d, b, h = items[i]
-            query = own_queries(queries[d, pl.ds(b * QUERY_BLOCK, QUERY_BLOCK)], h)
-        for c in range(chunks):
-            rows = pl.ds(c * chunk, chunk)
+            n, b, h = items[i]
+            if h == 0:
+                heads = head_queries(queries[n][pl.ds(b * QUERY_BLOCK, QUERY_BLOCK)], head_dim)
+            query = heads[h]
+        for c, (ref, base) in enumerate(sources):
+            rows = pl.ds(c * LANDMARKS, LANDMARKS)
             if i < len(items):
-                weights[i % 2][rows] = jnp.exp2(dot(mark_keys[rows], query) * scale).astype(BF16)
+                weights[i % 2][rows] = jnp.exp2(dot(mark_keys_of(ref, base), query) * scale).astype(BF16)
             if i > 0:
-                part = dot(mark_values[items[i - 1][2], :, rows], weights[1 - i % 2][rows])
-                mixed = part if c == 0 else mixed + part
-        if i == 0:
-            continue
-        d, b, h = items[i - 1]
-        total = mixed[head_dim : head_dim + 1]
-        least, most = jnp.minimum(least, total), jnp.maximum(most, total)
-        heads.append(mixed[:head_dim] / total)
+                part = dot(mark_values_of(ref, base, items[i - 1][2], head_dim), weights[1 - i % 2][rows])
+                sums = part if c == 0 else sums + part
+        if i > 0:
+            done(items[i - 1], sums)
+
+
+def near_kernel(team, frames, head_dim, *refs):
+    near, partial, weights = refs[:team], refs[team], refs[team + 1 :]
+
+    def done(item, sums):
+        n, b, h = item
+        partial[n, h, :, pl.ds(b * QUERY_BLOCK, QUERY_BLOCK)] = sums
+
+    gather_sums(near, [(ref, frames) for ref in near], weights, head_dim, team, frames, done)
+
+
+def mix_near(near, frames, head_dim):
+    team, strip_heads = len(near), LANES // head_dim
+    return pl.pallas_call(
+        functools.partial(near_kernel, team, frames, head_dim),
+        out_shape=jax.ShapeDtypeStruct((team, strip_heads, head_dim + ONES, frames), F32),
+        in_specs=[VMEM] * team,
+        out_specs=VMEM,
+        scratch_shapes=[pltpu.VMEM((team * LANDMARKS, QUERY_BLOCK), BF16)] * 2,
+        compiler_params=pltpu.CompilerParams(vmem_limit_bytes=16 << 20),
+    )(*near)
+
+
+def far_kernel(team, sources, dests, frames, head_dim, partial, *refs):
+    near, far = refs[:team], refs[team:sources]
+    outs = refs[sources : sources + len(dests)]
+    weight_a, weight_b, scores, all_keys, all_values, held = refs[sources + len(dests) :]
+    strip_heads = LANES // head_dim
+    scale = head_dim**-0.5 * math.log2(math.e)
+    bounds = [jnp.full((1, QUERY_BLOCK), 1.0, F32)] * 2
+    heads = []
+
+    def done(item, sums):
+        n, b, h = item
+        columns = pl.ds(b * QUERY_BLOCK, QUERY_BLOCK)
+        sums = sums + partial[dests[n], h, :, columns]
+        total = sums[head_dim : head_dim + 1]
+        bounds[:] = [jnp.minimum(bounds[0], total), jnp.maximum(bounds[1], total)]
+        heads.append(sums[:head_dim] / total)
         if h == strip_heads - 1:
-            mixed_all[d, pl.ds(b * QUERY_BLOCK, QUERY_BLOCK)] = jnp.concatenate(heads, axis=0).T.astype(BF16)
-            heads = []
-    unsafe = jnp.sum(jnp.where((least > 2.0**-40) & (most < 2.0**100), 0, 1))
+            outs[n][columns] = jnp.concatenate(heads, axis=0).T.astype(BF16)
+            heads.clear()
+
+    queries = [near[d] for d in dests]
+    gather_sums(queries, [(ref, 0) for ref in far], (weight_a, weight_b), head_dim, len(dests), frames, done)
+    unsafe = jnp.sum(jnp.where((bounds[0] > 2.0**-40) & (bounds[1] < 2.0**100), 0, 1))
 
     @pl.when(unsafe > 0)
     def _():
-        def exact(i, carry):
-            d, b = i // blocks, i % blocks
-            block = pl.ds(pl.multiple_of(b * QUERY_BLOCK, QUERY_BLOCK), QUERY_BLOCK)
-            parts = []
+        everything = [(ref, frames) for ref in near] + [(ref, 0) for ref in far]
+        for c, (ref, base) in enumerate(everything):
+            all_keys[pl.ds(c * LANDMARKS, LANDMARKS)] = mark_keys_of(ref, base)
             for h in range(strip_heads):
-                query = own_queries(queries[d, block], h)
+                all_values[h * sources + c] = mark_values_of(ref, base, h, head_dim)
+        lane = lax.broadcasted_iota(jnp.int32, (QUERY_BLOCK, LANES), 1)
+        for n, d in enumerate(dests):
+
+            def exact(i, carry):
+                b, h = i // strip_heads, i % strip_heads
+                block = pl.ds(pl.multiple_of(b * QUERY_BLOCK, QUERY_BLOCK), QUERY_BLOCK)
+                own = (lane >= h * head_dim) & (lane < (h + 1) * head_dim)
+                query = jnp.where(own, near[d][block].astype(F32), 0.0).T.astype(BF16)
+
+                def rows_of(c):
+                    return pl.ds(pl.multiple_of(c * LANDMARKS, LANDMARKS), LANDMARKS)
 
                 def score(c, top):
-                    rows = pl.ds(pl.multiple_of(c * chunk, chunk), chunk)
-                    part = dot(mark_keys[rows], query)
-                    scores[rows] = part
+                    part = dot(all_keys[rows_of(c)], query)
+                    scores[rows_of(c)] = part
                     return jnp.maximum(top, jnp.max(part, axis=0, keepdims=True))
 
-                top = lax.fori_loop(0, chunks, score, jnp.full((1, QUERY_BLOCK), -jnp.inf, F32))
-
-                def weigh(c, total):
-                    rows = pl.ds(pl.multiple_of(c * chunk, chunk), chunk)
-                    weight_a[rows] = jnp.exp2((scores[rows] - top) * scale).astype(BF16)
-                    return total
-
-                lax.fori_loop(0, chunks, weigh, 0)
-                mixed = dot(mark_values[h], weight_a[...])
-                parts.append(mixed[:head_dim] / mixed[head_dim : head_dim + 1])
-            mixed_all[d, block] = jnp.concatenate(parts, axis=0).T.astype(BF16)
-            return carry
-
-        lax.fori_loop(0, team * blocks, exact, 0)
-
-    for d in range(team):
-        outs[d][...] = mixed_all[d]
-
-
-def mix_strips(near, far, frames, head_dim):
+                top = lax.fori_loop(0, sources, score, jnp.full((1, QUERY_BLOCK), -jnp.inf, F32))
+
+                def mix(c, sums):
+                    weight = jnp.exp2((scores[rows_of(c)] - top) * scale).astype(BF16)
+                    return sums + dot(all_values[h * sources + c], weight)
+
+                sums = lax.fori_loop(0, sources, mix, jnp.zeros((head_dim + ONES, QUERY_BLOCK), F32))
+                held[pl.ds(pl.multiple_of(h * head_dim, head_dim), head_dim)] = sums[:head_dim] / sums[head_dim : head_dim + 1]
+
+                @pl.when(h == strip_heads - 1)
+                def _():
+                    outs[n][block] = held[...].T.astype(BF16)
+
+                return carry
+
+            lax.fori_loop(0, frames // QUERY_BLOCK * strip_heads, exact, 0)
+
+
+def mix_far(partial, near, far, dests, frames, head_dim):
     team, sources = len(near), len(near) + len(far)
-    all_marks, strip_heads = sources * LANDMARKS, LANES // head_dim
-    copies = sources * (1 + strip_heads * LANDMARKS // LANES) + team
     return pl.pallas_call(
-        functools.partial(mix_kernel, team, sources, frames, head_dim),
-        out_shape=[jax.ShapeDtypeStruct((frames, LANES), BF16)] * team,
-        in_specs=[ANY] * sources,
-        out_specs=[VMEM] * team,
+        functools.partial(far_kernel, team, sources, dests, frames, head_dim),
+        out_shape=[jax.ShapeDtypeStruct((frames, LANES), BF16)] * len(dests),
+        in_specs=[VMEM] * (1 + sources),
+        out_specs=[VMEM] * len(dests),
         scratch_shapes=[
-            pltpu.VMEM((team, frames, LANES), BF16),
-            pltpu.VMEM((all_marks, LANES), BF16),
-            pltpu.VMEM((strip_heads, head_dim + ONES, all_marks), BF16),
-            pltpu.VMEM((team, frames, LANES), BF16),
-            pltpu.VMEM((all_marks, QUERY_BLOCK), BF16),
-            pltpu.VMEM((all_marks, QUERY_BLOCK), BF16),
-            pltpu.VMEM((all_marks, QUERY_BLOCK), F32),
-            pltpu.SemaphoreType.DMA((copies,)),
+            pltpu.VMEM((len(far) * LANDMARKS, QUERY_BLOCK), BF16),
+            pltpu.VMEM((len(far) * LANDMARKS, QUERY_BLOCK), BF16),
+            pltpu.VMEM((sources * LANDMARKS, QUERY_BLOCK), F32),
+            pltpu.VMEM((sources * LANDMARKS, LANES), BF16),
+            pltpu.VMEM((LANES // head_dim * sources, head_dim + ONES, LANDMARKS), BF16),
+            pltpu.VMEM((LANES, QUERY_BLOCK), F32),
         ],
-        compiler_params=pltpu.CompilerParams(vmem_limit_bytes=32 << 20),
-    )(*near, *far)
+        compiler_params=pltpu.CompilerParams(vmem_limit_bytes=24 << 20),
+    )(partial, *near, *far)
 
 
 def finish_kernel(team, streams, packs, blocks, owners, bases, offsets, w_out, gain, *refs):
@@ -351,24 +384,28 @@
     tm, packs = lax.axis_size("tm"), lax.axis_size("pack")
     head_dim = model // HEADS
     streams = model // team // LANES
-    near_out, far_out = mark_strips(q, k, v, team, streams, head_dim)
-    strips = []
+    near, far, partial, strips = [], [], [], []
     for s in range(streams):
-        mine = range(s * team, (s + 1) * team)
-        far = [
-            swap(far_out[i], "tm", tm, other + d)
-            for other in range(team, tm, team)
-            for d, i in enumerate(mine)
-        ]
-        near = [near_out[s * team]]
-        near += [swap(near_out[mine[d]], "tm", tm, d) for d in range(1, team)]
-        mixed = mix_strips(near, far, frames, head_dim)
+        near_out, far_out = mark_strips(q, k, v, team, streams, s, head_dim)
+        far.append([swap(far_out[d], "tm", tm, other + d) for other in range(team, tm, team) for d in range(team)])
+        near.append([near_out[0]] + [swap(near_out[d], "tm", tm, d) for d in range(1, team)])
+    for s in range(streams):
+        partial.append(mix_near(near[s], frames, head_dim))
+    for s in range(streams):
+        mixed = {}
+        for dests in turns_of(team, streams, s):
+            mixed.update(zip(dests, mix_far(partial[s], near[s], far[s], dests, frames, head_dim)))
         strips += [mixed[0]] + [swap(mixed[d], "tm", tm, d) for d in range(1, team)]
     encoded, sends = finish(
         strips, w_out, norm_gain[None], block_owner[0], block_base, frame_offset[0], team, streams, packs
     )
     got = [sends[0]] + [swap(sends[e], "pack", packs, e) for e in range(1, packs)]
     return encoded[None], pool(got)[None]
+
+
+def turns_of(team, streams, stream):
+    dests = list(reversed(range(team)))
+    return [dests] if stream < streams - 1 or team < 4 else [dests[:-2], dests[-2:]]
 
 
 def solution(mesh):

time: 152 us -> 190 us (1.25)
  Pallas kernels: 84 us -> 127 us
  starting transfers between devices: 38.9 us -> 35.5 us
    pallas_call x3 -> x7, Pallas kernels: 79.9 us -> 123 us  [the longest x3 105 us: mix_far(): pl.pallas_call(functools.partial(far_kernel, team, sources, dests, frames...]
    ppermute x23, starting transfers between devices: 38.9 us -> 35.5 us  [swap(): return lax.ppermute(array, axis, [(i, i ^ bits) for i in range(size)])]
  transfers between devices with their start and end apart: 23 -> 23, of which waited for: 8 -> 9; matrix products, arithmetic and copies ran while one was open for 0% -> 0% of each run, Pallas kernels for 47% -> 62%
where the time goes in v1:
time: 190 us
  Pallas kernels  127 us (67%)
  starting transfers between devices  35.5 us (19%)
  waiting for transfers between devices  26.2 us (14%)
    pallas_call x3, Pallas kernels, mix_far(): pl.pallas_call(functools.partial(far_kernel, team, sources, dests, frames...  105 us
    ppermute x23, starting transfers between devices, swap(): return lax.ppermute(array, axis, [(i, i ^ bits) for i in range(size)])  35.5 us
    ppermute x23, waiting for transfers between devices, swap(): return lax.ppermute(array, axis, [(i, i ^ bits) for i in range(size)])  26.2 us
    pallas_call x2, Pallas kernels, mark_strips(): pl.pallas_call(functools.partial(marks_kernel, team, streams, stream, hea...  10.8 us
    pallas_call x2, Pallas kernels, mix_near(): pl.pallas_call(functools.partial(near_kernel, team, frames, head_dim), ou...  7 us
  transfers between devices with their start and end apart: 23, of which 9 were waited for; matrix products, arithmetic and copies ran while one was open for 0% of the time, Pallas kernels for 62%

profile of v1, /device:TPU:0, one launch (start us, length us, event | category | flops | bytes accessed | tf_op | source)
XLA Modules:
  0.0 190.1 jit_solution(4163161467355075609)
XLA Ops:
  0.6 5.4 %shard_map.98 = (bf16[1024,128]{1,0:T(8,128)(2,1)}, bf16[1024,128]{1,0:T(8,128)(2,1)}, bf16[1024,128]{1,0:T(8,128)(2,1)}, bf16[1024,128]{1,0:T(8,128)(2,1)}, bf1...) custom-call(bf16[512,1024]{1,0:T(8,128)(2,1)} %bitcast.10, ...), custom_call_target="tpu_custom_call" | custom-call | tf_op jit(solution)/shard_map/pallas_call | solution.py:115
  6.1 3.0 %collective-permute-start.10 = (bf16[1024,128]{1,0:T(8,128)(2,1)}, bf16[1024,128]{1,0:T(8,128)(2,1)S(1)}, u32[]{:S(2)}, u32[]{:S(2)}) collective-permute-start(bf16[1024,128]{1,0:T(8,128)(2,1)} %get-tuple-element.44), channel_id=1, source_target_pairs={{0,4},{4,0},{8,12},{12,8},{16,20},{20,16},{24,28},{28,24},{1,5},{5... | collective-permute-start | bytes 786440 | tf_op jit(solution)/shard_map/ppermute | solution.py:378
  9.1 2.6 %collective-permute-start.13 = (bf16[512,128]{1,0:T(8,128)(2,1)}, bf16[512,128]{1,0:T(8,128)(2,1)S(1)}, u32[]{:S(2)}, u32[]{:S(2)}) collective-permute-start(bf16[512,128]{1,0:T(8,128)(2,1)} %get-tuple-element.47), channel_id=1, source_target_pairs={{0,16},{4,20},{8,24},{12,28},{16,0},{20,4},{24,8},{28,12},{1,17},{... | collective-permute-start | bytes 393224 | tf_op jit(solution)/shard_map/ppermute | solution.py:378
  11.7 0.0 collective-permute-start.14
  11.7 3.9 %collective-permute-start.15 = (bf16[512,128]{1,0:T(8,128)(2,1)}, bf16[512,128]{1,0:T(8,128)(2,1)S(1)}, u32[]{:S(2)}, u32[]{:S(2)}) collective-permute-start(bf16[512,128]{1,0:T(8,128)(2,1)} %get-tuple-element.49), channel_id=1, source_target_pairs={{0,24},{4,28},{8,16},{12,20},{16,8},{20,12},{24,0},{28,4},{1,25},{... | collective-permute-start | bytes 393224 | tf_op jit(solution)/shard_map/ppermute | solution.py:378
  15.6 1.1 collective-permute-start.16
  16.7 5.4 %shard_map.95 = (bf16[1024,128]{1,0:T(8,128)(2,1)}, bf16[1024,128]{1,0:T(8,128)(2,1)}, bf16[1024,128]{1,0:T(8,128)(2,1)}, bf16[1024,128]{1,0:T(8,128)(2,1)}, bf1...) custom-call(bf16[512,1024]{1,0:T(8,128)(2,1)} %bitcast.11, ...), custom_call_target="tpu_custom_call" | custom-call | tf_op jit(solution)/shard_map/pallas_call | solution.py:115
  22.2 5.3 %collective-permute-done.13.refs_4_ = bf16[512,128]{1,0:T(8,128)(2,1)S(1)} collective-permute-done((bf16[512,128]{1,0:T(8,128)(2,1)}, bf16[512,128]{1,0:T(8,128)(2,1)S(1)}, u32[]{:S(2)}, u32[]{:S(2)}) %collective-permute-start.13) | collective-permute-done | bytes 131104 | tf_op jit(solution)/shard_map/ppermute | solution.py:378
  27.5 0.0 collective-permute-start.11
  27.5 2.7 %collective-permute-done.14.refs_5_ = bf16[512,128]{1,0:T(8,128)(2,1)S(1)} collective-permute-done((bf16[512,128]{1,0:T(8,128)(2,1)}, bf16[512,128]{1,0:T(8,128)(2,1)S(1)}, u32[]{:S(2)}, u32[]{:S(2)}) %collective-permute-start.14) | collective-permute-done | bytes 131104 | tf_op jit(solution)/shard_map/ppermute | solution.py:378
  30.3 0.0 collective-permute-done.15.refs_6_
  30.3 1.6 collective-permute-start
  31.9 0.0 collective-permute-done.16.refs_7_
  31.9 4.1 %collective-permute-start.1 = (bf16[1024,128]{1,0:T(8,128)(2,1)}, bf16[1024,128]{1,0:T(8,128)(2,1)S(1)}, u32[]{:S(2)}, u32[]{:S(2)}) collective-permute-start(bf16[1024,128]{1,0:T(8,128)(2,1)} %get-tuple-element.33), channel_id=1, source_target_pairs={{0,8},{4,12},{8,0},{12,4},{16,24},{20,28},{24,16},{28,20},{1,9},{5... | collective-permute-start | bytes 786440 | tf_op jit(solution)/shard_map/ppermute | solution.py:378
  36.0 0.0 collective-permute-done.10.refs_1_
  36.0 1.1 collective-permute-start.2
  37.1 4.0 %collective-permute-start.3 = (bf16[512,128]{1,0:T(8,128)(2,1)}, bf16[512,128]{1,0:T(8,128)(2,1)S(1)}, u32[]{:S(2)}, u32[]{:S(2)}) collective-permute-start(bf16[512,128]{1,0:T(8,128)(2,1)} %get-tuple-element.35), channel_id=1, source_target_pairs={{0,16},{4,20},{8,24},{12,28},{16,0},{20,4},{24,8},{28,12},{1,17},{... | collective-permute-start | bytes 393224 | tf_op jit(solution)/shard_map/ppermute | solution.py:378
  41.1 5.4 %collective-permute-done.12.refs_3_ = bf16[1024,128]{1,0:T(8,128)(2,1)S(1)} collective-permute-done((bf16[1024,128]{1,0:T(8,128)(2,1)S(1)}, bf16[1024,128]{1,0:T(8,128)(2,1)S(1)}, u32[]{:S(2)}, u32[]{:S(2)}) %collective-permute-start.12) | collective-permute-done | bytes 262176 | tf_op jit(solution)/shard_map/ppermute | solution.py:378
  46.5 1.8 collective-permute-start.5
  48.3 3.9 %collective-permute-done.1.refs_2_ = bf16[1024,128]{1,0:T(8,128)(2,1)S(1)} collective-permute-done((bf16[1024,128]{1,0:T(8,128)(2,1)}, bf16[1024,128]{1,0:T(8,128)(2,1)S(1)}, u32[]{:S(2)}, u32[]{:S(2)}) %collective-permute-start.1) | collective-permute-done | bytes 262176 | tf_op jit(solution)/shard_map/ppermute | solution.py:378
  52.2 3.2 %collective-permute-start.6 = (bf16[512,128]{1,0:T(8,128)(2,1)}, bf16[512,128]{1,0:T(8,128)(2,1)S(1)}, u32[]{:S(2)}, u32[]{:S(2)}) collective-permute-start(bf16[512,128]{1,0:T(8,128)(2,1)} %get-tuple-element.38), channel_id=1, source_target_pairs={{0,28},{4,24},{8,20},{12,16},{16,12},{20,8},{24,4},{28,0},{1,29},{... | collective-permute-start | bytes 393224 | tf_op jit(solution)/shard_map/ppermute | solution.py:378
  55.4 3.5 %shard_map.99.partial = f32[4,2,80,512]{3,2,1,0:T(8,128)S(1)} custom-call(bf16[1024,128]{1,0:T(8,128)(2,1)S(1)} %copy-done, bf16[1024,128]{1,0:T(8,128)(2,1)S(1)} %collective-permute-done.10.refs_1_, bf16[1024,128]{1,0:T(8,128)(2,1)S(1)} %collective-permute-done.11.refs_2_, bf16[1024,128]{1,0:T(8,128)(2,1)S(1)} %collective-permute-done.12.refs_3_), custom_call_target="tpu_custom_call" | custom-call | tf_op jit(solution)/shard_map/pallas_call | solution.py:190
  58.9 26.3 %shard_map.101 = (bf16[512,128]{1,0:T(8,128)(2,1)S(1)}, bf16[512,128]{1,0:T(8,128)(2,1)S(1)}) custom-call(f32[4,2,80,512]{3,2,1,0:T(8,128)S(1)} %shard_map.99.partial, bf16[1024,128]{1,0:T(8,128)(2,1)S(1)} %copy-done, bf16[1024,128]{1,0:T(8,128)(2,1)S(1)} %collective-permute-done.10.refs_1_, bf16[1024,128]{1,0:T(8,128)(2,1)S(1)} %collective-permute-done.11.refs_2_, ...), custom_call_target="tpu_custom_call" | custom-call | tf_op jit(solution)/shard_map/pallas_call | solution.py:268
  85.2 0.0 collective-permute-done.2.refs_3_
  85.2 0.0 copy-start.2
  85.2 0.1 collective-permute-start.18
  85.3 26.1 %shard_map.100 = (bf16[512,128]{1,0:T(8,128)(2,1)S(1)}, bf16[512,128]{1,0:T(8,128)(2,1)S(1)}) custom-call(f32[4,2,80,512]{3,2,1,0:T(8,128)S(1)} %shard_map.99.partial, bf16[1024,128]{1,0:T(8,128)(2,1)S(1)} %copy-done, bf16[1024,128]{1,0:T(8,128)(2,1)S(1)} %collective-permute-done.10.refs_1_, bf16[1024,128]{1,0:T(8,128)(2,1)S(1)} %collective-permute-done.11.refs_2_, ...), custom_call_target="tpu_custom_call" | custom-call | tf_op jit(solution)/shard_map/pallas_call | solution.py:268
  111.4 3.5 %shard_map.96.partial = f32[4,2,80,512]{3,2,1,0:T(8,128)S(1)} custom-call(bf16[1024,128]{1,0:T(8,128)(2,1)S(1)} %copy-done.2, bf16[1024,128]{1,0:T(8,128)(2,1)S(1)} %collective-permute-done.refs_1_, bf16[1024,128]{1,0:T(8,128)(2,1)S(1)} %collective-permute-done.1.refs_2_, bf16[1024,128]{1,0:T(8,128)(2,1)S(1)} %collective-permute-done.2.refs_3_), custom_call_target="tpu_custom_call" | custom-call | tf_op jit(solution)/shard_map/pallas_call | solution.py:190
  114.9 2.7 %collective-permute-start.19 = (bf16[512,128]{1,0:T(8,128)(2,1)S(1)}, bf16[512,128]{1,0:T(8,128)(2,1)S(1)}, u32[]{:S(2)}, u32[]{:S(2)}) collective-permute-start(bf16[512,128]{1,0:T(8,128)(2,1)S(1)} %get-tuple-element.54), channel_id=1, source_target_pairs={{0,12},{4,8},{8,4},{12,0},{16,28},{20,24},{24,20},{28,16},{1,13},{... | collective-permute-start | bytes 393224 | tf_op jit(solution)/shard_map/ppermute | solution.py:378
  117.7 0.0 collective-permute-done.4.refs_5_
  117.7 0.0 copy-start.5
  117.7 0.9 collective-permute-start.17
  118.6 52.5 %shard_map.97 = (bf16[512,128]{1,0:T(8,128)(2,1)S(1)}, bf16[512,128]{1,0:T(8,128)(2,1)}, bf16[512,128]{1,0:T(8,128)(2,1)}, bf16[512,128]{1,0:T(8,128)(2,1)S(1)}) custom-call(f32[4,2,80,512]{3,2,1,0:T(8,128)S(1)} %shard_map.96.partial, bf16[1024,128]{1,0:T(8,128)(2,1)S(1)} %copy-done.2, bf16[1024,128]{1,0:T(8,128)(2,1)S(1)} %collective-permute-done.refs_1_, ...), custom_call_target="tpu_custom_call" | custom-call | tf_op jit(solution)/shard_map/pallas_call | solution.py:268
  171.1 1.2 collective-permute-start.7
  172.3 0.0 collective-permute-start.8
  172.3 2.2 %collective-permute-start.9 = (bf16[512,128]{1,0:T(8,128)(2,1)S(1)}, bf16[512,128]{1,0:T(8,128)(2,1)S(1)}, u32[]{:S(2)}, u32[]{:S(2)}) collective-permute-start(bf16[512,128]{1,0:T(8,128)(2,1)S(1)} %get-tuple-element.42), channel_id=1, source_target_pairs={{0,12},{4,8},{8,4},{12,0},{16,28},{20,24},{24,20},{28,16},{1,13},{... | collective-permute-start | bytes 393224 | tf_op jit(solution)/shard_map/ppermute | solution.py:378
  174.6 0.7 copy.10.owners
  175.3 0.0 collective-permute-done.19.refs_7_
  175.3 0.0 collective-permute-done.17.refs_5_
  175.3 0.9 collective-permute-done.7.refs_1_
  176.3 1.2 collective-permute-done.8.refs_2_
  177.5 1.6 collective-permute-done.9.refs_3_
  179.2 3.2 %finish.1 = (bf16[512,1024]{1,0:T(8,128)(2,1)}, bf16[48,1024]{1,0:T(8,128)(2,1)S(1)}, bf16[48,1024]{1,0:T(8,128)(2,1)S(1)}, bf16[48,1024]{1,0:T(8,128)(2,1)S(1)}, bf16[48,1024]{1,0:T(8,128)(2,1)S(1)}) custom-call(s32[4,1]{1,0:T(4,128)S(1)} %copy.10.owners, s32[1,4]{1,0:T(1,128)S(1)} %copy-done.5, s32[4,128]{1,0:T(4,128)S(1)} %bitcast.9, ...), custom_call_target="tpu_custom_call" | custom-call | tf_op jit(solution)/shard_map/finish/pallas_call | solution.py:336
  182.3 1.5 collective-permute-start.21
  183.8 0.4 collective-permute-start.22
  184.2 3.8 %collective-permute-done.21.refs_2_ = bf16[48,1024]{1,0:T(8,128)(2,1)S(1)} collective-permute-done((bf16[48,1024]{1,0:T(8,128)(2,1)S(1)}, bf16[48,1024]{1,0:T(8,128)(2,1)S(1)}, u32[]{:S(2)}, u32[]{:S(2)}) %collective-permute-start.21) | collective-permute-done | bytes 98336 | tf_op jit(solution)/shard_map/ppermute | solution.py:378
  188.0 1.2 collective-permute-done.22.refs_3_
  189.2 0.9 pool.1
  (24 shorter events, 0.1 us)
Async XLA Ops:
  6.1 29.9 %collective-permute-start.10 = (bf16[1024,128]{1,0:T(8,128)(2,1)}, bf16[1024,128]{1,0:T(8,128)(2,1)S(1)}, u32[]{:S(2)}, u32[]{:S(2)}) collective-permute-start(bf16[1024,128]{1,0:T(8,128)(2,1)} %get-tuple-element.44), channel_id=1, source_target_pairs={{0,4},{4,0},{8,12},{12,8},{16,20},{20,16},{24,28},{28,24},{1,5},{5... | collective-permute-start | bytes 786440 | tf_op jit(solution)/shard_map/ppermute | solution.py:378
  9.1 18.4 %collective-permute-start.13 = (bf16[512,128]{1,0:T(8,128)(2,1)}, bf16[512,128]{1,0:T(8,128)(2,1)S(1)}, u32[]{:S(2)}, u32[]{:S(2)}) collective-permute-start(bf16[512,128]{1,0:T(8,128)(2,1)} %get-tuple-element.47), channel_id=1, source_target_pairs={{0,16},{4,20},{8,24},{12,28},{16,0},{20,4},{24,8},{28,12},{1,17},{... | collective-permute-start | bytes 393224 | tf_op jit(solution)/shard_map/ppermute | solution.py:378
  11.7 18.6 %collective-permute-start.14 = (bf16[512,128]{1,0:T(8,128)(2,1)}, bf16[512,128]{1,0:T(8,128)(2,1)S(1)}, u32[]{:S(2)}, u32[]{:S(2)}) collective-permute-start(bf16[512,128]{1,0:T(8,128)(2,1)} %get-tuple-element.48), channel_id=1, source_target_pairs={{0,20},{4,16},{8,28},{12,24},{16,4},{20,0},{24,12},{28,8},{1,21},{... | collective-permute-start | bytes 393224 | tf_op jit(solution)/shard_map/ppermute | solution.py:378
  11.7 18.6 %collective-permute-start.15 = (bf16[512,128]{1,0:T(8,128)(2,1)}, bf16[512,128]{1,0:T(8,128)(2,1)S(1)}, u32[]{:S(2)}, u32[]{:S(2)}) collective-permute-start(bf16[512,128]{1,0:T(8,128)(2,1)} %get-tuple-element.49), channel_id=1, source_target_pairs={{0,24},{4,28},{8,16},{12,20},{16,8},{20,12},{24,0},{28,4},{1,25},{... | collective-permute-start | bytes 393224 | tf_op jit(solution)/shard_map/ppermute | solution.py:378
  15.6 11.9 %copy-start.7 = (bf16[1024,128]{1,0:T(8,128)(2,1)S(1)}, bf16[1024,128]{1,0:T(8,128)(2,1)}, u32[]{:S(2)}) copy-start(bf16[1024,128]{1,0:T(8,128)(2,1)} %get-tuple-element.45) | copy-start | bytes 786436
  15.6 14.7 %copy-start.6 = (bf16[1024,128]{1,0:T(8,128)(2,1)S(1)}, bf16[1024,128]{1,0:T(8,128)(2,1)}, u32[]{:S(2)}) copy-start(bf16[1024,128]{1,0:T(8,128)(2,1)} %get-tuple-element.46) | copy-start | bytes 786436
  15.6 39.8 %copy-start = (bf16[1024,128]{1,0:T(8,128)(2,1)S(1)}, bf16[1024,128]{1,0:T(8,128)(2,1)}, u32[]{:S(2)}) copy-start(bf16[1024,128]{1,0:T(8,128)(2,1)} %get-tuple-element.43.refs_0_) | copy-start | bytes 786436
  15.6 16.3 %collective-permute-start.16 = (bf16[512,128]{1,0:T(8,128)(2,1)}, bf16[512,128]{1,0:T(8,128)(2,1)S(1)}, u32[]{:S(2)}, u32[]{:S(2)}) collective-permute-start(bf16[512,128]{1,0:T(8,128)(2,1)} %get-tuple-element.50), channel_id=1, source_target_pairs={{0,28},{4,24},{8,20},{12,16},{16,12},{20,8},{24,4},{28,0},{1,29},{... | collective-permute-start | bytes 393224 | tf_op jit(solution)/shard_map/ppermute | solution.py:378
  27.5 9.6 %collective-permute-start.11 = (bf16[1024,128]{1,0:T(8,128)(2,1)S(1)}, bf16[1024,128]{1,0:T(8,128)(2,1)S(1)}, u32[]{:S(2)}, u32[]{:S(2)}) collective-permute-start(bf16[1024,128]{1,0:T(8,128)(2,1)S(1)} %copy-done.7), channel_id=1, source_target_pairs={{0,8},{4,12},{8,0},{12,4},{16,24},{20,28},{24,16},{28,20},{1,9},{5... | collective-permute-start | bytes 786440 | tf_op jit(solution)/shard_map/ppermute | solution.py:378
  30.3 16.2 %collective-permute-start.12 = (bf16[1024,128]{1,0:T(8,128)(2,1)S(1)}, bf16[1024,128]{1,0:T(8,128)(2,1)S(1)}, u32[]{:S(2)}, u32[]{:S(2)}) collective-permute-start(bf16[1024,128]{1,0:T(8,128)(2,1)S(1)} %copy-done.6), channel_id=1, source_target_pairs={{0,12},{4,8},{8,4},{12,0},{16,28},{20,24},{24,20},{28,16},{1,13},{... | collective-permute-start | bytes 786440 | tf_op jit(solution)/shard_map/ppermute | solution.py:378
  30.3 16.2 %collective-permute-start = (bf16[1024,128]{1,0:T(8,128)(2,1)}, bf16[1024,128]{1,0:T(8,128)(2,1)S(1)}, u32[]{:S(2)}, u32[]{:S(2)}) collective-permute-start(bf16[1024,128]{1,0:T(8,128)(2,1)} %get-tuple-element.32), channel_id=1, source_target_pairs={{0,4},{4,0},{8,12},{12,8},{16,20},{20,16},{24,28},{28,24},{1,5},{5... | collective-permute-start | bytes 786440 | tf_op jit(solution)/shard_map/ppermute | solution.py:378
  31.9 20.3 %collective-permute-start.1 = (bf16[1024,128]{1,0:T(8,128)(2,1)}, bf16[1024,128]{1,0:T(8,128)(2,1)S(1)}, u32[]{:S(2)}, u32[]{:S(2)}) collective-permute-start(bf16[1024,128]{1,0:T(8,128)(2,1)} %get-tuple-element.33), channel_id=1, source_target_pairs={{0,8},{4,12},{8,0},{12,4},{16,24},{20,28},{24,16},{28,20},{1,9},{5... | collective-permute-start | bytes 786440 | tf_op jit(solution)/shard_map/ppermute | solution.py:378
  36.0 49.2 %collective-permute-start.2 = (bf16[1024,128]{1,0:T(8,128)(2,1)}, bf16[1024,128]{1,0:T(8,128)(2,1)S(1)}, u32[]{:S(2)}, u32[]{:S(2)}) collective-permute-start(bf16[1024,128]{1,0:T(8,128)(2,1)} %get-tuple-element.34), channel_id=1, source_target_pairs={{0,12},{4,8},{8,4},{12,0},{16,28},{20,24},{24,20},{28,16},{1,13},{... | collective-permute-start | bytes 786440 | tf_op jit(solution)/shard_map/ppermute | solution.py:378
  37.1 77.8 %collective-permute-start.3 = (bf16[512,128]{1,0:T(8,128)(2,1)}, bf16[512,128]{1,0:T(8,128)(2,1)S(1)}, u32[]{:S(2)}, u32[]{:S(2)}) collective-permute-start(bf16[512,128]{1,0:T(8,128)(2,1)} %get-tuple-element.35), channel_id=1, source_target_pairs={{0,16},{4,20},{8,24},{12,28},{16,0},{20,4},{24,8},{28,12},{1,17},{... | collective-permute-start | bytes 393224 | tf_op jit(solution)/shard_map/ppermute | solution.py:378
  46.5 71.2 %collective-permute-start.4 = (bf16[512,128]{1,0:T(8,128)(2,1)}, bf16[512,128]{1,0:T(8,128)(2,1)S(1)}, u32[]{:S(2)}, u32[]{:S(2)}) collective-permute-start(bf16[512,128]{1,0:T(8,128)(2,1)} %get-tuple-element.36), channel_id=1, source_target_pairs={{0,20},{4,16},{8,28},{12,24},{16,4},{20,0},{24,12},{28,8},{1,21},{... | collective-permute-start | bytes 393224 | tf_op jit(solution)/shard_map/ppermute | solution.py:378
  46.5 72.1 %collective-permute-start.5 = (bf16[512,128]{1,0:T(8,128)(2,1)}, bf16[512,128]{1,0:T(8,128)(2,1)S(1)}, u32[]{:S(2)}, u32[]{:S(2)}) collective-permute-start(bf16[512,128]{1,0:T(8,128)(2,1)} %get-tuple-element.37), channel_id=1, source_target_pairs={{0,24},{4,28},{8,16},{12,20},{16,8},{20,12},{24,0},{28,4},{1,25},{... | collective-permute-start | bytes 393224 | tf_op jit(solution)/shard_map/ppermute | solution.py:378
  52.2 66.4 %collective-permute-start.6 = (bf16[512,128]{1,0:T(8,128)(2,1)}, bf16[512,128]{1,0:T(8,128)(2,1)S(1)}, u32[]{:S(2)}, u32[]{:S(2)}) collective-permute-start(bf16[512,128]{1,0:T(8,128)(2,1)} %get-tuple-element.38), channel_id=1, source_target_pairs={{0,28},{4,24},{8,20},{12,16},{16,12},{20,8},{24,4},{28,0},{1,29},{... | collective-permute-start | bytes 393224 | tf_op jit(solution)/shard_map/ppermute | solution.py:378
  85.2 26.2 %copy-start.2 = (bf16[1024,128]{1,0:T(8,128)(2,1)S(1)}, bf16[1024,128]{1,0:T(8,128)(2,1)}, u32[]{:S(2)}) copy-start(bf16[1024,128]{1,0:T(8,128)(2,1)} %get-tuple-element.31.refs_0_) | copy-start | bytes 786436
  85.2 87.1 %collective-permute-start.18 = (bf16[512,128]{1,0:T(8,128)(2,1)S(1)}, bf16[512,128]{1,0:T(8,128)(2,1)S(1)}, u32[]{:S(2)}, u32[]{:S(2)}) collective-permute-start(bf16[512,128]{1,0:T(8,128)(2,1)S(1)} %get-tuple-element.53), channel_id=1, source_target_pairs={{0,8},{4,12},{8,0},{12,4},{16,24},{20,28},{24,16},{28,20},{1,9},{5... | collective-permute-start | bytes 393224 | tf_op jit(solution)/shard_map/ppermute | solution.py:378
  114.9 60.4 %collective-permute-start.19 = (bf16[512,128]{1,0:T(8,128)(2,1)S(1)}, bf16[512,128]{1,0:T(8,128)(2,1)S(1)}, u32[]{:S(2)}, u32[]{:S(2)}) collective-permute-start(bf16[512,128]{1,0:T(8,128)(2,1)S(1)} %get-tuple-element.54), channel_id=1, source_target_pairs={{0,12},{4,8},{8,4},{12,0},{16,28},{20,24},{24,20},{28,16},{1,13},{... | collective-permute-start | bytes 393224 | tf_op jit(solution)/shard_map/ppermute | solution.py:378
  117.7 61.5 %copy-start.1 = (bf16[1024,1024]{1,0:T(8,128)(2,1)S(1)}, bf16[1024,1024]{1,0:T(8,128)(2,1)}, u32[]{:S(2)}) copy-start(bf16[1024,1024]{1,0:T(8,128)(2,1)} %w_out.1) | copy-start | bytes 6291460
  117.7 61.5 %copy-start.3 = (f32[1024]{0:T(1024)S(1)}, f32[1024]{0:T(1024)}, u32[]{:S(2)}) copy-start(f32[1024]{0:T(1024)} %param.12) | copy-start | bytes 12292
  117.7 61.5 %copy-start.4 = (s32[1,4,128]{2,1,0:T(4,128)S(1)}, s32[1,4,128]{2,1,0:T(4,128)}, u32[]{:S(2)}) copy-start(s32[1,4,128]{2,1,0:T(4,128)} %param.15) | copy-start | bytes 6148
  117.7 61.5 %copy-start.5 = (s32[1,4]{1,0:T(1,128)S(1)}, s32[1,4]{1,0:T(1,128)}, u32[]{:S(2)}) copy-start(s32[1,4]{1,0:T(1,128)} %bases.1) | copy-start | bytes 52
  117.7 57.6 %collective-permute-start.17 = (bf16[512,128]{1,0:T(8,128)(2,1)S(1)}, bf16[512,128]{1,0:T(8,128)(2,1)S(1)}, u32[]{:S(2)}, u32[]{:S(2)}) collective-permute-start(bf16[512,128]{1,0:T(8,128)(2,1)S(1)} %get-tuple-element.52), channel_id=1, source_target_pairs={{0,4},{4,0},{8,12},{12,8},{16,20},{20,16},{24,28},{28,24},{1,5},{5... | collective-permute-start | bytes 393224 | tf_op jit(solution)/shard_map/ppermute | solution.py:378
  171.1 5.2 %collective-permute-start.7 = (bf16[512,128]{1,0:T(8,128)(2,1)}, bf16[512,128]{1,0:T(8,128)(2,1)S(1)}, u32[]{:S(2)}, u32[]{:S(2)}) collective-permute-start(bf16[512,128]{1,0:T(8,128)(2,1)} %get-tuple-element.40), channel_id=1, source_target_pairs={{0,4},{4,0},{8,12},{12,8},{16,20},{20,16},{24,28},{28,24},{1,5},{5... | collective-permute-start | bytes 393224 | tf_op jit(solution)/shard_map/ppermute | solution.py:378
  172.3 5.2 %collective-permute-start.8 = (bf16[512,128]{1,0:T(8,128)(2,1)}, bf16[512,128]{1,0:T(8,128)(2,1)S(1)}, u32[]{:S(2)}, u32[]{:S(2)}) collective-permute-start(bf16[512,128]{1,0:T(8,128)(2,1)} %get-tuple-element.41), channel_id=1, source_target_pairs={{0,8},{4,12},{8,0},{12,4},{16,24},{20,28},{24,16},{28,20},{1,9},{5... | collective-permute-start | bytes 393224 | tf_op jit(solution)/shard_map/ppermute | solution.py:378
  172.3 6.8 %collective-permute-start.9 = (bf16[512,128]{1,0:T(8,128)(2,1)S(1)}, bf16[512,128]{1,0:T(8,128)(2,1)S(1)}, u32[]{:S(2)}, u32[]{:S(2)}) collective-permute-start(bf16[512,128]{1,0:T(8,128)(2,1)S(1)} %get-tuple-element.42), channel_id=1, source_target_pairs={{0,12},{4,8},{8,4},{12,0},{16,28},{20,24},{24,20},{28,16},{1,13},{... | collective-permute-start | bytes 393224 | tf_op jit(solution)/shard_map/ppermute | solution.py:378
  182.3 1.9 collective-permute-start.20
  182.3 5.7 %collective-permute-start.21 = (bf16[48,1024]{1,0:T(8,128)(2,1)S(1)}, bf16[48,1024]{1,0:T(8,128)(2,1)S(1)}, u32[]{:S(2)}, u32[]{:S(2)}) collective-permute-start(bf16[48,1024]{1,0:T(8,128)(2,1)S(1)} %get-tuple-element.58), channel_id=1, source_target_pairs={{0,2},{1,3},{2,0},{3,1},{4,6},{5,7},{6,4},{7,5},{8,10},{9,11},{10,... | collective-permute-start | bytes 294920 | tf_op jit(solution)/shard_map/ppermute | solution.py:378
  183.8 5.4 %collective-permute-start.22 = (bf16[48,1024]{1,0:T(8,128)(2,1)S(1)}, bf16[48,1024]{1,0:T(8,128)(2,1)S(1)}, u32[]{:S(2)}, u32[]{:S(2)}) collective-permute-start(bf16[48,1024]{1,0:T(8,128)(2,1)S(1)} %get-tuple-element.59), channel_id=1, source_target_pairs={{0,3},{1,2},{2,1},{3,0},{4,7},{5,6},{6,5},{7,4},{8,11},{9,10},{10,... | collective-permute-start | bytes 294920 | tf_op jit(solution)/shard_map/ppermute | solution.py:378

commit v2 on v1

--- a/solution.py
+++ b/solution.py
@@ -17,7 +17,6 @@
 LANES = 128
 ONES = 16
 SLOTS = 2
-META = 16
 QUERY_BLOCK = 256
 BF16 = jnp.bfloat16
 F32 = jnp.float32
@@ -197,10 +196,10 @@
     )(*near)
 
 
-def far_kernel(team, sources, dests, frames, head_dim, partial, *refs):
+def far_kernel(team, sources, frames, head_dim, partial, *refs):
     near, far = refs[:team], refs[team:sources]
-    outs = refs[sources : sources + len(dests)]
-    weight_a, weight_b, scores, all_keys, all_values, held = refs[sources + len(dests) :]
+    outs = refs[sources : sources + team]
+    weight_a, weight_b, scores, all_keys, all_values, held = refs[sources + team :]
     strip_heads = LANES // head_dim
     scale = head_dim**-0.5 * math.log2(math.e)
     bounds = [jnp.full((1, QUERY_BLOCK), 1.0, F32)] * 2
@@ -209,7 +208,7 @@
     def done(item, sums):
         n, b, h = item
         columns = pl.ds(b * QUERY_BLOCK, QUERY_BLOCK)
-        sums = sums + partial[dests[n], h, :, columns]
+        sums = sums + partial[n, h, :, columns]
         total = sums[head_dim : head_dim + 1]
         bounds[:] = [jnp.minimum(bounds[0], total), jnp.maximum(bounds[1], total)]
         heads.append(sums[:head_dim] / total)
@@ -217,8 +216,7 @@
             outs[n][columns] = jnp.concatenate(heads, axis=0).T.astype(BF16)
             heads.clear()
 
-    queries = [near[d] for d in dests]
-    gather_sums(queries, [(ref, 0) for ref in far], (weight_a, weight_b), head_dim, len(dests), frames, done)
+    gather_sums(near, [(ref, 0) for ref in far], (weight_a, weight_b), head_dim, team, frames, done)
     unsafe = jnp.sum(jnp.where((bounds[0] > 2.0**-40) & (bounds[1] < 2.0**100), 0, 1))
 
     @pl.when(unsafe > 0)
@@ -229,13 +227,13 @@
             for h in range(strip_heads):
                 all_values[h * sources + c] = mark_values_of(ref, base, h, head_dim)
         lane = lax.broadcasted_iota(jnp.int32, (QUERY_BLOCK, LANES), 1)
-        for n, d in enumerate(dests):
+        for n in range(team):
 
             def exact(i, carry):
                 b, h = i // strip_heads, i % strip_heads
                 block = pl.ds(pl.multiple_of(b * QUERY_BLOCK, QUERY_BLOCK), QUERY_BLOCK)
                 own = (lane >= h * head_dim) & (lane < (h + 1) * head_dim)
-                query = jnp.where(own, near[d][block].astype(F32), 0.0).T.astype(BF16)
+                query = jnp.where(own, near[n][block].astype(F32), 0.0).T.astype(BF16)
 
                 def rows_of(c):
                     return pl.ds(pl.multiple_of(c * LANDMARKS, LANDMARKS), LANDMARKS)
@@ -263,13 +261,13 @@
             lax.fori_loop(0, frames // QUERY_BLOCK * strip_heads, exact, 0)
 
 
-def mix_far(partial, near, far, dests, frames, head_dim):
+def mix_far(partial, near, far, frames, head_dim):
     team, sources = len(near), len(near) + len(far)
     return pl.pallas_call(
-        functools.partial(far_kernel, team, sources, dests, frames, head_dim),
-        out_shape=[jax.ShapeDtypeStruct((frames, LANES), BF16)] * len(dests),
+        functools.partial(far_kernel, team, sources, frames, head_dim),
+        out_shape=[jax.ShapeDtypeStruct((frames, LANES), BF16)] * team,
         in_specs=[VMEM] * (1 + sources),
-        out_specs=[VMEM] * len(dests),
+        out_specs=[VMEM] * team,
         scratch_shapes=[
             pltpu.VMEM((len(far) * LANDMARKS, QUERY_BLOCK), BF16),
             pltpu.VMEM((len(far) * LANDMARKS, QUERY_BLOCK), BF16),
@@ -307,7 +305,7 @@
         rows_to = rows_to + jnp.where((step >= 0) & (step < WINDOW), step + (bases[0, b] + 1), 0)
     hit = jnp.concatenate(hits, axis=1)
     frame_counts = lax.dot_general(
-        jnp.ones((META, blocks * BLOCK), BF16), hit, (((1,), (1,)), ((), ())), preferred_element_type=F32
+        jnp.ones((SLOTS * WINDOW, blocks * BLOCK), BF16), hit, (((1,), (1,)), ((), ())), preferred_element_type=F32
     )
     for b in range(blocks):
         rows = pl.ds(b * BLOCK, BLOCK)
@@ -320,19 +318,19 @@
         power = jnp.mean(projected * projected, axis=-1, keepdims=True)
         encoded[rows] = (projected * lax.rsqrt(power + 1e-06) * gain[...]).astype(BF16)
     sums = dot(hit, encoded[...]).astype(BF16)
-    meta_row = lax.broadcasted_iota(jnp.int32, (META, slots), 0)
+    part = SLOTS * WINDOW
+    meta_row = lax.broadcasted_iota(jnp.int32, (part, slots), 0)
     meta = jnp.where(meta_row == 0, rows_to.astype(F32), jnp.where(meta_row == 1, frame_counts, 0.0))
-    part = SLOTS * WINDOW
     for e in range(packs):
-        sends[e][pl.ds(0, part)] = sums[e * part : (e + 1) * part]
-        sends[e][pl.ds(part, META)] = jnp.zeros((META, model), BF16)
-        sends[e][pl.ds(part, META), pl.ds(0, slots)] = meta.astype(BF16)
+        sends[e][:, pl.ds(0, model)] = sums[e * part : (e + 1) * part]
+        sends[e][:, pl.ds(model, slots)] = meta.astype(BF16)
 
 
 def finish(strips, w_out, gain, owners, bases, offsets, team, streams, packs):
     frames, model = strips[0].shape[0], w_out.shape[1]
     blocks = owners.shape[0]
-    send = jax.ShapeDtypeStruct((SLOTS * WINDOW + META, model), BF16)
+    part = SLOTS * WINDOW
+    send = jax.ShapeDtypeStruct((part, model + packs * part), BF16)
     out = pl.pallas_call(
         functools.partial(finish_kernel, team, streams, packs, blocks),
         out_shape=[jax.ShapeDtypeStruct((frames, model), BF16)] + [send] * packs,
@@ -348,17 +346,18 @@
     got, pooled = refs[:packs], refs[packs]
     part = SLOTS * WINDOW
     slots = packs * part
+    model = pooled.shape[1]
     lane = lax.broadcasted_iota(jnp.int32, (1, slots), 1)
     rows_to, counts = jnp.zeros((1, slots), F32), jnp.zeros((1, slots), F32)
     for e in range(packs):
-        meta = got[e][pl.ds(part, META), pl.ds(0, slots)].astype(F32)
+        meta = got[e][:, pl.ds(model, slots)].astype(F32)
         mine = (lane >= e * part) & (lane < (e + 1) * part)
         rows_to = jnp.where(mine, meta[0:1], rows_to)
         counts = jnp.where(mine, meta[1:2], counts)
     row = lax.broadcasted_iota(jnp.int32, (POOL_DEV, slots), 0)
     place = row + 1 == rows_to.astype(jnp.int32)
     total = jnp.sum(jnp.where(place, counts, 0.0), axis=1, keepdims=True)
-    rows = jnp.concatenate([got[e][pl.ds(0, part)] for e in range(packs)], axis=0)
+    rows = jnp.concatenate([got[e][:, pl.ds(0, model)] for e in range(packs)], axis=0)
     sums = dot(place.astype(F32).astype(BF16), rows)
     pooled[...] = (sums / jnp.maximum(total, 1.0)).astype(BF16)
 
@@ -366,7 +365,7 @@
 def pool(got):
     return pl.pallas_call(
         functools.partial(pool_kernel, len(got)),
-        out_shape=jax.ShapeDtypeStruct((POOL_DEV, got[0].shape[1]), BF16),
+        out_shape=jax.ShapeDtypeStruct((POOL_DEV, got[0].shape[1] - len(got) * SLOTS * WINDOW), BF16),
         in_specs=[VMEM] * len(got),
         out_specs=VMEM,
         compiler_params=pltpu.CompilerParams(vmem_limit_bytes=8 << 20),
@@ -392,20 +391,13 @@
     for s in range(streams):
         partial.append(mix_near(near[s], frames, head_dim))
     for s in range(streams):
-        mixed = {}
-        for dests in turns_of(team, streams, s):
-            mixed.update(zip(dests, mix_far(partial[s], near[s], far[s], dests, frames, head_dim)))
+        mixed = mix_far(partial[s], near[s], far[s], frames, head_dim)
         strips += [mixed[0]] + [swap(mixed[d], "tm", tm, d) for d in range(1, team)]
     encoded, sends = finish(
         strips, w_out, norm_gain[None], block_owner[0], block_base, frame_offset[0], team, streams, packs
     )
     got = [sends[0]] + [swap(sends[e], "pack", packs, e) for e in range(1, packs)]
     return encoded[None], pool(got)[None]
-
-
-def turns_of(team, streams, stream):
-    dests = list(reversed(range(team)))
-    return [dests] if stream < streams - 1 or team < 4 else [dests[:-2], dests[-2:]]
 
 
 def solution(mesh):

time: 190 us -> 189 us (level)
    pallas_call x3 -> x2, Pallas kernels: 105 us -> 104 us  [mix_far(): pl.pallas_call(functools.partial(far_kernel, team, sources, frames, head_...]
where the time goes in v2:
time: 189 us
  Pallas kernels  126 us (67%)
  starting transfers between devices  35.5 us (19%)
  waiting for transfers between devices  25.4 us (13%)
    pallas_call x2, Pallas kernels, mix_far(): pl.pallas_call(functools.partial(far_kernel, team, sources, frames, head_...  104 us
    ppermute x23, starting transfers between devices, swap(): return lax.ppermute(array, axis, [(i, i ^ bits) for i in range(size)])  35.5 us
    ppermute x23, waiting for transfers between devices, swap(): return lax.ppermute(array, axis, [(i, i ^ bits) for i in range(size)])  25.4 us
    pallas_call x2, Pallas kernels, mark_strips(): pl.pallas_call(functools.partial(marks_kernel, team, streams, stream, hea...  10.8 us
    pallas_call x2, Pallas kernels, mix_near(): pl.pallas_call(functools.partial(near_kernel, team, frames, head_dim), ou...  7 us
  transfers between devices with their start and end apart: 23, of which 9 were waited for; matrix products, arithmetic and copies ran while one was open for 0% of the time, Pallas kernels for 62%

profile of v2, /device:TPU:0, one launch (start us, length us, event | category | flops | bytes accessed | tf_op | source)
XLA Modules:
  0.0 188.7 jit_solution(13524345455908993941)
XLA Ops:
  0.6 5.4 %shard_map.98 = (bf16[1024,128]{1,0:T(8,128)(2,1)}, bf16[1024,128]{1,0:T(8,128)(2,1)}, bf16[1024,128]{1,0:T(8,128)(2,1)}, bf16[1024,128]{1,0:T(8,128)(2,1)}, bf1...) custom-call(bf16[512,1024]{1,0:T(8,128)(2,1)} %bitcast.10, ...), custom_call_target="tpu_custom_call" | custom-call | tf_op jit(solution)/shard_map/pallas_call | solution.py:114
  6.1 3.0 %collective-permute-start.10 = (bf16[1024,128]{1,0:T(8,128)(2,1)}, bf16[1024,128]{1,0:T(8,128)(2,1)S(1)}, u32[]{:S(2)}, u32[]{:S(2)}) collective-permute-start(bf16[1024,128]{1,0:T(8,128)(2,1)} %get-tuple-element.44), channel_id=1, source_target_pairs={{0,4},{4,0},{8,12},{12,8},{16,20},{20,16},{24,28},{28,24},{1,5},{5... | collective-permute-start | bytes 786440 | tf_op jit(solution)/shard_map/ppermute | solution.py:377
  9.1 2.6 %collective-permute-start.13 = (bf16[512,128]{1,0:T(8,128)(2,1)}, bf16[512,128]{1,0:T(8,128)(2,1)S(1)}, u32[]{:S(2)}, u32[]{:S(2)}) collective-permute-start(bf16[512,128]{1,0:T(8,128)(2,1)} %get-tuple-element.47), channel_id=1, source_target_pairs={{0,16},{4,20},{8,24},{12,28},{16,0},{20,4},{24,8},{28,12},{1,17},{... | collective-permute-start | bytes 393224 | tf_op jit(solution)/shard_map/ppermute | solution.py:377
  11.7 3.9 %collective-permute-start.15 = (bf16[512,128]{1,0:T(8,128)(2,1)}, bf16[512,128]{1,0:T(8,128)(2,1)S(1)}, u32[]{:S(2)}, u32[]{:S(2)}) collective-permute-start(bf16[512,128]{1,0:T(8,128)(2,1)} %get-tuple-element.49), channel_id=1, source_target_pairs={{0,24},{4,28},{8,16},{12,20},{16,8},{20,12},{24,0},{28,4},{1,25},{... | collective-permute-start | bytes 393224 | tf_op jit(solution)/shard_map/ppermute | solution.py:377
  15.6 1.1 collective-permute-start.16
  16.7 5.4 %shard_map.95 = (bf16[1024,128]{1,0:T(8,128)(2,1)}, bf16[1024,128]{1,0:T(8,128)(2,1)}, bf16[1024,128]{1,0:T(8,128)(2,1)}, bf16[1024,128]{1,0:T(8,128)(2,1)}, bf1...) custom-call(bf16[512,1024]{1,0:T(8,128)(2,1)} %bitcast.11, ...), custom_call_target="tpu_custom_call" | custom-call | tf_op jit(solution)/shard_map/pallas_call | solution.py:114
  22.2 5.3 %collective-permute-done.13.refs_4_ = bf16[512,128]{1,0:T(8,128)(2,1)S(1)} collective-permute-done((bf16[512,128]{1,0:T(8,128)(2,1)}, bf16[512,128]{1,0:T(8,128)(2,1)S(1)}, u32[]{:S(2)}, u32[]{:S(2)}) %collective-permute-start.13) | collective-permute-done | bytes 131104 | tf_op jit(solution)/shard_map/ppermute | solution.py:377
  27.5 2.7 %collective-permute-done.14.refs_5_ = bf16[512,128]{1,0:T(8,128)(2,1)S(1)} collective-permute-done((bf16[512,128]{1,0:T(8,128)(2,1)}, bf16[512,128]{1,0:T(8,128)(2,1)S(1)}, u32[]{:S(2)}, u32[]{:S(2)}) %collective-permute-start.14) | collective-permute-done | bytes 131104 | tf_op jit(solution)/shard_map/ppermute | solution.py:377
  30.2 0.0 collective-permute-start.12
  30.3 0.0 collective-permute-done.15.refs_6_
  30.3 1.6 collective-permute-start
  31.9 4.1 %collective-permute-start.1 = (bf16[1024,128]{1,0:T(8,128)(2,1)}, bf16[1024,128]{1,0:T(8,128)(2,1)S(1)}, u32[]{:S(2)}, u32[]{:S(2)}) collective-permute-start(bf16[1024,128]{1,0:T(8,128)(2,1)} %get-tuple-element.33), channel_id=1, source_target_pairs={{0,8},{4,12},{8,0},{12,4},{16,24},{20,28},{24,16},{28,20},{1,9},{5... | collective-permute-start | bytes 786440 | tf_op jit(solution)/shard_map/ppermute | solution.py:377
  35.9 1.1 collective-permute-start.2
  37.1 0.0 collective-permute-done.11.refs_2_
  37.1 4.0 %collective-permute-start.3 = (bf16[512,128]{1,0:T(8,128)(2,1)}, bf16[512,128]{1,0:T(8,128)(2,1)S(1)}, u32[]{:S(2)}, u32[]{:S(2)}) collective-permute-start(bf16[512,128]{1,0:T(8,128)(2,1)} %get-tuple-element.35), channel_id=1, source_target_pairs={{0,16},{4,20},{8,24},{12,28},{16,0},{20,4},{24,8},{28,12},{1,17},{... | collective-permute-start | bytes 393224 | tf_op jit(solution)/shard_map/ppermute | solution.py:377
  41.1 5.4 %collective-permute-done.12.refs_3_ = bf16[1024,128]{1,0:T(8,128)(2,1)S(1)} collective-permute-done((bf16[1024,128]{1,0:T(8,128)(2,1)S(1)}, bf16[1024,128]{1,0:T(8,128)(2,1)S(1)}, u32[]{:S(2)}, u32[]{:S(2)}) %collective-permute-start.12) | collective-permute-done | bytes 262176 | tf_op jit(solution)/shard_map/ppermute | solution.py:377
  46.5 0.0 collective-permute-start.4
  46.5 0.0 collective-permute-done.refs_1_
  46.5 1.8 collective-permute-start.5
  48.3 3.9 %collective-permute-done.1.refs_2_ = bf16[1024,128]{1,0:T(8,128)(2,1)S(1)} collective-permute-done((bf16[1024,128]{1,0:T(8,128)(2,1)}, bf16[1024,128]{1,0:T(8,128)(2,1)S(1)}, u32[]{:S(2)}, u32[]{:S(2)}) %collective-permute-start.1) | collective-permute-done | bytes 262176 | tf_op jit(solution)/shard_map/ppermute | solution.py:377
  52.2 3.2 %collective-permute-start.6 = (bf16[512,128]{1,0:T(8,128)(2,1)}, bf16[512,128]{1,0:T(8,128)(2,1)S(1)}, u32[]{:S(2)}, u32[]{:S(2)}) collective-permute-start(bf16[512,128]{1,0:T(8,128)(2,1)} %get-tuple-element.38), channel_id=1, source_target_pairs={{0,28},{4,24},{8,20},{12,16},{16,12},{20,8},{24,4},{28,0},{1,29},{... | collective-permute-start | bytes 393224 | tf_op jit(solution)/shard_map/ppermute | solution.py:377
  55.4 3.5 %shard_map.99.partial = f32[4,2,80,512]{3,2,1,0:T(8,128)S(1)} custom-call(bf16[1024,128]{1,0:T(8,128)(2,1)S(1)} %copy-done.2, bf16[1024,128]{1,0:T(8,128)(2,1)S(1)} %collective-permute-done.10.refs_1_, bf16[1024,128]{1,0:T(8,128)(2,1)S(1)} %collective-permute-done.11.refs_2_, bf16[1024,128]{1,0:T(8,128)(2,1)S(1)} %collective-permute-done.12.refs_3_), custom_call_target="tpu_custom_call" | custom-call | tf_op jit(solution)/shard_map/pallas_call | solution.py:189
  58.9 0.0 copy-start.1
  58.9 51.8 %shard_map.100 = (bf16[512,128]{1,0:T(8,128)(2,1)S(1)}, bf16[512,128]{1,0:T(8,128)(2,1)S(1)}, bf16[512,128]{1,0:T(8,128)(2,1)S(1)}, bf16[512,128]{1,0:T(8,128)(2,1)S(1)}) custom-call(f32[4,2,80,512]{3,2,1,0:T(8,128)S(1)} %shard_map.99.partial, bf16[1024,128]{1,0:T(8,128)(2,1)S(1)} %copy-done.2, bf16[1024,128]{1,0:T(8,128)(2,1)S(1)} %collective-permute-done.10.refs_1_, ...), custom_call_target="tpu_custom_call" | custom-call | tf_op jit(solution)/shard_map/pallas_call | solution.py:266
  110.7 1.3 collective-permute-start.17
  112.0 3.5 %shard_map.96.partial = f32[4,2,80,512]{3,2,1,0:T(8,128)S(1)} custom-call(bf16[1024,128]{1,0:T(8,128)(2,1)S(1)} %copy-done.1, bf16[1024,128]{1,0:T(8,128)(2,1)S(1)} %collective-permute-done.refs_1_, bf16[1024,128]{1,0:T(8,128)(2,1)S(1)} %collective-permute-done.1.refs_2_, bf16[1024,128]{1,0:T(8,128)(2,1)S(1)} %collective-permute-done.2.refs_3_), custom_call_target="tpu_custom_call" | custom-call | tf_op jit(solution)/shard_map/pallas_call | solution.py:189
  115.5 0.0 collective-permute-done.3.refs_4_
  115.6 0.1 collective-permute-start.18
  115.6 0.0 collective-permute-done.4.refs_5_
  115.6 0.0 copy-start
  115.7 0.0 copy-start.3
  115.7 0.0 copy-start.4
  115.7 0.0 copy-start.5
  115.7 2.3 %collective-permute-start.19 = (bf16[512,128]{1,0:T(8,128)(2,1)S(1)}, bf16[512,128]{1,0:T(8,128)(2,1)S(1)}, u32[]{:S(2)}, u32[]{:S(2)}) collective-permute-start(bf16[512,128]{1,0:T(8,128)(2,1)S(1)} %get-tuple-element.54), channel_id=1, source_target_pairs={{0,12},{4,8},{8,4},{12,0},{16,28},{20,24},{24,20},{28,16},{1,13},{... | collective-permute-start | bytes 393224 | tf_op jit(solution)/shard_map/ppermute | solution.py:377
  118.0 52.5 %shard_map.97 = (bf16[512,128]{1,0:T(8,128)(2,1)S(1)}, bf16[512,128]{1,0:T(8,128)(2,1)}, bf16[512,128]{1,0:T(8,128)(2,1)}, bf16[512,128]{1,0:T(8,128)(2,1)S(1)}) custom-call(f32[4,2,80,512]{3,2,1,0:T(8,128)S(1)} %shard_map.96.partial, bf16[1024,128]{1,0:T(8,128)(2,1)S(1)} %copy-done.1, bf16[1024,128]{1,0:T(8,128)(2,1)S(1)} %collective-permute-done.refs_1_, ...), custom_call_target="tpu_custom_call" | custom-call | tf_op jit(solution)/shard_map/pallas_call | solution.py:266
  170.5 1.2 collective-permute-start.7
  171.7 0.0 collective-permute-start.8
  171.8 2.2 %collective-permute-start.9 = (bf16[512,128]{1,0:T(8,128)(2,1)S(1)}, bf16[512,128]{1,0:T(8,128)(2,1)S(1)}, u32[]{:S(2)}, u32[]{:S(2)}) collective-permute-start(bf16[512,128]{1,0:T(8,128)(2,1)S(1)} %get-tuple-element.42), channel_id=1, source_target_pairs={{0,12},{4,8},{8,4},{12,0},{16,28},{20,24},{24,20},{28,16},{1,13},{... | collective-permute-start | bytes 393224 | tf_op jit(solution)/shard_map/ppermute | solution.py:377
  174.0 0.7 copy.10.owners
  174.7 0.9 collective-permute-done.7.refs_1_
  175.7 1.2 collective-permute-done.8.refs_2_
  176.9 1.6 collective-permute-done.9.refs_3_
  178.6 3.2 %finish.1 = (bf16[512,1024]{1,0:T(8,128)(2,1)}, bf16[32,1152]{1,0:T(8,128)(2,1)S(1)}, bf16[32,1152]{1,0:T(8,128)(2,1)S(1)}, bf16[32,1152]{1,0:T(8,128)(2,1)S(1)}, bf16[32,1152]{1,0:T(8,128)(2,1)S(1)}) custom-call(s32[4,1]{1,0:T(4,128)S(1)} %copy.10.owners, s32[1,4]{1,0:T(1,128)S(1)} %copy-done.5, s32[4,128]{1,0:T(4,128)S(1)} %bitcast.9, ...), custom_call_target="tpu_custom_call" | custom-call | tf_op jit(solution)/shard_map/finish/pallas_call | solution.py:334
  181.7 1.5 collective-permute-start.21
  183.2 0.4 collective-permute-start.22
  183.6 3.0 %collective-permute-done.21.refs_2_ = bf16[32,1152]{1,0:T(8,128)(2,1)S(1)} collective-permute-done((bf16[32,1152]{1,0:T(8,128)(2,1)S(1)}, bf16[32,1152]{1,0:T(8,128)(2,1)S(1)}, u32[]{:S(2)}, u32[]{:S(2)}) %collective-permute-start.21) | collective-permute-done | bytes 73760 | tf_op jit(solution)/shard_map/ppermute | solution.py:377
  186.6 1.2 collective-permute-done.22.refs_3_
  187.8 0.9 pool.1
  (23 shorter events, 0.1 us)
Async XLA Ops:
  6.1 29.9 %collective-permute-start.10 = (bf16[1024,128]{1,0:T(8,128)(2,1)}, bf16[1024,128]{1,0:T(8,128)(2,1)S(1)}, u32[]{:S(2)}, u32[]{:S(2)}) collective-permute-start(bf16[1024,128]{1,0:T(8,128)(2,1)} %get-tuple-element.44), channel_id=1, source_target_pairs={{0,4},{4,0},{8,12},{12,8},{16,20},{20,16},{24,28},{28,24},{1,5},{5... | collective-permute-start | bytes 786440 | tf_op jit(solution)/shard_map/ppermute | solution.py:377
  9.1 18.4 %collective-permute-start.13 = (bf16[512,128]{1,0:T(8,128)(2,1)}, bf16[512,128]{1,0:T(8,128)(2,1)S(1)}, u32[]{:S(2)}, u32[]{:S(2)}) collective-permute-start(bf16[512,128]{1,0:T(8,128)(2,1)} %get-tuple-element.47), channel_id=1, source_target_pairs={{0,16},{4,20},{8,24},{12,28},{16,0},{20,4},{24,8},{28,12},{1,17},{... | collective-permute-start | bytes 393224 | tf_op jit(solution)/shard_map/ppermute | solution.py:377
  11.7 18.6 %collective-permute-start.14 = (bf16[512,128]{1,0:T(8,128)(2,1)}, bf16[512,128]{1,0:T(8,128)(2,1)S(1)}, u32[]{:S(2)}, u32[]{:S(2)}) collective-permute-start(bf16[512,128]{1,0:T(8,128)(2,1)} %get-tuple-element.48), channel_id=1, source_target_pairs={{0,20},{4,16},{8,28},{12,24},{16,4},{20,0},{24,12},{28,8},{1,21},{... | collective-permute-start | bytes 393224 | tf_op jit(solution)/shard_map/ppermute | solution.py:377
  11.7 18.6 %collective-permute-start.15 = (bf16[512,128]{1,0:T(8,128)(2,1)}, bf16[512,128]{1,0:T(8,128)(2,1)S(1)}, u32[]{:S(2)}, u32[]{:S(2)}) collective-permute-start(bf16[512,128]{1,0:T(8,128)(2,1)} %get-tuple-element.49), channel_id=1, source_target_pairs={{0,24},{4,28},{8,16},{12,20},{16,8},{20,12},{24,0},{28,4},{1,25},{... | collective-permute-start | bytes 393224 | tf_op jit(solution)/shard_map/ppermute | solution.py:377
  15.6 11.9 %copy-start.7 = (bf16[1024,128]{1,0:T(8,128)(2,1)S(1)}, bf16[1024,128]{1,0:T(8,128)(2,1)}, u32[]{:S(2)}) copy-start(bf16[1024,128]{1,0:T(8,128)(2,1)} %get-tuple-element.45) | copy-start | bytes 786436
  15.6 14.7 %copy-start.6 = (bf16[1024,128]{1,0:T(8,128)(2,1)S(1)}, bf16[1024,128]{1,0:T(8,128)(2,1)}, u32[]{:S(2)}) copy-start(bf16[1024,128]{1,0:T(8,128)(2,1)} %get-tuple-element.46) | copy-start | bytes 786436
  15.6 39.8 %copy-start.2 = (bf16[1024,128]{1,0:T(8,128)(2,1)S(1)}, bf16[1024,128]{1,0:T(8,128)(2,1)}, u32[]{:S(2)}) copy-start(bf16[1024,128]{1,0:T(8,128)(2,1)} %get-tuple-element.43.refs_0_) | copy-start | bytes 786436
  15.6 16.3 %collective-permute-start.16 = (bf16[512,128]{1,0:T(8,128)(2,1)}, bf16[512,128]{1,0:T(8,128)(2,1)S(1)}, u32[]{:S(2)}, u32[]{:S(2)}) collective-permute-start(bf16[512,128]{1,0:T(8,128)(2,1)} %get-tuple-element.50), channel_id=1, source_target_pairs={{0,28},{4,24},{8,20},{12,16},{16,12},{20,8},{24,4},{28,0},{1,29},{... | collective-permute-start | bytes 393224 | tf_op jit(solution)/shard_map/ppermute | solution.py:377
  27.5 9.6 %collective-permute-start.11 = (bf16[1024,128]{1,0:T(8,128)(2,1)S(1)}, bf16[1024,128]{1,0:T(8,128)(2,1)S(1)}, u32[]{:S(2)}, u32[]{:S(2)}) collective-permute-start(bf16[1024,128]{1,0:T(8,128)(2,1)S(1)} %copy-done.7), channel_id=1, source_target_pairs={{0,8},{4,12},{8,0},{12,4},{16,24},{20,28},{24,16},{28,20},{1,9},{5... | collective-permute-start | bytes 786440 | tf_op jit(solution)/shard_map/ppermute | solution.py:377
  30.2 16.2 %collective-permute-start.12 = (bf16[1024,128]{1,0:T(8,128)(2,1)S(1)}, bf16[1024,128]{1,0:T(8,128)(2,1)S(1)}, u32[]{:S(2)}, u32[]{:S(2)}) collective-permute-start(bf16[1024,128]{1,0:T(8,128)(2,1)S(1)} %copy-done.6), channel_id=1, source_target_pairs={{0,12},{4,8},{8,4},{12,0},{16,28},{20,24},{24,20},{28,16},{1,13},{... | collective-permute-start | bytes 786440 | tf_op jit(solution)/shard_map/ppermute | solution.py:377
  30.3 16.2 %collective-permute-start = (bf16[1024,128]{1,0:T(8,128)(2,1)}, bf16[1024,128]{1,0:T(8,128)(2,1)S(1)}, u32[]{:S(2)}, u32[]{:S(2)}) collective-permute-start(bf16[1024,128]{1,0:T(8,128)(2,1)} %get-tuple-element.32), channel_id=1, source_target_pairs={{0,4},{4,0},{8,12},{12,8},{16,20},{20,16},{24,28},{28,24},{1,5},{5... | collective-permute-start | bytes 786440 | tf_op jit(solution)/shard_map/ppermute | solution.py:377
  31.9 20.3 %collective-permute-start.1 = (bf16[1024,128]{1,0:T(8,128)(2,1)}, bf16[1024,128]{1,0:T(8,128)(2,1)S(1)}, u32[]{:S(2)}, u32[]{:S(2)}) collective-permute-start(bf16[1024,128]{1,0:T(8,128)(2,1)} %get-tuple-element.33), channel_id=1, source_target_pairs={{0,8},{4,12},{8,0},{12,4},{16,24},{20,28},{24,16},{28,20},{1,9},{5... | collective-permute-start | bytes 786440 | tf_op jit(solution)/shard_map/ppermute | solution.py:377
  35.9 74.8 %collective-permute-start.2 = (bf16[1024,128]{1,0:T(8,128)(2,1)}, bf16[1024,128]{1,0:T(8,128)(2,1)S(1)}, u32[]{:S(2)}, u32[]{:S(2)}) collective-permute-start(bf16[1024,128]{1,0:T(8,128)(2,1)} %get-tuple-element.34), channel_id=1, source_target_pairs={{0,12},{4,8},{8,4},{12,0},{16,28},{20,24},{24,20},{28,16},{1,13},{... | collective-permute-start | bytes 786440 | tf_op jit(solution)/shard_map/ppermute | solution.py:377
  37.1 78.5 %collective-permute-start.3 = (bf16[512,128]{1,0:T(8,128)(2,1)}, bf16[512,128]{1,0:T(8,128)(2,1)S(1)}, u32[]{:S(2)}, u32[]{:S(2)}) collective-permute-start(bf16[512,128]{1,0:T(8,128)(2,1)} %get-tuple-element.35), channel_id=1, source_target_pairs={{0,16},{4,20},{8,24},{12,28},{16,0},{20,4},{24,8},{28,12},{1,17},{... | collective-permute-start | bytes 393224 | tf_op jit(solution)/shard_map/ppermute | solution.py:377
  46.5 69.1 %collective-permute-start.4 = (bf16[512,128]{1,0:T(8,128)(2,1)}, bf16[512,128]{1,0:T(8,128)(2,1)S(1)}, u32[]{:S(2)}, u32[]{:S(2)}) collective-permute-start(bf16[512,128]{1,0:T(8,128)(2,1)} %get-tuple-element.36), channel_id=1, source_target_pairs={{0,20},{4,16},{8,28},{12,24},{16,4},{20,0},{24,12},{28,8},{1,21},{... | collective-permute-start | bytes 393224 | tf_op jit(solution)/shard_map/ppermute | solution.py:377
  46.5 71.5 %collective-permute-start.5 = (bf16[512,128]{1,0:T(8,128)(2,1)}, bf16[512,128]{1,0:T(8,128)(2,1)S(1)}, u32[]{:S(2)}, u32[]{:S(2)}) collective-permute-start(bf16[512,128]{1,0:T(8,128)(2,1)} %get-tuple-element.37), channel_id=1, source_target_pairs={{0,24},{4,28},{8,16},{12,20},{16,8},{20,12},{24,0},{28,4},{1,25},{... | collective-permute-start | bytes 393224 | tf_op jit(solution)/shard_map/ppermute | solution.py:377
  52.2 65.8 %collective-permute-start.6 = (bf16[512,128]{1,0:T(8,128)(2,1)}, bf16[512,128]{1,0:T(8,128)(2,1)S(1)}, u32[]{:S(2)}, u32[]{:S(2)}) collective-permute-start(bf16[512,128]{1,0:T(8,128)(2,1)} %get-tuple-element.38), channel_id=1, source_target_pairs={{0,28},{4,24},{8,20},{12,16},{16,12},{20,8},{24,4},{28,0},{1,29},{... | collective-permute-start | bytes 393224 | tf_op jit(solution)/shard_map/ppermute | solution.py:377
  58.9 53.1 %copy-start.1 = (bf16[1024,128]{1,0:T(8,128)(2,1)S(1)}, bf16[1024,128]{1,0:T(8,128)(2,1)}, u32[]{:S(2)}) copy-start(bf16[1024,128]{1,0:T(8,128)(2,1)} %get-tuple-element.31.refs_0_) | copy-start | bytes 786436
  110.7 61.0 %collective-permute-start.17 = (bf16[512,128]{1,0:T(8,128)(2,1)S(1)}, bf16[512,128]{1,0:T(8,128)(2,1)S(1)}, u32[]{:S(2)}, u32[]{:S(2)}) collective-permute-start(bf16[512,128]{1,0:T(8,128)(2,1)S(1)} %get-tuple-element.52), channel_id=1, source_target_pairs={{0,4},{4,0},{8,12},{12,8},{16,20},{20,16},{24,28},{28,24},{1,5},{5... | collective-permute-start | bytes 393224 | tf_op jit(solution)/shard_map/ppermute | solution.py:377
  115.6 59.2 %collective-permute-start.18 = (bf16[512,128]{1,0:T(8,128)(2,1)S(1)}, bf16[512,128]{1,0:T(8,128)(2,1)S(1)}, u32[]{:S(2)}, u32[]{:S(2)}) collective-permute-start(bf16[512,128]{1,0:T(8,128)(2,1)S(1)} %get-tuple-element.53), channel_id=1, source_target_pairs={{0,8},{4,12},{8,0},{12,4},{16,24},{20,28},{24,16},{28,20},{1,9},{5... | collective-permute-start | bytes 393224 | tf_op jit(solution)/shard_map/ppermute | solution.py:377
  115.6 62.9 %copy-start = (bf16[1024,1024]{1,0:T(8,128)(2,1)S(1)}, bf16[1024,1024]{1,0:T(8,128)(2,1)}, u32[]{:S(2)}) copy-start(bf16[1024,1024]{1,0:T(8,128)(2,1)} %w_out.1) | copy-start | bytes 6291460
  115.7 62.9 %copy-start.3 = (f32[1024]{0:T(1024)S(1)}, f32[1024]{0:T(1024)}, u32[]{:S(2)}) copy-start(f32[1024]{0:T(1024)} %param.12) | copy-start | bytes 12292
  115.7 62.9 %copy-start.4 = (s32[1,4,128]{2,1,0:T(4,128)S(1)}, s32[1,4,128]{2,1,0:T(4,128)}, u32[]{:S(2)}) copy-start(s32[1,4,128]{2,1,0:T(4,128)} %param.15) | copy-start | bytes 6148
  115.7 62.9 %copy-start.5 = (s32[1,4]{1,0:T(1,128)S(1)}, s32[1,4]{1,0:T(1,128)}, u32[]{:S(2)}) copy-start(s32[1,4]{1,0:T(1,128)} %bases.1) | copy-start | bytes 52
  115.7 59.1 %collective-permute-start.19 = (bf16[512,128]{1,0:T(8,128)(2,1)S(1)}, bf16[512,128]{1,0:T(8,128)(2,1)S(1)}, u32[]{:S(2)}, u32[]{:S(2)}) collective-permute-start(bf16[512,128]{1,0:T(8,128)(2,1)S(1)} %get-tuple-element.54), channel_id=1, source_target_pairs={{0,12},{4,8},{8,4},{12,0},{16,28},{20,24},{24,20},{28,16},{1,13},{... | collective-permute-start | bytes 393224 | tf_op jit(solution)/shard_map/ppermute | solution.py:377
  170.5 5.2 %collective-permute-start.7 = (bf16[512,128]{1,0:T(8,128)(2,1)}, bf16[512,128]{1,0:T(8,128)(2,1)S(1)}, u32[]{:S(2)}, u32[]{:S(2)}) collective-permute-start(bf16[512,128]{1,0:T(8,128)(2,1)} %get-tuple-element.40), channel_id=1, source_target_pairs={{0,4},{4,0},{8,12},{12,8},{16,20},{20,16},{24,28},{28,24},{1,5},{5... | collective-permute-start | bytes 393224 | tf_op jit(solution)/shard_map/ppermute | solution.py:377
  171.7 5.2 %collective-permute-start.8 = (bf16[512,128]{1,0:T(8,128)(2,1)}, bf16[512,128]{1,0:T(8,128)(2,1)S(1)}, u32[]{:S(2)}, u32[]{:S(2)}) collective-permute-start(bf16[512,128]{1,0:T(8,128)(2,1)} %get-tuple-element.41), channel_id=1, source_target_pairs={{0,8},{4,12},{8,0},{12,4},{16,24},{20,28},{24,16},{28,20},{1,9},{5... | collective-permute-start | bytes 393224 | tf_op jit(solution)/shard_map/ppermute | solution.py:377
  171.8 6.8 %collective-permute-start.9 = (bf16[512,128]{1,0:T(8,128)(2,1)S(1)}, bf16[512,128]{1,0:T(8,128)(2,1)S(1)}, u32[]{:S(2)}, u32[]{:S(2)}) collective-permute-start(bf16[512,128]{1,0:T(8,128)(2,1)S(1)} %get-tuple-element.42), channel_id=1, source_target_pairs={{0,12},{4,8},{8,4},{12,0},{16,28},{20,24},{24,20},{28,16},{1,13},{... | collective-permute-start | bytes 393224 | tf_op jit(solution)/shard_map/ppermute | solution.py:377
  181.7 1.9 collective-permute-start.20
  181.7 4.9 %collective-permute-start.21 = (bf16[32,1152]{1,0:T(8,128)(2,1)S(1)}, bf16[32,1152]{1,0:T(8,128)(2,1)S(1)}, u32[]{:S(2)}, u32[]{:S(2)}) collective-permute-start(bf16[32,1152]{1,0:T(8,128)(2,1)S(1)} %get-tuple-element.58), channel_id=1, source_target_pairs={{0,2},{1,3},{2,0},{3,1},{4,6},{5,7},{6,4},{7,5},{8,10},{9,11},{10,... | collective-permute-start | bytes 221192 | tf_op jit(solution)/shard_map/ppermute | solution.py:377
  183.2 4.6 %collective-permute-start.22 = (bf16[32,1152]{1,0:T(8,128)(2,1)S(1)}, bf16[32,1152]{1,0:T(8,128)(2,1)S(1)}, u32[]{:S(2)}, u32[]{:S(2)}) collective-permute-start(bf16[32,1152]{1,0:T(8,128)(2,1)S(1)} %get-tuple-element.59), channel_id=1, source_target_pairs={{0,3},{1,2},{2,1},{3,0},{4,7},{5,6},{6,5},{7,4},{8,11},{9,10},{10,... | collective-permute-start | bytes 221192 | tf_op jit(solution)/shard_map/ppermute | solution.py:377

commit v3 on v2

--- a/solution.py
+++ b/solution.py
@@ -32,9 +32,9 @@
     return jnp.dot(a, b, preferred_element_type=F32)
 
 
-def marks_kernel(team, streams, stream, head_dim, q_hbm, k_hbm, v_hbm, *refs):
+def marks_kernel(team, streams, stream, dests, head_dim, q_hbm, k_hbm, v_hbm, *refs):
     frames = q_hbm.shape[0]
-    strips = team
+    strips = len(dests)
     near, far = refs[:strips], refs[strips : 2 * strips]
     packs, ins, score_a, score_b, in_sems, out_sems = refs[2 * strips :]
     me = lax.axis_index("tm") % team
@@ -43,7 +43,7 @@
     scale = head_dim**-0.5 * math.log2(math.e)
     loads = []
     for i in range(strips):
-        column = pl.multiple_of((jnp.bitwise_xor(me, i) * streams + stream) * LANES, LANES)
+        column = pl.multiple_of((jnp.bitwise_xor(me, dests[i]) * streams + stream) * LANES, LANES)
         columns = pl.ds(column, LANES)
         three = [
             pltpu.make_async_copy(q_hbm.at[:, columns], packs.at[i, pl.ds(0, frames)], in_sems.at[i, 0]),
@@ -106,13 +106,13 @@
         store.wait()
 
 
-def mark_strips(q, k, v, team, streams, stream, head_dim):
+def mark_strips(q, k, v, team, streams, stream, dests, head_dim):
     frames = q.shape[0]
-    strips = team
+    strips = len(dests)
     near = jax.ShapeDtypeStruct((frames + 2 * LANDMARKS, LANES), BF16)
     far = jax.ShapeDtypeStruct((2 * LANDMARKS, LANES), BF16)
     out = pl.pallas_call(
-        functools.partial(marks_kernel, team, streams, stream, head_dim),
+        functools.partial(marks_kernel, team, streams, stream, dests, head_dim),
         out_shape=[near] * strips + [far] * strips,
         in_specs=[HBM] * 3,
         out_specs=[ANY] * (2 * strips),
@@ -174,29 +174,34 @@
             done(items[i - 1], sums)
 
 
-def near_kernel(team, frames, head_dim, *refs):
-    near, partial, weights = refs[:team], refs[team], refs[team + 1 :]
+def part_kernel(team, sources, base, frames, head_dim, more, *refs):
+    queries, marks = refs[:team], refs[team : team + sources]
+    before, refs = (refs[team + sources], refs[team + sources + 1 :]) if more else (None, refs[team + sources :])
+    partial, weights = refs[0], refs[1:]
 
     def done(item, sums):
         n, b, h = item
-        partial[n, h, :, pl.ds(b * QUERY_BLOCK, QUERY_BLOCK)] = sums
-
-    gather_sums(near, [(ref, frames) for ref in near], weights, head_dim, team, frames, done)
-
-
-def mix_near(near, frames, head_dim):
+        columns = pl.ds(b * QUERY_BLOCK, QUERY_BLOCK)
+        partial[n, h, :, columns] = sums + before[n, h, :, columns] if more else sums
+
+    gather_sums(queries, [(ref, base) for ref in marks], weights, head_dim, team, frames, done)
+
+
+def mix_part(near, marks, base, before, frames, head_dim):
     team, strip_heads = len(near), LANES // head_dim
+    more = before is not None
+    operands = [*near, *marks] + ([before] if more else [])
     return pl.pallas_call(
-        functools.partial(near_kernel, team, frames, head_dim),
+        functools.partial(part_kernel, team, len(marks), base, frames, head_dim, more),
         out_shape=jax.ShapeDtypeStruct((team, strip_heads, head_dim + ONES, frames), F32),
-        in_specs=[VMEM] * team,
+        in_specs=[VMEM] * len(operands),
         out_specs=VMEM,
-        scratch_shapes=[pltpu.VMEM((team * LANDMARKS, QUERY_BLOCK), BF16)] * 2,
+        scratch_shapes=[pltpu.VMEM((len(marks) * LANDMARKS, QUERY_BLOCK), BF16)] * 2,
         compiler_params=pltpu.CompilerParams(vmem_limit_bytes=16 << 20),
-    )(*near)
-
-
-def far_kernel(team, sources, frames, head_dim, partial, *refs):
+    )(*operands)
+
+
+def far_kernel(team, sources, first, frames, head_dim, partial, *refs):
     near, far = refs[:team], refs[team:sources]
     outs = refs[sources : sources + team]
     weight_a, weight_b, scores, all_keys, all_values, held = refs[sources + team :]
@@ -216,7 +221,7 @@
             outs[n][columns] = jnp.concatenate(heads, axis=0).T.astype(BF16)
             heads.clear()
 
-    gather_sums(near, [(ref, 0) for ref in far], (weight_a, weight_b), head_dim, team, frames, done)
+    gather_sums(near, [(ref, 0) for ref in far[first:]], (weight_a, weight_b), head_dim, team, frames, done)
     unsafe = jnp.sum(jnp.where((bounds[0] > 2.0**-40) & (bounds[1] < 2.0**100), 0, 1))
 
     @pl.when(unsafe > 0)
@@ -261,16 +266,16 @@
             lax.fori_loop(0, frames // QUERY_BLOCK * strip_heads, exact, 0)
 
 
-def mix_far(partial, near, far, frames, head_dim):
+def mix_far(partial, near, far, first, frames, head_dim):
     team, sources = len(near), len(near) + len(far)
     return pl.pallas_call(
-        functools.partial(far_kernel, team, sources, frames, head_dim),
+        functools.partial(far_kernel, team, sources, first, frames, head_dim),
         out_shape=[jax.ShapeDtypeStruct((frames, LANES), BF16)] * team,
         in_specs=[VMEM] * (1 + sources),
         out_specs=[VMEM] * team,
         scratch_shapes=[
-            pltpu.VMEM((len(far) * LANDMARKS, QUERY_BLOCK), BF16),
-            pltpu.VMEM((len(far) * LANDMARKS, QUERY_BLOCK), BF16),
+            pltpu.VMEM(((len(far) - first) * LANDMARKS, QUERY_BLOCK), BF16),
+            pltpu.VMEM(((len(far) - first) * LANDMARKS, QUERY_BLOCK), BF16),
             pltpu.VMEM((sources * LANDMARKS, QUERY_BLOCK), F32),
             pltpu.VMEM((sources * LANDMARKS, LANES), BF16),
             pltpu.VMEM((LANES // head_dim * sources, head_dim + ONES, LANDMARKS), BF16),
@@ -383,21 +388,36 @@
     tm, packs = lax.axis_size("tm"), lax.axis_size("pack")
     head_dim = model // HEADS
     streams = model // team // LANES
-    near, far, partial, strips = [], [], [], []
+    near, far, strips = [], [], []
     for s in range(streams):
-        near_out, far_out = mark_strips(q, k, v, team, streams, s, head_dim)
-        far.append([swap(far_out[d], "tm", tm, other + d) for other in range(team, tm, team) for d in range(team)])
+        near_out, far_out = {}, {}
+        for dests in marks_turns(team, s):
+            outs = mark_strips(q, k, v, team, streams, s, dests, head_dim)
+            near_out.update(zip(dests, outs[0]))
+            far_out.update(zip(dests, outs[1]))
+        far.append([swap(far_out[x % team], "tm", tm, x) for x in far_turns(team, tm)])
         near.append([near_out[0]] + [swap(near_out[d], "tm", tm, d) for d in range(1, team)])
     for s in range(streams):
-        partial.append(mix_near(near[s], frames, head_dim))
-    for s in range(streams):
-        mixed = mix_far(partial[s], near[s], far[s], frames, head_dim)
+        half = len(far[s]) // 2 if s == streams - 1 else 0
+        partial = mix_part(near[s], near[s], frames, None, frames, head_dim)
+        if half:
+            partial = mix_part(near[s], far[s][:half], 0, partial, frames, head_dim)
+        mixed = mix_far(partial, near[s], far[s], half, frames, head_dim)
         strips += [mixed[0]] + [swap(mixed[d], "tm", tm, d) for d in range(1, team)]
     encoded, sends = finish(
         strips, w_out, norm_gain[None], block_owner[0], block_base, frame_offset[0], team, streams, packs
     )
     got = [sends[0]] + [swap(sends[e], "pack", packs, e) for e in range(1, packs)]
     return encoded[None], pool(got)[None]
+
+
+def marks_turns(team, stream):
+    dests = list(reversed(range(team)))
+    return [dests[: team // 2], dests[team // 2 :]] if stream == 0 else [dests]
+
+
+def far_turns(team, tm):
+    return [other + d for other in range(team, tm, team) for d in reversed(range(team))]
 
 
 def solution(mesh):

time: 189 us -> 195 us (1.032)
  starting transfers between devices: 35.5 us -> 39.2 us
  Pallas kernels: 126 us -> 129 us
    ppermute x23, starting transfers between devices: 35.5 us -> 39.2 us  [swap(): return lax.ppermute(array, axis, [(i, i ^ bits) for i in range(size)])]
    pallas_call x6 -> x8, Pallas kernels: 122 us -> 125 us  [the longest x2 103 us: mix_far(): pl.pallas_call(functools.partial(far_kernel, team, sources, first, frames...]
  transfers between devices with their start and end apart: 23 -> 23, of which waited for: 9 -> 10; matrix products, arithmetic and copies ran while one was open for 0% -> 0% of each run, Pallas kernels for 62% -> 61%
where the time goes in v3:
time: 195 us
  Pallas kernels  129 us (66%)
  starting transfers between devices  39.2 us (20%)
  waiting for transfers between devices  25 us (13%)
    pallas_call x2, Pallas kernels, mix_far(): pl.pallas_call(functools.partial(far_kernel, team, sources, first, frames...  103 us
    ppermute x23, starting transfers between devices, swap(): return lax.ppermute(array, axis, [(i, i ^ bits) for i in range(size)])  39.2 us
    ppermute x23, waiting for transfers between devices, swap(): return lax.ppermute(array, axis, [(i, i ^ bits) for i in range(size)])  25 us
    pallas_call x3, Pallas kernels, mark_strips(): pl.pallas_call(functools.partial(marks_kernel, team, streams, stream, des...  12.9 us
    pallas_call x3, Pallas kernels, mix_part(): pl.pallas_call(functools.partial(part_kernel, team, len(marks), base, fra...  9.56 us
  transfers between devices with their start and end apart: 23, of which 10 were waited for; matrix products, arithmetic and copies ran while one was open for 0% of the time, Pallas kernels for 61%

profile of v3, /device:TPU:0, one launch (start us, length us, event | category | flops | bytes accessed | tf_op | source)
XLA Modules:
  0.0 195.3 jit_solution(7552605065946869357)
XLA Ops:
  0.6 5.4 %shard_map.99 = (bf16[1024,128]{1,0:T(8,128)(2,1)}, bf16[1024,128]{1,0:T(8,128)(2,1)}, bf16[1024,128]{1,0:T(8,128)(2,1)}, bf16[1024,128]{1,0:T(8,128)(2,1)}, bf1...) custom-call(bf16[512,1024]{1,0:T(8,128)(2,1)} %bitcast.10, ...), custom_call_target="tpu_custom_call" | custom-call | tf_op jit(solution)/shard_map/pallas_call | solution.py:114
  6.1 3.0 %collective-permute-start.10 = (bf16[1024,128]{1,0:T(8,128)(2,1)}, bf16[1024,128]{1,0:T(8,128)(2,1)S(1)}, u32[]{:S(2)}, u32[]{:S(2)}) collective-permute-start(bf16[1024,128]{1,0:T(8,128)(2,1)} %get-tuple-element.44), channel_id=1, source_target_pairs={{0,4},{4,0},{8,12},{12,8},{16,20},{20,16},{24,28},{28,24},{1,5},{5... | collective-permute-start | bytes 786440 | tf_op jit(solution)/shard_map/ppermute | solution.py:382
  9.1 3.6 %collective-permute-start.13 = (bf16[512,128]{1,0:T(8,128)(2,1)}, bf16[512,128]{1,0:T(8,128)(2,1)S(1)}, u32[]{:S(2)}, u32[]{:S(2)}) collective-permute-start(bf16[512,128]{1,0:T(8,128)(2,1)} %get-tuple-element.47), channel_id=1, source_target_pairs={{0,28},{4,24},{8,20},{12,16},{16,12},{20,8},{24,4},{28,0},{1,29},{... | collective-permute-start | bytes 393224 | tf_op jit(solution)/shard_map/ppermute | solution.py:382
  12.7 0.0 collective-permute-start.14
  12.7 1.9 collective-permute-start.15
  14.6 2.1 %collective-permute-start.16 = (bf16[512,128]{1,0:T(8,128)(2,1)}, bf16[512,128]{1,0:T(8,128)(2,1)S(1)}, u32[]{:S(2)}, u32[]{:S(2)}) collective-permute-start(bf16[512,128]{1,0:T(8,128)(2,1)} %get-tuple-element.50), channel_id=1, source_target_pairs={{0,16},{4,20},{8,24},{12,28},{16,0},{20,4},{24,8},{28,12},{1,17},{... | collective-permute-start | bytes 393224 | tf_op jit(solution)/shard_map/ppermute | solution.py:382
  16.8 3.7 %shard_map.95 = (bf16[1024,128]{1,0:T(8,128)(2,1)}, bf16[1024,128]{1,0:T(8,128)(2,1)}, bf16[512,128]{1,0:T(8,128)(2,1)}, bf16[512,128]{1,0:T(8,128)(2,1)}) custom-call(bf16[512,1024]{1,0:T(8,128)(2,1)} %bitcast.11, bf16[512,1024]{1,0:T(8,128)(2,1)} %bitcast.14, bf16[512,1024]{1,0:T(8,128)(2,1)} %bitcast.17), custom_call_target="tpu_custom_call" | custom-call | tf_op jit(solution)/shard_map/pallas_call | solution.py:114
  20.4 0.0 copy-start.8
  20.5 3.8 %shard_map.96 = (bf16[1024,128]{1,0:T(8,128)(2,1)}, bf16[1024,128]{1,0:T(8,128)(2,1)}, bf16[512,128]{1,0:T(8,128)(2,1)}, bf16[512,128]{1,0:T(8,128)(2,1)}) custom-call(bf16[512,1024]{1,0:T(8,128)(2,1)} %bitcast.12, bf16[512,1024]{1,0:T(8,128)(2,1)} %bitcast.15, bf16[512,1024]{1,0:T(8,128)(2,1)} %bitcast.18), custom_call_target="tpu_custom_call" | custom-call | tf_op jit(solution)/shard_map/pallas_call | solution.py:114
  24.3 4.6 %collective-permute-start.11 = (bf16[1024,128]{1,0:T(8,128)(2,1)S(1)}, bf16[1024,128]{1,0:T(8,128)(2,1)S(1)}, u32[]{:S(2)}, u32[]{:S(2)}) collective-permute-start(bf16[1024,128]{1,0:T(8,128)(2,1)S(1)} %copy-done.7), channel_id=1, source_target_pairs={{0,8},{4,12},{8,0},{12,4},{16,24},{20,28},{24,16},{28,20},{1,9},{5... | collective-permute-start | bytes 786440 | tf_op jit(solution)/shard_map/ppermute | solution.py:382
  28.9 0.0 collective-permute-done.14.refs_5_
  28.9 2.8 %collective-permute-start.12 = (bf16[1024,128]{1,0:T(8,128)(2,1)S(1)}, bf16[1024,128]{1,0:T(8,128)(2,1)S(1)}, u32[]{:S(2)}, u32[]{:S(2)}) collective-permute-start(bf16[1024,128]{1,0:T(8,128)(2,1)S(1)} %copy-done.6), channel_id=1, source_target_pairs={{0,12},{4,8},{8,4},{12,0},{16,28},{20,24},{24,20},{28,16},{1,13},{... | collective-permute-start | bytes 786440 | tf_op jit(solution)/shard_map/ppermute | solution.py:382
  31.7 2.3 %collective-permute-done.15.refs_6_ = bf16[512,128]{1,0:T(8,128)(2,1)S(1)} collective-permute-done((bf16[512,128]{1,0:T(8,128)(2,1)}, bf16[512,128]{1,0:T(8,128)(2,1)S(1)}, u32[]{:S(2)}, u32[]{:S(2)}) %collective-permute-start.15) | collective-permute-done | bytes 131104 | tf_op jit(solution)/shard_map/ppermute | solution.py:382
  34.0 0.6 collective-permute-start
  34.7 0.4 collective-permute-done.16.refs_7_
  35.0 3.0 %collective-permute-start.2 = (bf16[1024,128]{1,0:T(8,128)(2,1)}, bf16[1024,128]{1,0:T(8,128)(2,1)S(1)}, u32[]{:S(2)}, u32[]{:S(2)}) collective-permute-start(bf16[1024,128]{1,0:T(8,128)(2,1)} %get-tuple-element.34), channel_id=1, source_target_pairs={{0,12},{4,8},{8,4},{12,0},{16,28},{20,24},{24,20},{28,16},{1,13},{... | collective-permute-start | bytes 786440 | tf_op jit(solution)/shard_map/ppermute | solution.py:382
  38.0 2.7 %collective-permute-done.11.refs_2_.refs_6_ = bf16[1024,128]{1,0:T(8,128)(2,1)S(1)} collective-permute-done((bf16[1024,128]{1,0:T(8,128)(2,1)S(1)}, bf16[1024,128]{1,0:T(8,128)(2,1)S(1)}, u32[]{:S(2)}, u32[]{:S(2)}) %collective-permute-start.11) | collective-permute-done | bytes 262176 | tf_op jit(solution)/shard_map/ppermute | solution.py:382
  40.6 3.0 %collective-permute-start.3 = (bf16[512,128]{1,0:T(8,128)(2,1)}, bf16[512,128]{1,0:T(8,128)(2,1)S(1)}, u32[]{:S(2)}, u32[]{:S(2)}) collective-permute-start(bf16[512,128]{1,0:T(8,128)(2,1)} %get-tuple-element.35), channel_id=1, source_target_pairs={{0,28},{4,24},{8,20},{12,16},{16,12},{20,8},{24,4},{28,0},{1,29},{... | collective-permute-start | bytes 393224 | tf_op jit(solution)/shard_map/ppermute | solution.py:382
  43.6 3.2 %collective-permute-done.12.refs_3_.refs_7_ = bf16[1024,128]{1,0:T(8,128)(2,1)S(1)} collective-permute-done((bf16[1024,128]{1,0:T(8,128)(2,1)S(1)}, bf16[1024,128]{1,0:T(8,128)(2,1)S(1)}, u32[]{:S(2)}, u32[]{:S(2)}) %collective-permute-start.12) | collective-permute-done | bytes 262176 | tf_op jit(solution)/shard_map/ppermute | solution.py:382
  46.8 2.4 %collective-permute-start.4 = (bf16[512,128]{1,0:T(8,128)(2,1)}, bf16[512,128]{1,0:T(8,128)(2,1)S(1)}, u32[]{:S(2)}, u32[]{:S(2)}) collective-permute-start(bf16[512,128]{1,0:T(8,128)(2,1)} %get-tuple-element.36), channel_id=1, source_target_pairs={{0,24},{4,28},{8,16},{12,20},{16,8},{20,12},{24,0},{28,4},{1,25},{... | collective-permute-start | bytes 393224 | tf_op jit(solution)/shard_map/ppermute | solution.py:382
  49.2 0.0 collective-permute-done.refs_1_.refs_5_
  49.2 1.7 collective-permute-start.5
  51.0 7.2 %collective-permute-done.1.refs_2_.refs_6_ = bf16[1024,128]{1,0:T(8,128)(2,1)S(1)} collective-permute-done((bf16[1024,128]{1,0:T(8,128)(2,1)}, bf16[1024,128]{1,0:T(8,128)(2,1)S(1)}, u32[]{:S(2)}, u32[]{:S(2)}) %collective-permute-start.1) | collective-permute-done | bytes 262176 | tf_op jit(solution)/shard_map/ppermute | solution.py:382
  58.1 3.5 %shard_map.100.refs_6_ = f32[4,2,80,512]{3,2,1,0:T(8,128)S(1)} custom-call(bf16[1024,128]{1,0:T(8,128)(2,1)S(1)} %copy-done, bf16[1024,128]{1,0:T(8,128)(2,1)S(1)} %collective-permute-done.10.refs_1_.refs_5_, bf16[1024,128]{1,0:T(8,128)(2,1)S(1)} %collective-permute-done.11.refs_2_.refs_6_, bf16[1024,128]{1,0:T(8,128)(2,1)S(1)} %collective-permute-done.12.refs_3_.refs_7_, ...), custom_call_target="tpu_custom_call" | custom-call | tf_op jit(solution)/shard_map/pallas_call | solution.py:194
  61.6 2.5 %shard_map.101.partial = f32[4,2,80,512]{3,2,1,0:T(8,128)S(1)} custom-call(bf16[1024,128]{1,0:T(8,128)(2,1)S(1)} %copy-done, bf16[1024,128]{1,0:T(8,128)(2,1)S(1)} %collective-permute-done.10.refs_1_.refs_5_, bf16[1024,128]{1,0:T(8,128)(2,1)S(1)} %collective-permute-done.11.refs_2_.refs_6_, bf16[1024,128]{1,0:T(8,128)(2,1)S(1)} %collective-permute-done.12.refs_3_.refs_7_, ...), custom_call_target="tpu_custom_call" | custom-call | tf_op jit(solution)/shard_map/pallas_call | solution.py:194
  64.2 0.0 copy-start.1
  64.2 50.4 %shard_map.102 = (bf16[512,128]{1,0:T(8,128)(2,1)S(1)}, bf16[512,128]{1,0:T(8,128)(2,1)S(1)}, bf16[512,128]{1,0:T(8,128)(2,1)S(1)}, bf16[512,128]{1,0:T(8,128)(2,1)S(1)}) custom-call(f32[4,2,80,512]{3,2,1,0:T(8,128)S(1)} %shard_map.101.partial, bf16[1024,128]{1,0:T(8,128)(2,1)S(1)} %copy-done, bf16[1024,128]{1,0:T(8,128)(2,1)S(1)} %collective-permute-done.10.refs_1_.refs_5_, ...), custom_call_target="tpu_custom_call" | custom-call | tf_op jit(solution)/shard_map/pallas_call | solution.py:271
  114.6 0.0 collective-permute-done.2.refs_3_.refs_7_
  114.7 2.4 %collective-permute-start.17 = (bf16[512,128]{1,0:T(8,128)(2,1)S(1)}, bf16[512,128]{1,0:T(8,128)(2,1)S(1)}, u32[]{:S(2)}, u32[]{:S(2)}) collective-permute-start(bf16[512,128]{1,0:T(8,128)(2,1)S(1)} %get-tuple-element.52), channel_id=1, source_target_pairs={{0,4},{4,0},{8,12},{12,8},{16,20},{20,16},{24,28},{28,24},{1,5},{5... | collective-permute-start | bytes 393224 | tf_op jit(solution)/shard_map/ppermute | solution.py:382
  117.0 3.5 %shard_map.97.partial = f32[4,2,80,512]{3,2,1,0:T(8,128)S(1)} custom-call(bf16[1024,128]{1,0:T(8,128)(2,1)S(1)} %copy-done.1, bf16[1024,128]{1,0:T(8,128)(2,1)S(1)} %collective-permute-done.refs_1_.refs_5_, bf16[1024,128]{1,0:T(8,128)(2,1)S(1)} %collective-permute-done.1.refs_2_.refs_6_, bf16[1024,128]{1,0:T(8,128)(2,1)S(1)} %collective-permute-done.2.refs_3_.refs_7_, ...), custom_call_target="tpu_custom_call" | custom-call | tf_op jit(solution)/shard_map/pallas_call | solution.py:194
  120.6 2.6 %collective-permute-start.18 = (bf16[512,128]{1,0:T(8,128)(2,1)S(1)}, bf16[512,128]{1,0:T(8,128)(2,1)S(1)}, u32[]{:S(2)}, u32[]{:S(2)}) collective-permute-start(bf16[512,128]{1,0:T(8,128)(2,1)S(1)} %get-tuple-element.53), channel_id=1, source_target_pairs={{0,8},{4,12},{8,0},{12,4},{16,24},{20,28},{24,16},{28,20},{1,9},{5... | collective-permute-start | bytes 393224 | tf_op jit(solution)/shard_map/ppermute | solution.py:382
  123.2 0.0 collective-permute-done.4.refs_5_
  123.2 0.0 copy-start.5
  123.2 0.1 collective-permute-start.19
  123.3 52.5 %shard_map.98 = (bf16[512,128]{1,0:T(8,128)(2,1)S(1)}, bf16[512,128]{1,0:T(8,128)(2,1)}, bf16[512,128]{1,0:T(8,128)(2,1)}, bf16[512,128]{1,0:T(8,128)(2,1)S(1)}) custom-call(f32[4,2,80,512]{3,2,1,0:T(8,128)S(1)} %shard_map.97.partial, bf16[1024,128]{1,0:T(8,128)(2,1)S(1)} %copy-done.1, bf16[1024,128]{1,0:T(8,128)(2,1)S(1)} %collective-permute-done.refs_1_.refs_5_, ...), custom_call_target="tpu_custom_call" | custom-call | tf_op jit(solution)/shard_map/pallas_call | solution.py:271
  175.8 1.5 collective-permute-start.7
  177.3 2.0 %collective-permute-start.8 = (bf16[512,128]{1,0:T(8,128)(2,1)}, bf16[512,128]{1,0:T(8,128)(2,1)S(1)}, u32[]{:S(2)}, u32[]{:S(2)}) collective-permute-start(bf16[512,128]{1,0:T(8,128)(2,1)} %get-tuple-element.41), channel_id=1, source_target_pairs={{0,8},{4,12},{8,0},{12,4},{16,24},{20,28},{24,16},{28,20},{1,9},{5... | collective-permute-start | bytes 393224 | tf_op jit(solution)/shard_map/ppermute | solution.py:382
  179.3 0.0 collective-permute-start.9
  179.3 0.7 copy.10.owners
  180.1 0.9 collective-permute-done.7.refs_1_
  181.0 1.5 collective-permute-done.8.refs_2_
  182.5 2.7 %collective-permute-done.9.refs_3_ = bf16[512,128]{1,0:T(8,128)(2,1)S(1)} collective-permute-done((bf16[512,128]{1,0:T(8,128)(2,1)S(1)}, bf16[512,128]{1,0:T(8,128)(2,1)S(1)}, u32[]{:S(2)}, u32[]{:S(2)}) %collective-permute-start.9) | collective-permute-done | bytes 131104 | tf_op jit(solution)/shard_map/ppermute | solution.py:382
  185.2 3.2 %finish.1 = (bf16[512,1024]{1,0:T(8,128)(2,1)}, bf16[32,1152]{1,0:T(8,128)(2,1)S(1)}, bf16[32,1152]{1,0:T(8,128)(2,1)S(1)}, bf16[32,1152]{1,0:T(8,128)(2,1)S(1)}, bf16[32,1152]{1,0:T(8,128)(2,1)S(1)}) custom-call(s32[4,1]{1,0:T(4,128)S(1)} %copy.10.owners, s32[1,4]{1,0:T(1,128)S(1)} %copy-done.5, s32[4,128]{1,0:T(4,128)S(1)} %bitcast.9, ...), custom_call_target="tpu_custom_call" | custom-call | tf_op jit(solution)/shard_map/finish/pallas_call | solution.py:339
  188.3 1.5 collective-permute-start.21
  189.9 0.3 collective-permute-start.22
  190.2 3.0 %collective-permute-done.21.refs_2_ = bf16[32,1152]{1,0:T(8,128)(2,1)S(1)} collective-permute-done((bf16[32,1152]{1,0:T(8,128)(2,1)S(1)}, bf16[32,1152]{1,0:T(8,128)(2,1)S(1)}, u32[]{:S(2)}, u32[]{:S(2)}) %collective-permute-start.21) | collective-permute-done | bytes 73760 | tf_op jit(solution)/shard_map/ppermute | solution.py:382
  193.2 1.2 collective-permute-done.22.refs_3_
  194.3 0.9 pool.1
  (31 shorter events, 0.1 us)
Async XLA Ops:
  6.1 29.0 %collective-permute-start.10 = (bf16[1024,128]{1,0:T(8,128)(2,1)}, bf16[1024,128]{1,0:T(8,128)(2,1)S(1)}, u32[]{:S(2)}, u32[]{:S(2)}) collective-permute-start(bf16[1024,128]{1,0:T(8,128)(2,1)} %get-tuple-element.44), channel_id=1, source_target_pairs={{0,4},{4,0},{8,12},{12,8},{16,20},{20,16},{24,28},{28,24},{1,5},{5... | collective-permute-start | bytes 786440 | tf_op jit(solution)/shard_map/ppermute | solution.py:382
  9.1 15.2 %collective-permute-start.13 = (bf16[512,128]{1,0:T(8,128)(2,1)}, bf16[512,128]{1,0:T(8,128)(2,1)S(1)}, u32[]{:S(2)}, u32[]{:S(2)}) collective-permute-start(bf16[512,128]{1,0:T(8,128)(2,1)} %get-tuple-element.47), channel_id=1, source_target_pairs={{0,28},{4,24},{8,20},{12,16},{16,12},{20,8},{24,4},{28,0},{1,29},{... | collective-permute-start | bytes 393224 | tf_op jit(solution)/shard_map/ppermute | solution.py:382
  12.7 16.2 %collective-permute-start.14 = (bf16[512,128]{1,0:T(8,128)(2,1)}, bf16[512,128]{1,0:T(8,128)(2,1)S(1)}, u32[]{:S(2)}, u32[]{:S(2)}) collective-permute-start(bf16[512,128]{1,0:T(8,128)(2,1)} %get-tuple-element.48), channel_id=1, source_target_pairs={{0,24},{4,28},{8,16},{12,20},{16,8},{20,12},{24,0},{28,4},{1,25},{... | collective-permute-start | bytes 393224 | tf_op jit(solution)/shard_map/ppermute | solution.py:382
  12.7 21.3 %collective-permute-start.15 = (bf16[512,128]{1,0:T(8,128)(2,1)}, bf16[512,128]{1,0:T(8,128)(2,1)S(1)}, u32[]{:S(2)}, u32[]{:S(2)}) collective-permute-start(bf16[512,128]{1,0:T(8,128)(2,1)} %get-tuple-element.49), channel_id=1, source_target_pairs={{0,20},{4,16},{8,28},{12,24},{16,4},{20,0},{24,12},{28,8},{1,21},{... | collective-permute-start | bytes 393224 | tf_op jit(solution)/shard_map/ppermute | solution.py:382
  14.6 20.4 %collective-permute-start.16 = (bf16[512,128]{1,0:T(8,128)(2,1)}, bf16[512,128]{1,0:T(8,128)(2,1)S(1)}, u32[]{:S(2)}, u32[]{:S(2)}) collective-permute-start(bf16[512,128]{1,0:T(8,128)(2,1)} %get-tuple-element.50), channel_id=1, source_target_pairs={{0,16},{4,20},{8,24},{12,28},{16,0},{20,4},{24,8},{28,12},{1,17},{... | collective-permute-start | bytes 393224 | tf_op jit(solution)/shard_map/ppermute | solution.py:382
  20.4 3.8 %copy-start.7 = (bf16[1024,128]{1,0:T(8,128)(2,1)S(1)}, bf16[1024,128]{1,0:T(8,128)(2,1)}, u32[]{:S(2)}) copy-start(bf16[1024,128]{1,0:T(8,128)(2,1)} %get-tuple-element.45) | copy-start | bytes 786436
  20.4 8.4 %copy-start.6 = (bf16[1024,128]{1,0:T(8,128)(2,1)S(1)}, bf16[1024,128]{1,0:T(8,128)(2,1)}, u32[]{:S(2)}) copy-start(bf16[1024,128]{1,0:T(8,128)(2,1)} %get-tuple-element.46) | copy-start | bytes 786436
  20.4 13.6 %copy-start.8 = (bf16[1024,128]{1,0:T(8,128)(2,1)S(1)}, bf16[1024,128]{1,0:T(8,128)(2,1)}, u32[]{:S(2)}) copy-start(bf16[1024,128]{1,0:T(8,128)(2,1)} %get-tuple-element.32) | copy-start | bytes 786436
  20.5 28.8 %copy-start.10 = (bf16[512,128]{1,0:T(8,128)(2,1)S(1)}, bf16[512,128]{1,0:T(8,128)(2,1)}, u32[]{:S(2)}) copy-start(bf16[512,128]{1,0:T(8,128)(2,1)} %get-tuple-element.37) | copy-start | bytes 393220
  20.5 37.6 %copy-start.9 = (bf16[512,128]{1,0:T(8,128)(2,1)S(1)}, bf16[512,128]{1,0:T(8,128)(2,1)}, u32[]{:S(2)}) copy-start(bf16[512,128]{1,0:T(8,128)(2,1)} %get-tuple-element.38) | copy-start | bytes 393220
  20.5 37.6 %copy-start = (bf16[1024,128]{1,0:T(8,128)(2,1)S(1)}, bf16[1024,128]{1,0:T(8,128)(2,1)}, u32[]{:S(2)}) copy-start(bf16[1024,128]{1,0:T(8,128)(2,1)} %get-tuple-element.43.refs_0_.refs_4_) | copy-start | bytes 786436
  24.3 16.4 %collective-permute-start.11 = (bf16[1024,128]{1,0:T(8,128)(2,1)S(1)}, bf16[1024,128]{1,0:T(8,128)(2,1)S(1)}, u32[]{:S(2)}, u32[]{:S(2)}) collective-permute-start(bf16[1024,128]{1,0:T(8,128)(2,1)S(1)} %copy-done.7), channel_id=1, source_target_pairs={{0,8},{4,12},{8,0},{12,4},{16,24},{20,28},{24,16},{28,20},{1,9},{5... | collective-permute-start | bytes 786440 | tf_op jit(solution)/shard_map/ppermute | solution.py:382
  28.9 17.9 %collective-permute-start.12 = (bf16[1024,128]{1,0:T(8,128)(2,1)S(1)}, bf16[1024,128]{1,0:T(8,128)(2,1)S(1)}, u32[]{:S(2)}, u32[]{:S(2)}) collective-permute-start(bf16[1024,128]{1,0:T(8,128)(2,1)S(1)} %copy-done.6), channel_id=1, source_target_pairs={{0,12},{4,8},{8,4},{12,0},{16,28},{20,24},{24,20},{28,16},{1,13},{... | collective-permute-start | bytes 786440 | tf_op jit(solution)/shard_map/ppermute | solution.py:382
  34.0 15.2 %collective-permute-start = (bf16[1024,128]{1,0:T(8,128)(2,1)S(1)}, bf16[1024,128]{1,0:T(8,128)(2,1)S(1)}, u32[]{:S(2)}, u32[]{:S(2)}) collective-permute-start(bf16[1024,128]{1,0:T(8,128)(2,1)S(1)} %copy-done.8), channel_id=1, source_target_pairs={{0,4},{4,0},{8,12},{12,8},{16,20},{20,16},{24,28},{28,24},{1,5},{5... | collective-permute-start | bytes 786440 | tf_op jit(solution)/shard_map/ppermute | solution.py:382
  35.0 23.1 %collective-permute-start.1 = (bf16[1024,128]{1,0:T(8,128)(2,1)}, bf16[1024,128]{1,0:T(8,128)(2,1)S(1)}, u32[]{:S(2)}, u32[]{:S(2)}) collective-permute-start(bf16[1024,128]{1,0:T(8,128)(2,1)} %get-tuple-element.33), channel_id=1, source_target_pairs={{0,8},{4,12},{8,0},{12,4},{16,24},{20,28},{24,16},{28,20},{1,9},{5... | collective-permute-start | bytes 786440 | tf_op jit(solution)/shard_map/ppermute | solution.py:382
  35.0 79.6 %collective-permute-start.2 = (bf16[1024,128]{1,0:T(8,128)(2,1)}, bf16[1024,128]{1,0:T(8,128)(2,1)S(1)}, u32[]{:S(2)}, u32[]{:S(2)}) collective-permute-start(bf16[1024,128]{1,0:T(8,128)(2,1)} %get-tuple-element.34), channel_id=1, source_target_pairs={{0,12},{4,8},{8,4},{12,0},{16,28},{20,24},{24,20},{28,16},{1,13},{... | collective-permute-start | bytes 786440 | tf_op jit(solution)/shard_map/ppermute | solution.py:382
  40.6 79.9 %collective-permute-start.3 = (bf16[512,128]{1,0:T(8,128)(2,1)}, bf16[512,128]{1,0:T(8,128)(2,1)S(1)}, u32[]{:S(2)}, u32[]{:S(2)}) collective-permute-start(bf16[512,128]{1,0:T(8,128)(2,1)} %get-tuple-element.35), channel_id=1, source_target_pairs={{0,28},{4,24},{8,20},{12,16},{16,12},{20,8},{24,4},{28,0},{1,29},{... | collective-permute-start | bytes 393224 | tf_op jit(solution)/shard_map/ppermute | solution.py:382
  46.8 76.3 %collective-permute-start.4 = (bf16[512,128]{1,0:T(8,128)(2,1)}, bf16[512,128]{1,0:T(8,128)(2,1)S(1)}, u32[]{:S(2)}, u32[]{:S(2)}) collective-permute-start(bf16[512,128]{1,0:T(8,128)(2,1)} %get-tuple-element.36), channel_id=1, source_target_pairs={{0,24},{4,28},{8,16},{12,20},{16,8},{20,12},{24,0},{28,4},{1,25},{... | collective-permute-start | bytes 393224 | tf_op jit(solution)/shard_map/ppermute | solution.py:382
  49.2 74.0 %collective-permute-start.5 = (bf16[512,128]{1,0:T(8,128)(2,1)S(1)}, bf16[512,128]{1,0:T(8,128)(2,1)S(1)}, u32[]{:S(2)}, u32[]{:S(2)}) collective-permute-start(bf16[512,128]{1,0:T(8,128)(2,1)S(1)} %copy-done.10), channel_id=1, source_target_pairs={{0,20},{4,16},{8,28},{12,24},{16,4},{20,0},{24,12},{28,8},{1,21},{... | collective-permute-start | bytes 393224 | tf_op jit(solution)/shard_map/ppermute | solution.py:382
  58.1 65.2 %collective-permute-start.6 = (bf16[512,128]{1,0:T(8,128)(2,1)S(1)}, bf16[512,128]{1,0:T(8,128)(2,1)S(1)}, u32[]{:S(2)}, u32[]{:S(2)}) collective-permute-start(bf16[512,128]{1,0:T(8,128)(2,1)S(1)} %copy-done.9), channel_id=1, source_target_pairs={{0,16},{4,20},{8,24},{12,28},{16,0},{20,4},{24,8},{28,12},{1,17},{... | collective-permute-start | bytes 393224 | tf_op jit(solution)/shard_map/ppermute | solution.py:382
  64.2 52.9 %copy-start.1 = (bf16[1024,128]{1,0:T(8,128)(2,1)S(1)}, bf16[1024,128]{1,0:T(8,128)(2,1)}, u32[]{:S(2)}) copy-start(bf16[1024,128]{1,0:T(8,128)(2,1)} %get-tuple-element.31.refs_0_.refs_4_) | copy-start | bytes 786436
  114.7 64.6 %collective-permute-start.17 = (bf16[512,128]{1,0:T(8,128)(2,1)S(1)}, bf16[512,128]{1,0:T(8,128)(2,1)S(1)}, u32[]{:S(2)}, u32[]{:S(2)}) collective-permute-start(bf16[512,128]{1,0:T(8,128)(2,1)S(1)} %get-tuple-element.52), channel_id=1, source_target_pairs={{0,4},{4,0},{8,12},{12,8},{16,20},{20,16},{24,28},{28,24},{1,5},{5... | collective-permute-start | bytes 393224 | tf_op jit(solution)/shard_map/ppermute | solution.py:382
  120.6 59.5 %collective-permute-start.18 = (bf16[512,128]{1,0:T(8,128)(2,1)S(1)}, bf16[512,128]{1,0:T(8,128)(2,1)S(1)}, u32[]{:S(2)}, u32[]{:S(2)}) collective-permute-start(bf16[512,128]{1,0:T(8,128)(2,1)S(1)} %get-tuple-element.53), channel_id=1, source_target_pairs={{0,8},{4,12},{8,0},{12,4},{16,24},{20,28},{24,16},{28,20},{1,9},{5... | collective-permute-start | bytes 393224 | tf_op jit(solution)/shard_map/ppermute | solution.py:382
  123.2 62.0 %copy-start.2 = (bf16[1024,1024]{1,0:T(8,128)(2,1)S(1)}, bf16[1024,1024]{1,0:T(8,128)(2,1)}, u32[]{:S(2)}) copy-start(bf16[1024,1024]{1,0:T(8,128)(2,1)} %w_out.1) | copy-start | bytes 6291460
  123.2 62.0 %copy-start.3 = (f32[1024]{0:T(1024)S(1)}, f32[1024]{0:T(1024)}, u32[]{:S(2)}) copy-start(f32[1024]{0:T(1024)} %param.12) | copy-start | bytes 12292
  123.2 62.0 %copy-start.4 = (s32[1,4,128]{2,1,0:T(4,128)S(1)}, s32[1,4,128]{2,1,0:T(4,128)}, u32[]{:S(2)}) copy-start(s32[1,4,128]{2,1,0:T(4,128)} %param.15) | copy-start | bytes 6148
  123.2 62.0 %copy-start.5 = (s32[1,4]{1,0:T(1,128)S(1)}, s32[1,4]{1,0:T(1,128)}, u32[]{:S(2)}) copy-start(s32[1,4]{1,0:T(1,128)} %bases.1) | copy-start | bytes 52
  123.2 56.9 %collective-permute-start.19 = (bf16[512,128]{1,0:T(8,128)(2,1)S(1)}, bf16[512,128]{1,0:T(8,128)(2,1)S(1)}, u32[]{:S(2)}, u32[]{:S(2)}) collective-permute-start(bf16[512,128]{1,0:T(8,128)(2,1)S(1)} %get-tuple-element.54), channel_id=1, source_target_pairs={{0,12},{4,8},{8,4},{12,0},{16,28},{20,24},{24,20},{28,16},{1,13},{... | collective-permute-start | bytes 393224 | tf_op jit(solution)/shard_map/ppermute | solution.py:382
  175.8 5.2 %collective-permute-start.7 = (bf16[512,128]{1,0:T(8,128)(2,1)}, bf16[512,128]{1,0:T(8,128)(2,1)S(1)}, u32[]{:S(2)}, u32[]{:S(2)}) collective-permute-start(bf16[512,128]{1,0:T(8,128)(2,1)} %get-tuple-element.40), channel_id=1, source_target_pairs={{0,4},{4,0},{8,12},{12,8},{16,20},{20,16},{24,28},{28,24},{1,5},{5... | collective-permute-start | bytes 393224 | tf_op jit(solution)/shard_map/ppermute | solution.py:382
  177.3 5.2 %collective-permute-start.8 = (bf16[512,128]{1,0:T(8,128)(2,1)}, bf16[512,128]{1,0:T(8,128)(2,1)S(1)}, u32[]{:S(2)}, u32[]{:S(2)}) collective-permute-start(bf16[512,128]{1,0:T(8,128)(2,1)} %get-tuple-element.41), channel_id=1, source_target_pairs={{0,8},{4,12},{8,0},{12,4},{16,24},{20,28},{24,16},{28,20},{1,9},{5... | collective-permute-start | bytes 393224 | tf_op jit(solution)/shard_map/ppermute | solution.py:382
  179.3 5.9 %collective-permute-start.9 = (bf16[512,128]{1,0:T(8,128)(2,1)S(1)}, bf16[512,128]{1,0:T(8,128)(2,1)S(1)}, u32[]{:S(2)}, u32[]{:S(2)}) collective-permute-start(bf16[512,128]{1,0:T(8,128)(2,1)S(1)} %get-tuple-element.42), channel_id=1, source_target_pairs={{0,12},{4,8},{8,4},{12,0},{16,28},{20,24},{24,20},{28,16},{1,13},{... | collective-permute-start | bytes 393224 | tf_op jit(solution)/shard_map/ppermute | solution.py:382
  188.3 1.9 collective-permute-start.20
  188.3 4.8 %collective-permute-start.21 = (bf16[32,1152]{1,0:T(8,128)(2,1)S(1)}, bf16[32,1152]{1,0:T(8,128)(2,1)S(1)}, u32[]{:S(2)}, u32[]{:S(2)}) collective-permute-start(bf16[32,1152]{1,0:T(8,128)(2,1)S(1)} %get-tuple-element.58), channel_id=1, source_target_pairs={{0,2},{1,3},{2,0},{3,1},{4,6},{5,7},{6,4},{7,5},{8,10},{9,11},{10,... | collective-permute-start | bytes 221192 | tf_op jit(solution)/shard_map/ppermute | solution.py:382
  189.9 4.5 %collective-permute-start.22 = (bf16[32,1152]{1,0:T(8,128)(2,1)S(1)}, bf16[32,1152]{1,0:T(8,128)(2,1)S(1)}, u32[]{:S(2)}, u32[]{:S(2)}) collective-permute-start(bf16[32,1152]{1,0:T(8,128)(2,1)S(1)} %get-tuple-element.59), channel_id=1, source_target_pairs={{0,3},{1,2},{2,1},{3,0},{4,7},{5,6},{6,5},{7,4},{8,11},{9,10},{10,... | collective-permute-start | bytes 221192 | tf_op jit(solution)/shard_map/ppermute | solution.py:382

commit v4 on v3

--- a/solution.py
+++ b/solution.py
@@ -56,7 +56,6 @@
     row = lax.broadcasted_iota(jnp.int32, (LANDMARKS, frames), 0)
     frame = lax.broadcasted_iota(jnp.int32, (LANDMARKS, frames), 1)
     member = ((frame >= row * span) & (frame < (row + 1) * span)).astype(BF16)
-    lane_row = lax.broadcasted_iota(jnp.int32, (LANES, LANDMARKS), 0)
     ones = jnp.ones((ONES, frames), BF16)
     scores = (score_a, score_b)
     stores = []
@@ -64,15 +63,13 @@
     def prepare(i):
         for load in loads[i]:
             load.wait()
-        mark_q = (dot(member, packs[i, pl.ds(0, frames)]) * (1.0 / span)).astype(BF16).astype(F32).T
+        mark_q = (dot(member, packs[i, pl.ds(0, frames)]) * (1.0 / span)).astype(BF16)
         mark_k = (dot(member, ins[i, 0]) * (1.0 / span)).astype(BF16)
         packs[i, pl.ds(frames, LANDMARKS)] = mark_k
-        return mark_q, ins[i, 1].astype(F32).T.astype(BF16)
+        return head_queries(mark_q, head_dim), ins[i, 1].T
 
     def score(i, h, slot, mark_q):
-        low = h * head_dim
-        own = jnp.where((lane_row >= low) & (lane_row < low + head_dim), mark_q, 0.0).astype(BF16)
-        part = dot(ins[i, 0], own)
+        part = dot(ins[i, 0], mark_q[h])
         scores[slot][...] = part
         return jnp.max(part, axis=0, keepdims=True)
 
@@ -130,7 +127,7 @@
 
 
 def head_queries(block, head_dim):
-    flat = block.astype(F32).T.astype(BF16)
+    flat = block.T
     parts = []
     for low in range(0, LANES, head_dim):
         pieces = [jnp.zeros((low, flat.shape[1]), BF16), flat[low : low + head_dim]]

time: 195 us -> 195 us (level)
  no operation moved by 1% of the time
where the time goes in v4:
time: 195 us
  Pallas kernels  129 us (66%)
  starting transfers between devices  39.2 us (20%)
  waiting for transfers between devices  25 us (13%)
    pallas_call x2, Pallas kernels, mix_far(): pl.pallas_call(functools.partial(far_kernel, team, sources, first, frames...  103 us
    ppermute x23, starting transfers between devices, swap(): return lax.ppermute(array, axis, [(i, i ^ bits) for i in range(size)])  39.2 us
    ppermute x23, waiting for transfers between devices, swap(): return lax.ppermute(array, axis, [(i, i ^ bits) for i in range(size)])  25 us
    pallas_call x3, Pallas kernels, mark_strips(): pl.pallas_call(functools.partial(marks_kernel, team, streams, stream, des...  12.8 us
    pallas_call x3, Pallas kernels, mix_part(): pl.pallas_call(functools.partial(part_kernel, team, len(marks), base, fra...  9.28 us
  transfers between devices with their start and end apart: 23, of which 10 were waited for; matrix products, arithmetic and copies ran while one was open for 0% of the time, Pallas kernels for 61%

profile of v4, /device:TPU:0, one launch (start us, length us, event | category | flops | bytes accessed | tf_op | source)
XLA Modules:
  0.0 195.2 jit_solution(11296737681966111101)
XLA Ops:
  0.6 5.4 %shard_map.99 = (bf16[1024,128]{1,0:T(8,128)(2,1)}, bf16[1024,128]{1,0:T(8,128)(2,1)}, bf16[1024,128]{1,0:T(8,128)(2,1)}, bf16[1024,128]{1,0:T(8,128)(2,1)}, bf1...) custom-call(bf16[512,1024]{1,0:T(8,128)(2,1)} %bitcast.10, ...), custom_call_target="tpu_custom_call" | custom-call | tf_op jit(solution)/shard_map/pallas_call | solution.py:111
  6.0 3.0 %collective-permute-start.10 = (bf16[1024,128]{1,0:T(8,128)(2,1)}, bf16[1024,128]{1,0:T(8,128)(2,1)S(1)}, u32[]{:S(2)}, u32[]{:S(2)}) collective-permute-start(bf16[1024,128]{1,0:T(8,128)(2,1)} %get-tuple-element.44), channel_id=1, source_target_pairs={{0,4},{4,0},{8,12},{12,8},{16,20},{20,16},{24,28},{28,24},{1,5},{5... | collective-permute-start | bytes 786440 | tf_op jit(solution)/shard_map/ppermute | solution.py:379
  9.1 3.6 %collective-permute-start.13 = (bf16[512,128]{1,0:T(8,128)(2,1)}, bf16[512,128]{1,0:T(8,128)(2,1)S(1)}, u32[]{:S(2)}, u32[]{:S(2)}) collective-permute-start(bf16[512,128]{1,0:T(8,128)(2,1)} %get-tuple-element.47), channel_id=1, source_target_pairs={{0,28},{4,24},{8,20},{12,16},{16,12},{20,8},{24,4},{28,0},{1,29},{... | collective-permute-start | bytes 393224 | tf_op jit(solution)/shard_map/ppermute | solution.py:379
  12.6 0.0 collective-permute-start.14
  12.7 1.9 collective-permute-start.15
  14.6 2.1 %collective-permute-start.16 = (bf16[512,128]{1,0:T(8,128)(2,1)}, bf16[512,128]{1,0:T(8,128)(2,1)S(1)}, u32[]{:S(2)}, u32[]{:S(2)}) collective-permute-start(bf16[512,128]{1,0:T(8,128)(2,1)} %get-tuple-element.50), channel_id=1, source_target_pairs={{0,16},{4,20},{8,24},{12,28},{16,0},{20,4},{24,8},{28,12},{1,17},{... | collective-permute-start | bytes 393224 | tf_op jit(solution)/shard_map/ppermute | solution.py:379
  16.7 3.6 %shard_map.95 = (bf16[1024,128]{1,0:T(8,128)(2,1)}, bf16[1024,128]{1,0:T(8,128)(2,1)}, bf16[512,128]{1,0:T(8,128)(2,1)}, bf16[512,128]{1,0:T(8,128)(2,1)}) custom-call(bf16[512,1024]{1,0:T(8,128)(2,1)} %bitcast.11, bf16[512,1024]{1,0:T(8,128)(2,1)} %bitcast.14, bf16[512,1024]{1,0:T(8,128)(2,1)} %bitcast.17), custom_call_target="tpu_custom_call" | custom-call | tf_op jit(solution)/shard_map/pallas_call | solution.py:111
  20.4 0.0 copy-start.8
  20.4 3.7 %shard_map.96 = (bf16[1024,128]{1,0:T(8,128)(2,1)}, bf16[1024,128]{1,0:T(8,128)(2,1)}, bf16[512,128]{1,0:T(8,128)(2,1)}, bf16[512,128]{1,0:T(8,128)(2,1)}) custom-call(bf16[512,1024]{1,0:T(8,128)(2,1)} %bitcast.12, bf16[512,1024]{1,0:T(8,128)(2,1)} %bitcast.15, bf16[512,1024]{1,0:T(8,128)(2,1)} %bitcast.18), custom_call_target="tpu_custom_call" | custom-call | tf_op jit(solution)/shard_map/pallas_call | solution.py:111
  24.2 0.0 collective-permute-done.13.refs_4_
  24.2 4.7 %collective-permute-start.11 = (bf16[1024,128]{1,0:T(8,128)(2,1)S(1)}, bf16[1024,128]{1,0:T(8,128)(2,1)S(1)}, u32[]{:S(2)}, u32[]{:S(2)}) collective-permute-start(bf16[1024,128]{1,0:T(8,128)(2,1)S(1)} %copy-done.7), channel_id=1, source_target_pairs={{0,8},{4,12},{8,0},{12,4},{16,24},{20,28},{24,16},{28,20},{1,9},{5... | collective-permute-start | bytes 786440 | tf_op jit(solution)/shard_map/ppermute | solution.py:379
  28.8 2.8 %collective-permute-start.12 = (bf16[1024,128]{1,0:T(8,128)(2,1)S(1)}, bf16[1024,128]{1,0:T(8,128)(2,1)S(1)}, u32[]{:S(2)}, u32[]{:S(2)}) collective-permute-start(bf16[1024,128]{1,0:T(8,128)(2,1)S(1)} %copy-done.6), channel_id=1, source_target_pairs={{0,12},{4,8},{8,4},{12,0},{16,28},{20,24},{24,20},{28,16},{1,13},{... | collective-permute-start | bytes 786440 | tf_op jit(solution)/shard_map/ppermute | solution.py:379
  31.6 2.3 %collective-permute-done.15.refs_6_ = bf16[512,128]{1,0:T(8,128)(2,1)S(1)} collective-permute-done((bf16[512,128]{1,0:T(8,128)(2,1)}, bf16[512,128]{1,0:T(8,128)(2,1)S(1)}, u32[]{:S(2)}, u32[]{:S(2)}) %collective-permute-start.15) | collective-permute-done | bytes 131104 | tf_op jit(solution)/shard_map/ppermute | solution.py:379
  34.0 0.6 collective-permute-start
  34.6 0.4 collective-permute-done.16.refs_7_
  35.0 3.0 %collective-permute-start.2 = (bf16[1024,128]{1,0:T(8,128)(2,1)}, bf16[1024,128]{1,0:T(8,128)(2,1)S(1)}, u32[]{:S(2)}, u32[]{:S(2)}) collective-permute-start(bf16[1024,128]{1,0:T(8,128)(2,1)} %get-tuple-element.34), channel_id=1, source_target_pairs={{0,12},{4,8},{8,4},{12,0},{16,28},{20,24},{24,20},{28,16},{1,13},{... | collective-permute-start | bytes 786440 | tf_op jit(solution)/shard_map/ppermute | solution.py:379
  37.9 2.7 %collective-permute-done.11.refs_2_.refs_6_ = bf16[1024,128]{1,0:T(8,128)(2,1)S(1)} collective-permute-done((bf16[1024,128]{1,0:T(8,128)(2,1)S(1)}, bf16[1024,128]{1,0:T(8,128)(2,1)S(1)}, u32[]{:S(2)}, u32[]{:S(2)}) %collective-permute-start.11) | collective-permute-done | bytes 262176 | tf_op jit(solution)/shard_map/ppermute | solution.py:379
  40.6 3.0 %collective-permute-start.3 = (bf16[512,128]{1,0:T(8,128)(2,1)}, bf16[512,128]{1,0:T(8,128)(2,1)S(1)}, u32[]{:S(2)}, u32[]{:S(2)}) collective-permute-start(bf16[512,128]{1,0:T(8,128)(2,1)} %get-tuple-element.35), channel_id=1, source_target_pairs={{0,28},{4,24},{8,20},{12,16},{16,12},{20,8},{24,4},{28,0},{1,29},{... | collective-permute-start | bytes 393224 | tf_op jit(solution)/shard_map/ppermute | solution.py:379
  43.6 3.2 %collective-permute-done.12.refs_3_.refs_7_ = bf16[1024,128]{1,0:T(8,128)(2,1)S(1)} collective-permute-done((bf16[1024,128]{1,0:T(8,128)(2,1)S(1)}, bf16[1024,128]{1,0:T(8,128)(2,1)S(1)}, u32[]{:S(2)}, u32[]{:S(2)}) %collective-permute-start.12) | collective-permute-done | bytes 262176 | tf_op jit(solution)/shard_map/ppermute | solution.py:379
  46.8 2.4 %collective-permute-start.4 = (bf16[512,128]{1,0:T(8,128)(2,1)}, bf16[512,128]{1,0:T(8,128)(2,1)S(1)}, u32[]{:S(2)}, u32[]{:S(2)}) collective-permute-start(bf16[512,128]{1,0:T(8,128)(2,1)} %get-tuple-element.36), channel_id=1, source_target_pairs={{0,24},{4,28},{8,16},{12,20},{16,8},{20,12},{24,0},{28,4},{1,25},{... | collective-permute-start | bytes 393224 | tf_op jit(solution)/shard_map/ppermute | solution.py:379
  49.2 0.0 collective-permute-done.refs_1_.refs_5_
  49.2 1.7 collective-permute-start.5
  50.9 7.2 %collective-permute-done.1.refs_2_.refs_6_ = bf16[1024,128]{1,0:T(8,128)(2,1)S(1)} collective-permute-done((bf16[1024,128]{1,0:T(8,128)(2,1)}, bf16[1024,128]{1,0:T(8,128)(2,1)S(1)}, u32[]{:S(2)}, u32[]{:S(2)}) %collective-permute-start.1) | collective-permute-done | bytes 262176 | tf_op jit(solution)/shard_map/ppermute | solution.py:379
  58.1 0.0 collective-permute-start.6
  58.1 3.5 %shard_map.100.refs_6_ = f32[4,2,80,512]{3,2,1,0:T(8,128)S(1)} custom-call(bf16[1024,128]{1,0:T(8,128)(2,1)S(1)} %copy-done, bf16[1024,128]{1,0:T(8,128)(2,1)S(1)} %collective-permute-done.10.refs_1_.refs_5_, bf16[1024,128]{1,0:T(8,128)(2,1)S(1)} %collective-permute-done.11.refs_2_.refs_6_, bf16[1024,128]{1,0:T(8,128)(2,1)S(1)} %collective-permute-done.12.refs_3_.refs_7_, ...), custom_call_target="tpu_custom_call" | custom-call | tf_op jit(solution)/shard_map/pallas_call | solution.py:191
  61.6 2.3 %shard_map.101.partial = f32[4,2,80,512]{3,2,1,0:T(8,128)S(1)} custom-call(bf16[1024,128]{1,0:T(8,128)(2,1)S(1)} %copy-done, bf16[1024,128]{1,0:T(8,128)(2,1)S(1)} %collective-permute-done.10.refs_1_.refs_5_, bf16[1024,128]{1,0:T(8,128)(2,1)S(1)} %collective-permute-done.11.refs_2_.refs_6_, bf16[1024,128]{1,0:T(8,128)(2,1)S(1)} %collective-permute-done.12.refs_3_.refs_7_, ...), custom_call_target="tpu_custom_call" | custom-call | tf_op jit(solution)/shard_map/pallas_call | solution.py:191
  63.9 0.0 copy-start.1
  63.9 50.6 %shard_map.102 = (bf16[512,128]{1,0:T(8,128)(2,1)S(1)}, bf16[512,128]{1,0:T(8,128)(2,1)S(1)}, bf16[512,128]{1,0:T(8,128)(2,1)S(1)}, bf16[512,128]{1,0:T(8,128)(2,1)S(1)}) custom-call(f32[4,2,80,512]{3,2,1,0:T(8,128)S(1)} %shard_map.101.partial, bf16[1024,128]{1,0:T(8,128)(2,1)S(1)} %copy-done, bf16[1024,128]{1,0:T(8,128)(2,1)S(1)} %collective-permute-done.10.refs_1_.refs_5_, ...), custom_call_target="tpu_custom_call" | custom-call | tf_op jit(solution)/shard_map/pallas_call | solution.py:268
  114.5 0.0 collective-permute-done.2.refs_3_.refs_7_
  114.5 2.4 %collective-permute-start.17 = (bf16[512,128]{1,0:T(8,128)(2,1)S(1)}, bf16[512,128]{1,0:T(8,128)(2,1)S(1)}, u32[]{:S(2)}, u32[]{:S(2)}) collective-permute-start(bf16[512,128]{1,0:T(8,128)(2,1)S(1)} %get-tuple-element.52), channel_id=1, source_target_pairs={{0,4},{4,0},{8,12},{12,8},{16,20},{20,16},{24,28},{28,24},{1,5},{5... | collective-permute-start | bytes 393224 | tf_op jit(solution)/shard_map/ppermute | solution.py:379
  116.9 3.5 %shard_map.97.partial = f32[4,2,80,512]{3,2,1,0:T(8,128)S(1)} custom-call(bf16[1024,128]{1,0:T(8,128)(2,1)S(1)} %copy-done.1, bf16[1024,128]{1,0:T(8,128)(2,1)S(1)} %collective-permute-done.refs_1_.refs_5_, bf16[1024,128]{1,0:T(8,128)(2,1)S(1)} %collective-permute-done.1.refs_2_.refs_6_, bf16[1024,128]{1,0:T(8,128)(2,1)S(1)} %collective-permute-done.2.refs_3_.refs_7_, ...), custom_call_target="tpu_custom_call" | custom-call | tf_op jit(solution)/shard_map/pallas_call | solution.py:191
  120.4 2.6 %collective-permute-start.18 = (bf16[512,128]{1,0:T(8,128)(2,1)S(1)}, bf16[512,128]{1,0:T(8,128)(2,1)S(1)}, u32[]{:S(2)}, u32[]{:S(2)}) collective-permute-start(bf16[512,128]{1,0:T(8,128)(2,1)S(1)} %get-tuple-element.53), channel_id=1, source_target_pairs={{0,8},{4,12},{8,0},{12,4},{16,24},{20,28},{24,16},{28,20},{1,9},{5... | collective-permute-start | bytes 393224 | tf_op jit(solution)/shard_map/ppermute | solution.py:379
  123.0 0.0 copy-start.5
  123.0 0.1 collective-permute-start.19
  123.1 52.6 %shard_map.98 = (bf16[512,128]{1,0:T(8,128)(2,1)S(1)}, bf16[512,128]{1,0:T(8,128)(2,1)}, bf16[512,128]{1,0:T(8,128)(2,1)}, bf16[512,128]{1,0:T(8,128)(2,1)S(1)}) custom-call(f32[4,2,80,512]{3,2,1,0:T(8,128)S(1)} %shard_map.97.partial, bf16[1024,128]{1,0:T(8,128)(2,1)S(1)} %copy-done.1, bf16[1024,128]{1,0:T(8,128)(2,1)S(1)} %collective-permute-done.refs_1_.refs_5_, ...), custom_call_target="tpu_custom_call" | custom-call | tf_op jit(solution)/shard_map/pallas_call | solution.py:268
  175.7 1.5 collective-permute-start.7
  177.1 2.0 %collective-permute-start.8 = (bf16[512,128]{1,0:T(8,128)(2,1)}, bf16[512,128]{1,0:T(8,128)(2,1)S(1)}, u32[]{:S(2)}, u32[]{:S(2)}) collective-permute-start(bf16[512,128]{1,0:T(8,128)(2,1)} %get-tuple-element.41), channel_id=1, source_target_pairs={{0,8},{4,12},{8,0},{12,4},{16,24},{20,28},{24,16},{28,20},{1,9},{5... | collective-permute-start | bytes 393224 | tf_op jit(solution)/shard_map/ppermute | solution.py:379
  179.1 0.0 collective-permute-start.9
  179.2 0.7 copy.10.owners
  179.9 0.9 collective-permute-done.7.refs_1_
  180.9 1.5 collective-permute-done.8.refs_2_
  182.3 2.7 %collective-permute-done.9.refs_3_ = bf16[512,128]{1,0:T(8,128)(2,1)S(1)} collective-permute-done((bf16[512,128]{1,0:T(8,128)(2,1)S(1)}, bf16[512,128]{1,0:T(8,128)(2,1)S(1)}, u32[]{:S(2)}, u32[]{:S(2)}) %collective-permute-start.9) | collective-permute-done | bytes 131104 | tf_op jit(solution)/shard_map/ppermute | solution.py:379
  185.0 3.2 %finish.1 = (bf16[512,1024]{1,0:T(8,128)(2,1)}, bf16[32,1152]{1,0:T(8,128)(2,1)S(1)}, bf16[32,1152]{1,0:T(8,128)(2,1)S(1)}, bf16[32,1152]{1,0:T(8,128)(2,1)S(1)}, bf16[32,1152]{1,0:T(8,128)(2,1)S(1)}) custom-call(s32[4,1]{1,0:T(4,128)S(1)} %copy.10.owners, s32[1,4]{1,0:T(1,128)S(1)} %copy-done.5, s32[4,128]{1,0:T(4,128)S(1)} %bitcast.9, ...), custom_call_target="tpu_custom_call" | custom-call | tf_op jit(solution)/shard_map/finish/pallas_call | solution.py:336
  188.2 1.5 collective-permute-start.21
  189.7 0.4 collective-permute-start.22
  190.1 3.0 %collective-permute-done.21.refs_2_ = bf16[32,1152]{1,0:T(8,128)(2,1)S(1)} collective-permute-done((bf16[32,1152]{1,0:T(8,128)(2,1)S(1)}, bf16[32,1152]{1,0:T(8,128)(2,1)S(1)}, u32[]{:S(2)}, u32[]{:S(2)}) %collective-permute-start.21) | collective-permute-done | bytes 73760 | tf_op jit(solution)/shard_map/ppermute | solution.py:379
  193.1 1.2 collective-permute-done.22.refs_3_
  194.2 0.9 pool.1
  (31 shorter events, 0.1 us)
Async XLA Ops:
  6.0 29.0 %collective-permute-start.10 = (bf16[1024,128]{1,0:T(8,128)(2,1)}, bf16[1024,128]{1,0:T(8,128)(2,1)S(1)}, u32[]{:S(2)}, u32[]{:S(2)}) collective-permute-start(bf16[1024,128]{1,0:T(8,128)(2,1)} %get-tuple-element.44), channel_id=1, source_target_pairs={{0,4},{4,0},{8,12},{12,8},{16,20},{20,16},{24,28},{28,24},{1,5},{5... | collective-permute-start | bytes 786440 | tf_op jit(solution)/shard_map/ppermute | solution.py:379
  9.1 15.1 %collective-permute-start.13 = (bf16[512,128]{1,0:T(8,128)(2,1)}, bf16[512,128]{1,0:T(8,128)(2,1)S(1)}, u32[]{:S(2)}, u32[]{:S(2)}) collective-permute-start(bf16[512,128]{1,0:T(8,128)(2,1)} %get-tuple-element.47), channel_id=1, source_target_pairs={{0,28},{4,24},{8,20},{12,16},{16,12},{20,8},{24,4},{28,0},{1,29},{... | collective-permute-start | bytes 393224 | tf_op jit(solution)/shard_map/ppermute | solution.py:379
  12.6 16.2 %collective-permute-start.14 = (bf16[512,128]{1,0:T(8,128)(2,1)}, bf16[512,128]{1,0:T(8,128)(2,1)S(1)}, u32[]{:S(2)}, u32[]{:S(2)}) collective-permute-start(bf16[512,128]{1,0:T(8,128)(2,1)} %get-tuple-element.48), channel_id=1, source_target_pairs={{0,24},{4,28},{8,16},{12,20},{16,8},{20,12},{24,0},{28,4},{1,25},{... | collective-permute-start | bytes 393224 | tf_op jit(solution)/shard_map/ppermute | solution.py:379
  12.7 21.3 %collective-permute-start.15 = (bf16[512,128]{1,0:T(8,128)(2,1)}, bf16[512,128]{1,0:T(8,128)(2,1)S(1)}, u32[]{:S(2)}, u32[]{:S(2)}) collective-permute-start(bf16[512,128]{1,0:T(8,128)(2,1)} %get-tuple-element.49), channel_id=1, source_target_pairs={{0,20},{4,16},{8,28},{12,24},{16,4},{20,0},{24,12},{28,8},{1,21},{... | collective-permute-start | bytes 393224 | tf_op jit(solution)/shard_map/ppermute | solution.py:379
  14.6 20.4 %collective-permute-start.16 = (bf16[512,128]{1,0:T(8,128)(2,1)}, bf16[512,128]{1,0:T(8,128)(2,1)S(1)}, u32[]{:S(2)}, u32[]{:S(2)}) collective-permute-start(bf16[512,128]{1,0:T(8,128)(2,1)} %get-tuple-element.50), channel_id=1, source_target_pairs={{0,16},{4,20},{8,24},{12,28},{16,0},{20,4},{24,8},{28,12},{1,17},{... | collective-permute-start | bytes 393224 | tf_op jit(solution)/shard_map/ppermute | solution.py:379
  20.4 3.8 %copy-start.7 = (bf16[1024,128]{1,0:T(8,128)(2,1)S(1)}, bf16[1024,128]{1,0:T(8,128)(2,1)}, u32[]{:S(2)}) copy-start(bf16[1024,128]{1,0:T(8,128)(2,1)} %get-tuple-element.45) | copy-start | bytes 786436
  20.4 8.5 %copy-start.6 = (bf16[1024,128]{1,0:T(8,128)(2,1)S(1)}, bf16[1024,128]{1,0:T(8,128)(2,1)}, u32[]{:S(2)}) copy-start(bf16[1024,128]{1,0:T(8,128)(2,1)} %get-tuple-element.46) | copy-start | bytes 786436
  20.4 13.6 %copy-start.8 = (bf16[1024,128]{1,0:T(8,128)(2,1)S(1)}, bf16[1024,128]{1,0:T(8,128)(2,1)}, u32[]{:S(2)}) copy-start(bf16[1024,128]{1,0:T(8,128)(2,1)} %get-tuple-element.32) | copy-start | bytes 786436
  20.4 28.8 %copy-start.10 = (bf16[512,128]{1,0:T(8,128)(2,1)S(1)}, bf16[512,128]{1,0:T(8,128)(2,1)}, u32[]{:S(2)}) copy-start(bf16[512,128]{1,0:T(8,128)(2,1)} %get-tuple-element.37) | copy-start | bytes 393220
  20.4 37.7 %copy-start.9 = (bf16[512,128]{1,0:T(8,128)(2,1)S(1)}, bf16[512,128]{1,0:T(8,128)(2,1)}, u32[]{:S(2)}) copy-start(bf16[512,128]{1,0:T(8,128)(2,1)} %get-tuple-element.38) | copy-start | bytes 393220
  20.4 37.7 %copy-start = (bf16[1024,128]{1,0:T(8,128)(2,1)S(1)}, bf16[1024,128]{1,0:T(8,128)(2,1)}, u32[]{:S(2)}) copy-start(bf16[1024,128]{1,0:T(8,128)(2,1)} %get-tuple-element.43.refs_0_.refs_4_) | copy-start | bytes 786436
  24.2 16.4 %collective-permute-start.11 = (bf16[1024,128]{1,0:T(8,128)(2,1)S(1)}, bf16[1024,128]{1,0:T(8,128)(2,1)S(1)}, u32[]{:S(2)}, u32[]{:S(2)}) collective-permute-start(bf16[1024,128]{1,0:T(8,128)(2,1)S(1)} %copy-done.7), channel_id=1, source_target_pairs={{0,8},{4,12},{8,0},{12,4},{16,24},{20,28},{24,16},{28,20},{1,9},{5... | collective-permute-start | bytes 786440 | tf_op jit(solution)/shard_map/ppermute | solution.py:379
  28.8 17.9 %collective-permute-start.12 = (bf16[1024,128]{1,0:T(8,128)(2,1)S(1)}, bf16[1024,128]{1,0:T(8,128)(2,1)S(1)}, u32[]{:S(2)}, u32[]{:S(2)}) collective-permute-start(bf16[1024,128]{1,0:T(8,128)(2,1)S(1)} %copy-done.6), channel_id=1, source_target_pairs={{0,12},{4,8},{8,4},{12,0},{16,28},{20,24},{24,20},{28,16},{1,13},{... | collective-permute-start | bytes 786440 | tf_op jit(solution)/shard_map/ppermute | solution.py:379
  34.0 15.2 %collective-permute-start = (bf16[1024,128]{1,0:T(8,128)(2,1)S(1)}, bf16[1024,128]{1,0:T(8,128)(2,1)S(1)}, u32[]{:S(2)}, u32[]{:S(2)}) collective-permute-start(bf16[1024,128]{1,0:T(8,128)(2,1)S(1)} %copy-done.8), channel_id=1, source_target_pairs={{0,4},{4,0},{8,12},{12,8},{16,20},{20,16},{24,28},{28,24},{1,5},{5... | collective-permute-start | bytes 786440 | tf_op jit(solution)/shard_map/ppermute | solution.py:379
  35.0 23.1 %collective-permute-start.1 = (bf16[1024,128]{1,0:T(8,128)(2,1)}, bf16[1024,128]{1,0:T(8,128)(2,1)S(1)}, u32[]{:S(2)}, u32[]{:S(2)}) collective-permute-start(bf16[1024,128]{1,0:T(8,128)(2,1)} %get-tuple-element.33), channel_id=1, source_target_pairs={{0,8},{4,12},{8,0},{12,4},{16,24},{20,28},{24,16},{28,20},{1,9},{5... | collective-permute-start | bytes 786440 | tf_op jit(solution)/shard_map/ppermute | solution.py:379
  35.0 79.5 %collective-permute-start.2 = (bf16[1024,128]{1,0:T(8,128)(2,1)}, bf16[1024,128]{1,0:T(8,128)(2,1)S(1)}, u32[]{:S(2)}, u32[]{:S(2)}) collective-permute-start(bf16[1024,128]{1,0:T(8,128)(2,1)} %get-tuple-element.34), channel_id=1, source_target_pairs={{0,12},{4,8},{8,4},{12,0},{16,28},{20,24},{24,20},{28,16},{1,13},{... | collective-permute-start | bytes 786440 | tf_op jit(solution)/shard_map/ppermute | solution.py:379
  40.6 79.8 %collective-permute-start.3 = (bf16[512,128]{1,0:T(8,128)(2,1)}, bf16[512,128]{1,0:T(8,128)(2,1)S(1)}, u32[]{:S(2)}, u32[]{:S(2)}) collective-permute-start(bf16[512,128]{1,0:T(8,128)(2,1)} %get-tuple-element.35), channel_id=1, source_target_pairs={{0,28},{4,24},{8,20},{12,16},{16,12},{20,8},{24,4},{28,0},{1,29},{... | collective-permute-start | bytes 393224 | tf_op jit(solution)/shard_map/ppermute | solution.py:379
  46.8 76.3 %collective-permute-start.4 = (bf16[512,128]{1,0:T(8,128)(2,1)}, bf16[512,128]{1,0:T(8,128)(2,1)S(1)}, u32[]{:S(2)}, u32[]{:S(2)}) collective-permute-start(bf16[512,128]{1,0:T(8,128)(2,1)} %get-tuple-element.36), channel_id=1, source_target_pairs={{0,24},{4,28},{8,16},{12,20},{16,8},{20,12},{24,0},{28,4},{1,25},{... | collective-permute-start | bytes 393224 | tf_op jit(solution)/shard_map/ppermute | solution.py:379
  49.2 73.9 %collective-permute-start.5 = (bf16[512,128]{1,0:T(8,128)(2,1)S(1)}, bf16[512,128]{1,0:T(8,128)(2,1)S(1)}, u32[]{:S(2)}, u32[]{:S(2)}) collective-permute-start(bf16[512,128]{1,0:T(8,128)(2,1)S(1)} %copy-done.10), channel_id=1, source_target_pairs={{0,20},{4,16},{8,28},{12,24},{16,4},{20,0},{24,12},{28,8},{1,21},{... | collective-permute-start | bytes 393224 | tf_op jit(solution)/shard_map/ppermute | solution.py:379
  58.1 65.1 %collective-permute-start.6 = (bf16[512,128]{1,0:T(8,128)(2,1)S(1)}, bf16[512,128]{1,0:T(8,128)(2,1)S(1)}, u32[]{:S(2)}, u32[]{:S(2)}) collective-permute-start(bf16[512,128]{1,0:T(8,128)(2,1)S(1)} %copy-done.9), channel_id=1, source_target_pairs={{0,16},{4,20},{8,24},{12,28},{16,0},{20,4},{24,8},{28,12},{1,17},{... | collective-permute-start | bytes 393224 | tf_op jit(solution)/shard_map/ppermute | solution.py:379
  63.9 53.0 %copy-start.1 = (bf16[1024,128]{1,0:T(8,128)(2,1)S(1)}, bf16[1024,128]{1,0:T(8,128)(2,1)}, u32[]{:S(2)}) copy-start(bf16[1024,128]{1,0:T(8,128)(2,1)} %get-tuple-element.31.refs_0_.refs_4_) | copy-start | bytes 786436
  114.5 64.6 %collective-permute-start.17 = (bf16[512,128]{1,0:T(8,128)(2,1)S(1)}, bf16[512,128]{1,0:T(8,128)(2,1)S(1)}, u32[]{:S(2)}, u32[]{:S(2)}) collective-permute-start(bf16[512,128]{1,0:T(8,128)(2,1)S(1)} %get-tuple-element.52), channel_id=1, source_target_pairs={{0,4},{4,0},{8,12},{12,8},{16,20},{20,16},{24,28},{28,24},{1,5},{5... | collective-permute-start | bytes 393224 | tf_op jit(solution)/shard_map/ppermute | solution.py:379
  120.4 59.5 %collective-permute-start.18 = (bf16[512,128]{1,0:T(8,128)(2,1)S(1)}, bf16[512,128]{1,0:T(8,128)(2,1)S(1)}, u32[]{:S(2)}, u32[]{:S(2)}) collective-permute-start(bf16[512,128]{1,0:T(8,128)(2,1)S(1)} %get-tuple-element.53), channel_id=1, source_target_pairs={{0,8},{4,12},{8,0},{12,4},{16,24},{20,28},{24,16},{28,20},{1,9},{5... | collective-permute-start | bytes 393224 | tf_op jit(solution)/shard_map/ppermute | solution.py:379
  123.0 62.0 %copy-start.2 = (bf16[1024,1024]{1,0:T(8,128)(2,1)S(1)}, bf16[1024,1024]{1,0:T(8,128)(2,1)}, u32[]{:S(2)}) copy-start(bf16[1024,1024]{1,0:T(8,128)(2,1)} %w_out.1) | copy-start | bytes 6291460
  123.0 62.0 %copy-start.3 = (f32[1024]{0:T(1024)S(1)}, f32[1024]{0:T(1024)}, u32[]{:S(2)}) copy-start(f32[1024]{0:T(1024)} %param.12) | copy-start | bytes 12292
  123.0 62.0 %copy-start.4 = (s32[1,4,128]{2,1,0:T(4,128)S(1)}, s32[1,4,128]{2,1,0:T(4,128)}, u32[]{:S(2)}) copy-start(s32[1,4,128]{2,1,0:T(4,128)} %param.15) | copy-start | bytes 6148
  123.0 62.0 %copy-start.5 = (s32[1,4]{1,0:T(1,128)S(1)}, s32[1,4]{1,0:T(1,128)}, u32[]{:S(2)}) copy-start(s32[1,4]{1,0:T(1,128)} %bases.1) | copy-start | bytes 52
  123.0 56.9 %collective-permute-start.19 = (bf16[512,128]{1,0:T(8,128)(2,1)S(1)}, bf16[512,128]{1,0:T(8,128)(2,1)S(1)}, u32[]{:S(2)}, u32[]{:S(2)}) collective-permute-start(bf16[512,128]{1,0:T(8,128)(2,1)S(1)} %get-tuple-element.54), channel_id=1, source_target_pairs={{0,12},{4,8},{8,4},{12,0},{16,28},{20,24},{24,20},{28,16},{1,13},{... | collective-permute-start | bytes 393224 | tf_op jit(solution)/shard_map/ppermute | solution.py:379
  175.7 5.2 %collective-permute-start.7 = (bf16[512,128]{1,0:T(8,128)(2,1)}, bf16[512,128]{1,0:T(8,128)(2,1)S(1)}, u32[]{:S(2)}, u32[]{:S(2)}) collective-permute-start(bf16[512,128]{1,0:T(8,128)(2,1)} %get-tuple-element.40), channel_id=1, source_target_pairs={{0,4},{4,0},{8,12},{12,8},{16,20},{20,16},{24,28},{28,24},{1,5},{5... | collective-permute-start | bytes 393224 | tf_op jit(solution)/shard_map/ppermute | solution.py:379
  177.1 5.2 %collective-permute-start.8 = (bf16[512,128]{1,0:T(8,128)(2,1)}, bf16[512,128]{1,0:T(8,128)(2,1)S(1)}, u32[]{:S(2)}, u32[]{:S(2)}) collective-permute-start(bf16[512,128]{1,0:T(8,128)(2,1)} %get-tuple-element.41), channel_id=1, source_target_pairs={{0,8},{4,12},{8,0},{12,4},{16,24},{20,28},{24,16},{28,20},{1,9},{5... | collective-permute-start | bytes 393224 | tf_op jit(solution)/shard_map/ppermute | solution.py:379
  179.1 5.9 %collective-permute-start.9 = (bf16[512,128]{1,0:T(8,128)(2,1)S(1)}, bf16[512,128]{1,0:T(8,128)(2,1)S(1)}, u32[]{:S(2)}, u32[]{:S(2)}) collective-permute-start(bf16[512,128]{1,0:T(8,128)(2,1)S(1)} %get-tuple-element.42), channel_id=1, source_target_pairs={{0,12},{4,8},{8,4},{12,0},{16,28},{20,24},{24,20},{28,16},{1,13},{... | collective-permute-start | bytes 393224 | tf_op jit(solution)/shard_map/ppermute | solution.py:379
  188.2 1.9 collective-permute-start.20
  188.2 4.9 %collective-permute-start.21 = (bf16[32,1152]{1,0:T(8,128)(2,1)S(1)}, bf16[32,1152]{1,0:T(8,128)(2,1)S(1)}, u32[]{:S(2)}, u32[]{:S(2)}) collective-permute-start(bf16[32,1152]{1,0:T(8,128)(2,1)S(1)} %get-tuple-element.58), channel_id=1, source_target_pairs={{0,2},{1,3},{2,0},{3,1},{4,6},{5,7},{6,4},{7,5},{8,10},{9,11},{10,... | collective-permute-start | bytes 221192 | tf_op jit(solution)/shard_map/ppermute | solution.py:379
  189.7 4.6 %collective-permute-start.22 = (bf16[32,1152]{1,0:T(8,128)(2,1)S(1)}, bf16[32,1152]{1,0:T(8,128)(2,1)S(1)}, u32[]{:S(2)}, u32[]{:S(2)}) collective-permute-start(bf16[32,1152]{1,0:T(8,128)(2,1)S(1)} %get-tuple-element.59), channel_id=1, source_target_pairs={{0,3},{1,2},{2,1},{3,0},{4,7},{5,6},{6,5},{7,4},{8,11},{9,10},{10,... | collective-permute-start | bytes 221192 | tf_op jit(solution)/shard_map/ppermute | solution.py:379

commit v5 on v4

--- a/solution.py
+++ b/solution.py
@@ -17,7 +17,7 @@
 LANES = 128
 ONES = 16
 SLOTS = 2
-QUERY_BLOCK = 256
+QUERY_BLOCK = 512
 BF16 = jnp.bfloat16
 F32 = jnp.float32
 
@@ -85,7 +85,7 @@
             top = score(j, g, 1 - slot, mark_q)
         weights = jnp.exp2((scores[slot][...] - most) * scale).astype(BF16)
         mixed = dot(jnp.concatenate([v_t[h * head_dim : (h + 1) * head_dim], ones], axis=0), weights)
-        heads.append(mixed[:head_dim] / mixed[head_dim : head_dim + 1])
+        heads.append(mixed[:head_dim] * (1.0 / mixed[head_dim : head_dim + 1]))
         if h < strip_heads - 1:
             continue
         mark_v, heads = jnp.concatenate(heads, axis=0).astype(BF16), []
@@ -213,9 +213,9 @@
         sums = sums + partial[n, h, :, columns]
         total = sums[head_dim : head_dim + 1]
         bounds[:] = [jnp.minimum(bounds[0], total), jnp.maximum(bounds[1], total)]
-        heads.append(sums[:head_dim] / total)
+        heads.append((sums[:head_dim] * (1.0 / total)).astype(BF16))
         if h == strip_heads - 1:
-            outs[n][columns] = jnp.concatenate(heads, axis=0).T.astype(BF16)
+            outs[n][columns] = jnp.concatenate(heads, axis=0).T
             heads.clear()
 
     gather_sums(near, [(ref, 0) for ref in far[first:]], (weight_a, weight_b), head_dim, team, frames, done)
@@ -282,13 +282,43 @@
     )(partial, *near, *far)
 
 
-def finish_kernel(team, streams, packs, blocks, owners, bases, offsets, w_out, gain, *refs):
-    strips = refs[: team * streams]
-    encoded = refs[team * streams]
-    sends = refs[team * streams + 1 :]
+def strips_product(strips, places, rows, w_out, me, streams):
+    total = None
+    for i in range(0, len(strips), 2):
+        left, right = [], []
+        for strip, (s, d) in zip(strips[i : i + 2], places[i : i + 2]):
+            first = pl.multiple_of((jnp.bitwise_xor(me, d) * streams + s) * LANES, LANES)
+            left.append(strip[rows])
+            right.append(w_out[pl.ds(first, LANES)])
+        part = dot(jnp.concatenate(left, axis=1), jnp.concatenate(right, axis=0))
+        total = part if total is None else total + part
+    return total
+
+
+def project_kernel(team, streams, places, w_out, *refs):
+    strips, projected = refs[:-1], refs[-1]
+    me = lax.axis_index("tm") % team
+    for b in range(projected.shape[0] // BLOCK):
+        rows = pl.ds(b * BLOCK, BLOCK)
+        projected[rows] = strips_product(strips, places, rows, w_out, me, streams)
+
+
+def project(strips, places, w_out, team, streams):
+    return pl.pallas_call(
+        functools.partial(project_kernel, team, streams, places),
+        out_shape=jax.ShapeDtypeStruct((strips[0].shape[0], w_out.shape[1]), F32),
+        in_specs=[VMEM] * (1 + len(strips)),
+        out_specs=VMEM,
+        compiler_params=pltpu.CompilerParams(vmem_limit_bytes=16 << 20),
+        name="project",
+    )(w_out, *strips)
+
+
+def finish_kernel(team, streams, packs, blocks, places, owners, bases, offsets, w_out, gain, begun, *refs):
+    strips, refs = refs[: len(places)], refs[len(places) :]
+    encoded_out, sends, (encoded, sems) = refs[0], refs[1 : 1 + packs], refs[1 + packs :]
     me = lax.axis_index("tm") % team
     my_pack = lax.axis_index("pack")
-    width = streams * LANES
     model = w_out.shape[1]
     slots = packs * SLOTS * WINDOW
     owner = [owners[b, 0] for b in range(blocks)]
@@ -309,16 +339,14 @@
     frame_counts = lax.dot_general(
         jnp.ones((SLOTS * WINDOW, blocks * BLOCK), BF16), hit, (((1,), (1,)), ((), ())), preferred_element_type=F32
     )
+    copies = []
     for b in range(blocks):
         rows = pl.ds(b * BLOCK, BLOCK)
-        projected = None
-        for d in range(team):
-            strip = jnp.concatenate([strips[s * team + d][rows] for s in range(streams)], axis=1)
-            first = pl.multiple_of(jnp.bitwise_xor(me, d) * width, LANES)
-            part = dot(strip, w_out[pl.ds(first, width)])
-            projected = part if projected is None else projected + part
+        projected = begun[rows] + strips_product(strips, places, rows, w_out, me, streams)
         power = jnp.mean(projected * projected, axis=-1, keepdims=True)
         encoded[rows] = (projected * lax.rsqrt(power + 1e-06) * gain[...]).astype(BF16)
+        copies.append(pltpu.make_async_copy(encoded.at[rows], encoded_out.at[rows], sems.at[b]))
+        copies[-1].start()
     sums = dot(hit, encoded[...]).astype(BF16)
     part = SLOTS * WINDOW
     meta_row = lax.broadcasted_iota(jnp.int32, (part, slots), 0)
@@ -326,21 +354,24 @@
     for e in range(packs):
         sends[e][:, pl.ds(0, model)] = sums[e * part : (e + 1) * part]
         sends[e][:, pl.ds(model, slots)] = meta.astype(BF16)
-
-
-def finish(strips, w_out, gain, owners, bases, offsets, team, streams, packs):
-    frames, model = strips[0].shape[0], w_out.shape[1]
+    for copy in copies:
+        copy.wait()
+
+
+def finish(begun, strips, places, w_out, gain, owners, bases, offsets, team, streams, packs):
+    frames, model = begun.shape
     blocks = owners.shape[0]
     part = SLOTS * WINDOW
     send = jax.ShapeDtypeStruct((part, model + packs * part), BF16)
     out = pl.pallas_call(
-        functools.partial(finish_kernel, team, streams, packs, blocks),
+        functools.partial(finish_kernel, team, streams, packs, blocks, places),
         out_shape=[jax.ShapeDtypeStruct((frames, model), BF16)] + [send] * packs,
-        in_specs=[SMEM, SMEM] + [VMEM] * (3 + len(strips)),
-        out_specs=[VMEM] * (1 + packs),
-        compiler_params=pltpu.CompilerParams(vmem_limit_bytes=24 << 20),
+        in_specs=[SMEM, SMEM] + [VMEM] * (4 + len(strips)),
+        out_specs=[ANY] + [VMEM] * packs,
+        scratch_shapes=[pltpu.VMEM((frames, model), BF16), pltpu.SemaphoreType.DMA((blocks,))],
+        compiler_params=pltpu.CompilerParams(vmem_limit_bytes=16 << 20),
         name="finish",
-    )(owners, bases, offsets, w_out, gain, *strips)
+    )(owners, bases, offsets, w_out, gain, begun, *strips)
     return out[0], out[1:]
 
 
@@ -385,7 +416,7 @@
     tm, packs = lax.axis_size("tm"), lax.axis_size("pack")
     head_dim = model // HEADS
     streams = model // team // LANES
-    near, far, strips = [], [], []
+    near, far, strips = [], [], {}
     for s in range(streams):
         near_out, far_out = {}, {}
         for dests in marks_turns(team, s):
@@ -400,9 +431,23 @@
         if half:
             partial = mix_part(near[s], far[s][:half], 0, partial, frames, head_dim)
         mixed = mix_far(partial, near[s], far[s], half, frames, head_dim)
-        strips += [mixed[0]] + [swap(mixed[d], "tm", tm, d) for d in range(1, team)]
+        strips[s, 0] = mixed[0]
+        strips.update({(s, d): swap(mixed[d], "tm", tm, d) for d in range(1, team)})
+    ends = [(streams - 1, d) for d in range(1, team)]
+    early = [place for place in strips if place not in ends]
+    begun = project([strips[place] for place in early], early, w_out, team, streams)
     encoded, sends = finish(
-        strips, w_out, norm_gain[None], block_owner[0], block_base, frame_offset[0], team, streams, packs
+        begun,
+        [strips[place] for place in ends],
+        ends,
+        w_out,
+        norm_gain[None],
+        block_owner[0],
+        block_base,
+        frame_offset[0],
+        team,
+        streams,
+        packs,
     )
     got = [sends[0]] + [swap(sends[e], "pack", packs, e) for e in range(1, packs)]
     return encoded[None], pool(got)[None]

time: 195 us -> 164 us (0.84)
  Pallas kernels: 129 us -> 92.8 us
  waiting for transfers between devices: 25 us -> 31.6 us
    pallas_call x2, Pallas kernels: 103 us -> 67 us  [mix_far(): pl.pallas_call(functools.partial(far_kernel, team, sources, first, frames...]
    ppermute x23, waiting for transfers between devices: 25 us -> 31.6 us  [swap(): return lax.ppermute(array, axis, [(i, i ^ bits) for i in range(size)])]
  transfers between devices with their start and end apart: 23 -> 23, of which waited for: 10 -> 10; matrix products, arithmetic and copies ran while one was open for 0% -> 0% of each run, Pallas kernels for 61% -> 51%
where the time goes in v5:
time: 164 us
  Pallas kernels  92.8 us (57%)
  starting transfers between devices  37.5 us (23%)
  waiting for transfers between devices  31.6 us (19%)
    pallas_call x2, Pallas kernels, mix_far(): pl.pallas_call(functools.partial(far_kernel, team, sources, first, frames...  67 us
    ppermute x23, starting transfers between devices, swap(): return lax.ppermute(array, axis, [(i, i ^ bits) for i in range(size)])  37.5 us
    ppermute x23, waiting for transfers between devices, swap(): return lax.ppermute(array, axis, [(i, i ^ bits) for i in range(size)])  31.6 us
    pallas_call x3, Pallas kernels, mark_strips(): pl.pallas_call(functools.partial(marks_kernel, team, streams, stream, des...  12.8 us
    pallas_call x3, Pallas kernels, mix_part(): pl.pallas_call(functools.partial(part_kernel, team, len(marks), base, fra...  8.82 us
  transfers between devices with their start and end apart: 23, of which 10 were waited for; matrix products, arithmetic and copies ran while one was open for 0% of the time, Pallas kernels for 51%

profile of v5, /device:TPU:0, one launch (start us, length us, event | category | flops | bytes accessed | tf_op | source)
XLA Modules:
  0.0 163.9 jit_solution(13974382640893062535)
XLA Ops:
  0.6 5.4 %shard_map.99 = (bf16[1024,128]{1,0:T(8,128)(2,1)}, bf16[1024,128]{1,0:T(8,128)(2,1)}, bf16[1024,128]{1,0:T(8,128)(2,1)}, bf16[1024,128]{1,0:T(8,128)(2,1)}, bf1...) custom-call(bf16[512,1024]{1,0:T(8,128)(2,1)} %bitcast.10, ...), custom_call_target="tpu_custom_call" | custom-call | tf_op jit(solution)/shard_map/pallas_call | solution.py:111
  6.0 3.0 %collective-permute-start.10 = (bf16[1024,128]{1,0:T(8,128)(2,1)}, bf16[1024,128]{1,0:T(8,128)(2,1)S(1)}, u32[]{:S(2)}, u32[]{:S(2)}) collective-permute-start(bf16[1024,128]{1,0:T(8,128)(2,1)} %get-tuple-element.44), channel_id=1, source_target_pairs={{0,4},{4,0},{8,12},{12,8},{16,20},{20,16},{24,28},{28,24},{1,5},{5... | collective-permute-start | bytes 786440 | tf_op jit(solution)/shard_map/ppermute | solution.py:410
  9.1 3.6 %shard_map.96 = (bf16[1024,128]{1,0:T(8,128)(2,1)}, bf16[1024,128]{1,0:T(8,128)(2,1)}, bf16[512,128]{1,0:T(8,128)(2,1)}, bf16[512,128]{1,0:T(8,128)(2,1)}) custom-call(bf16[512,1024]{1,0:T(8,128)(2,1)} %bitcast.11, bf16[512,1024]{1,0:T(8,128)(2,1)} %bitcast.14, bf16[512,1024]{1,0:T(8,128)(2,1)} %bitcast.17), custom_call_target="tpu_custom_call" | custom-call | tf_op jit(solution)/shard_map/pallas_call | solution.py:111
  12.7 3.6 %collective-permute-start.3 = (bf16[512,128]{1,0:T(8,128)(2,1)}, bf16[512,128]{1,0:T(8,128)(2,1)S(1)}, u32[]{:S(2)}, u32[]{:S(2)}) collective-permute-start(bf16[512,128]{1,0:T(8,128)(2,1)} %get-tuple-element.35), channel_id=1, source_target_pairs={{0,28},{4,24},{8,20},{12,16},{16,12},{20,8},{24,4},{28,0},{1,29},{... | collective-permute-start | bytes 393224 | tf_op jit(solution)/shard_map/ppermute | solution.py:410
  16.4 0.1 collective-permute-start.4
  16.5 3.7 %shard_map.95 = (bf16[1024,128]{1,0:T(8,128)(2,1)}, bf16[1024,128]{1,0:T(8,128)(2,1)}, bf16[512,128]{1,0:T(8,128)(2,1)}, bf16[512,128]{1,0:T(8,128)(2,1)}) custom-call(bf16[512,1024]{1,0:T(8,128)(2,1)} %bitcast.12, bf16[512,1024]{1,0:T(8,128)(2,1)} %bitcast.15, bf16[512,1024]{1,0:T(8,128)(2,1)} %bitcast.18), custom_call_target="tpu_custom_call" | custom-call | tf_op jit(solution)/shard_map/pallas_call | solution.py:111
  20.3 1.8 %collective-permute-start.5 = (bf16[512,128]{1,0:T(8,128)(2,1)}, bf16[512,128]{1,0:T(8,128)(2,1)S(1)}, u32[]{:S(2)}, u32[]{:S(2)}) collective-permute-start(bf16[512,128]{1,0:T(8,128)(2,1)} %get-tuple-element.37), channel_id=1, source_target_pairs={{0,20},{4,16},{8,28},{12,24},{16,4},{20,0},{24,12},{28,8},{1,21},{... | collective-permute-start | bytes 393224 | tf_op jit(solution)/shard_map/ppermute | solution.py:410
  22.1 2.2 %collective-permute-start.6 = (bf16[512,128]{1,0:T(8,128)(2,1)}, bf16[512,128]{1,0:T(8,128)(2,1)S(1)}, u32[]{:S(2)}, u32[]{:S(2)}) collective-permute-start(bf16[512,128]{1,0:T(8,128)(2,1)} %get-tuple-element.38), channel_id=1, source_target_pairs={{0,16},{4,20},{8,24},{12,28},{16,0},{20,4},{24,8},{28,12},{1,17},{... | collective-permute-start | bytes 393224 | tf_op jit(solution)/shard_map/ppermute | solution.py:410
  24.3 7.8 %collective-permute-start.11 = (bf16[1024,128]{1,0:T(8,128)(2,1)S(1)}, bf16[1024,128]{1,0:T(8,128)(2,1)S(1)}, u32[]{:S(2)}, u32[]{:S(2)}) collective-permute-start(bf16[1024,128]{1,0:T(8,128)(2,1)S(1)} %copy-done.11), channel_id=1, source_target_pairs={{0,8},{4,12},{8,0},{12,4},{16,24},{20,28},{24,16},{28,20},{1,9},{5... | collective-permute-start | bytes 786440 | tf_op jit(solution)/shard_map/ppermute | solution.py:410
  32.1 0.7 collective-permute-start
  32.8 4.9 %collective-permute-done.5.refs_6_ = bf16[512,128]{1,0:T(8,128)(2,1)S(1)} collective-permute-done((bf16[512,128]{1,0:T(8,128)(2,1)}, bf16[512,128]{1,0:T(8,128)(2,1)S(1)}, u32[]{:S(2)}, u32[]{:S(2)}) %collective-permute-start.5) | collective-permute-done | bytes 131104 | tf_op jit(solution)/shard_map/ppermute | solution.py:410
  37.7 1.0 collective-permute-done.6.refs_7_
  38.7 1.1 collective-permute-start.2
  39.8 1.8 %collective-permute-start.12 = (bf16[1024,128]{1,0:T(8,128)(2,1)S(1)}, bf16[1024,128]{1,0:T(8,128)(2,1)S(1)}, u32[]{:S(2)}, u32[]{:S(2)}) collective-permute-start(bf16[1024,128]{1,0:T(8,128)(2,1)S(1)} %copy-done.8), channel_id=1, source_target_pairs={{0,12},{4,8},{8,4},{12,0},{16,28},{20,24},{24,20},{28,16},{1,13},{... | collective-permute-start | bytes 786440 | tf_op jit(solution)/shard_map/ppermute | solution.py:410
  41.6 2.2 %collective-permute-done.11.refs_2_.refs_6_ = bf16[1024,128]{1,0:T(8,128)(2,1)S(1)} collective-permute-done((bf16[1024,128]{1,0:T(8,128)(2,1)S(1)}, bf16[1024,128]{1,0:T(8,128)(2,1)S(1)}, u32[]{:S(2)}, u32[]{:S(2)}) %collective-permute-start.11) | collective-permute-done | bytes 262176 | tf_op jit(solution)/shard_map/ppermute | solution.py:410
  43.8 2.9 %collective-permute-start.13 = (bf16[512,128]{1,0:T(8,128)(2,1)S(1)}, bf16[512,128]{1,0:T(8,128)(2,1)S(1)}, u32[]{:S(2)}, u32[]{:S(2)}) collective-permute-start(bf16[512,128]{1,0:T(8,128)(2,1)S(1)} %copy-done.15), channel_id=1, source_target_pairs={{0,28},{4,24},{8,20},{12,16},{16,12},{20,8},{24,4},{28,0},{1,29},{... | collective-permute-start | bytes 393224 | tf_op jit(solution)/shard_map/ppermute | solution.py:410
  46.8 1.1 collective-permute-start.14
  47.9 2.2 %collective-permute-done.1.refs_2_.refs_6_ = bf16[1024,128]{1,0:T(8,128)(2,1)S(1)} collective-permute-done((bf16[1024,128]{1,0:T(8,128)(2,1)S(1)}, bf16[1024,128]{1,0:T(8,128)(2,1)S(1)}, u32[]{:S(2)}, u32[]{:S(2)}) %collective-permute-start.1) | collective-permute-done | bytes 262176 | tf_op jit(solution)/shard_map/ppermute | solution.py:410
  50.1 1.0 collective-permute-start.15
  51.0 12.7 %collective-permute-done.2.refs_3_.refs_7_ = bf16[1024,128]{1,0:T(8,128)(2,1)S(1)} collective-permute-done((bf16[1024,128]{1,0:T(8,128)(2,1)S(1)}, bf16[1024,128]{1,0:T(8,128)(2,1)S(1)}, u32[]{:S(2)}, u32[]{:S(2)}) %collective-permute-start.2) | collective-permute-done | bytes 262176 | tf_op jit(solution)/shard_map/ppermute | solution.py:410
  63.8 0.9 copy-done.2
  64.7 3.4 %shard_map.97.partial = f32[4,2,80,512]{3,2,1,0:T(8,128)S(1)} custom-call(bf16[1024,128]{1,0:T(8,128)(2,1)S(1)} %copy-done.2, bf16[1024,128]{1,0:T(8,128)(2,1)S(1)} %collective-permute-done.refs_1_.refs_5_, bf16[1024,128]{1,0:T(8,128)(2,1)S(1)} %collective-permute-done.1.refs_2_.refs_6_, bf16[1024,128]{1,0:T(8,128)(2,1)S(1)} %collective-permute-done.2.refs_3_.refs_7_, ...), custom_call_target="tpu_custom_call" | custom-call | tf_op jit(solution)/shard_map/pallas_call | solution.py:191
  68.2 33.9 %shard_map.98 = (bf16[512,128]{1,0:T(8,128)(2,1)S(1)}, bf16[512,128]{1,0:T(8,128)(2,1)S(1)}, bf16[512,128]{1,0:T(8,128)(2,1)S(1)}, bf16[512,128]{1,0:T(8,128)(2,1)S(1)}) custom-call(f32[4,2,80,512]{3,2,1,0:T(8,128)S(1)} %shard_map.97.partial, bf16[1024,128]{1,0:T(8,128)(2,1)S(1)} %copy-done.3, bf16[1024,128]{1,0:T(8,128)(2,1)S(1)} %collective-permute-done.refs_1_.refs_5_, ...), custom_call_target="tpu_custom_call" | custom-call | tf_op jit(solution)/shard_map/pallas_call | solution.py:268
  102.0 1.5 collective-permute-start.7
  103.6 3.4 %shard_map.100.refs_6_ = f32[4,2,80,512]{3,2,1,0:T(8,128)S(1)} custom-call(bf16[1024,128]{1,0:T(8,128)(2,1)S(1)} %copy-done.1, bf16[1024,128]{1,0:T(8,128)(2,1)S(1)} %collective-permute-done.10.refs_1_.refs_5_, bf16[1024,128]{1,0:T(8,128)(2,1)S(1)} %collective-permute-done.11.refs_2_.refs_6_, bf16[1024,128]{1,0:T(8,128)(2,1)S(1)} %collective-permute-done.12.refs_3_.refs_7_, ...), custom_call_target="tpu_custom_call" | custom-call | tf_op jit(solution)/shard_map/pallas_call | solution.py:191
  107.0 3.0 %collective-permute-start.8 = (bf16[512,128]{1,0:T(8,128)(2,1)S(1)}, bf16[512,128]{1,0:T(8,128)(2,1)S(1)}, u32[]{:S(2)}, u32[]{:S(2)}) collective-permute-start(bf16[512,128]{1,0:T(8,128)(2,1)S(1)} %get-tuple-element.41), channel_id=1, source_target_pairs={{0,8},{4,12},{8,0},{12,4},{16,24},{20,28},{24,16},{28,20},{1,9},{5... | collective-permute-start | bytes 393224 | tf_op jit(solution)/shard_map/ppermute | solution.py:410
  110.0 0.2 collective-permute-start.9
  110.3 2.0 %shard_map.101.partial = f32[4,2,80,512]{3,2,1,0:T(8,128)S(1)} custom-call(bf16[1024,128]{1,0:T(8,128)(2,1)S(1)} %copy-done.1, bf16[1024,128]{1,0:T(8,128)(2,1)S(1)} %collective-permute-done.10.refs_1_.refs_5_, bf16[1024,128]{1,0:T(8,128)(2,1)S(1)} %collective-permute-done.11.refs_2_.refs_6_, bf16[1024,128]{1,0:T(8,128)(2,1)S(1)} %collective-permute-done.12.refs_3_.refs_7_, ...), custom_call_target="tpu_custom_call" | custom-call | tf_op jit(solution)/shard_map/pallas_call | solution.py:191
  112.3 0.0 copy-start.7
  112.3 0.0 copy-start
  112.3 33.1 %shard_map.102 = (bf16[512,128]{1,0:T(8,128)(2,1)S(1)}, bf16[512,128]{1,0:T(8,128)(2,1)}, bf16[512,128]{1,0:T(8,128)(2,1)}, bf16[512,128]{1,0:T(8,128)(2,1)S(1)}) custom-call(f32[4,2,80,512]{3,2,1,0:T(8,128)S(1)} %shard_map.101.partial, bf16[1024,128]{1,0:T(8,128)(2,1)S(1)} %copy-done.1, bf16[1024,128]{1,0:T(8,128)(2,1)S(1)} %collective-permute-done.10.refs_1_.refs_5_, ...), custom_call_target="tpu_custom_call" | custom-call | tf_op jit(solution)/shard_map/pallas_call | solution.py:268
  145.4 1.3 collective-permute-start.17
  146.7 1.9 %collective-permute-start.18 = (bf16[512,128]{1,0:T(8,128)(2,1)}, bf16[512,128]{1,0:T(8,128)(2,1)S(1)}, u32[]{:S(2)}, u32[]{:S(2)}) collective-permute-start(bf16[512,128]{1,0:T(8,128)(2,1)} %get-tuple-element.53), channel_id=1, source_target_pairs={{0,8},{4,12},{8,0},{12,4},{16,24},{20,28},{24,16},{28,20},{1,9},{5... | collective-permute-start | bytes 393224 | tf_op jit(solution)/shard_map/ppermute | solution.py:410
  148.7 0.2 collective-permute-start.19
  148.9 0.1 copy.10.owners
  149.0 0.0 copy-start.4
  149.1 0.0 copy-start.6
  149.1 1.0 project.1.begun
  150.1 0.5 collective-permute-done.17.refs_0_
  150.6 1.3 collective-permute-done.18.refs_1_
  151.9 2.6 %collective-permute-done.19.refs_2_ = bf16[512,128]{1,0:T(8,128)(2,1)S(1)} collective-permute-done((bf16[512,128]{1,0:T(8,128)(2,1)S(1)}, bf16[512,128]{1,0:T(8,128)(2,1)S(1)}, u32[]{:S(2)}, u32[]{:S(2)}) %collective-permute-start.19) | collective-permute-done | bytes 131104 | tf_op jit(solution)/shard_map/ppermute | solution.py:410
  154.6 2.3 %finish.1 = (bf16[512,1024]{1,0:T(8,128)(2,1)}, bf16[32,1152]{1,0:T(8,128)(2,1)S(1)}, bf16[32,1152]{1,0:T(8,128)(2,1)S(1)}, bf16[32,1152]{1,0:T(8,128)(2,1)S(1)}, bf16[32,1152]{1,0:T(8,128)(2,1)S(1)}) custom-call(s32[4,1]{1,0:T(4,128)S(1)} %copy.10.owners, s32[1,4]{1,0:T(1,128)S(1)} %copy-done.6, s32[4,128]{1,0:T(4,128)S(1)} %bitcast.9, ...), custom_call_target="tpu_custom_call" | custom-call | tf_op jit(solution)/shard_map/finish/pallas_call | solution.py:366
  156.9 0.1 collective-permute-start.20
  157.0 1.6 collective-permute-start.21
  158.6 0.2 collective-permute-start.22
  158.8 2.9 %collective-permute-done.21.refs_2_ = bf16[32,1152]{1,0:T(8,128)(2,1)S(1)} collective-permute-done((bf16[32,1152]{1,0:T(8,128)(2,1)S(1)}, bf16[32,1152]{1,0:T(8,128)(2,1)S(1)}, u32[]{:S(2)}, u32[]{:S(2)}) %collective-permute-start.21) | collective-permute-done | bytes 73760 | tf_op jit(solution)/shard_map/ppermute | solution.py:410
  161.7 1.3 collective-permute-done.22.refs_3_
  162.9 0.9 pool.1
  (42 shorter events, 0.1 us)
Async XLA Ops:
  6.0 33.8 %collective-permute-start.10 = (bf16[1024,128]{1,0:T(8,128)(2,1)}, bf16[1024,128]{1,0:T(8,128)(2,1)S(1)}, u32[]{:S(2)}, u32[]{:S(2)}) collective-permute-start(bf16[1024,128]{1,0:T(8,128)(2,1)} %get-tuple-element.44), channel_id=1, source_target_pairs={{0,4},{4,0},{8,12},{12,8},{16,20},{20,16},{24,28},{28,24},{1,5},{5... | collective-permute-start | bytes 786440 | tf_op jit(solution)/shard_map/ppermute | solution.py:410
  12.7 11.6 %collective-permute-start.3 = (bf16[512,128]{1,0:T(8,128)(2,1)}, bf16[512,128]{1,0:T(8,128)(2,1)S(1)}, u32[]{:S(2)}, u32[]{:S(2)}) collective-permute-start(bf16[512,128]{1,0:T(8,128)(2,1)} %get-tuple-element.35), channel_id=1, source_target_pairs={{0,28},{4,24},{8,20},{12,16},{16,12},{20,8},{24,4},{28,0},{1,29},{... | collective-permute-start | bytes 393224 | tf_op jit(solution)/shard_map/ppermute | solution.py:410
  16.3 8.0 %copy-start.11 = (bf16[1024,128]{1,0:T(8,128)(2,1)S(1)}, bf16[1024,128]{1,0:T(8,128)(2,1)}, u32[]{:S(2)}) copy-start(bf16[1024,128]{1,0:T(8,128)(2,1)} %get-tuple-element.45) | copy-start | bytes 786436
  16.3 21.3 %copy-start.10 = (bf16[1024,128]{1,0:T(8,128)(2,1)S(1)}, bf16[1024,128]{1,0:T(8,128)(2,1)}, u32[]{:S(2)}) copy-start(bf16[1024,128]{1,0:T(8,128)(2,1)} %get-tuple-element.33) | copy-start | bytes 786436
  16.4 22.3 %copy-start.9 = (bf16[1024,128]{1,0:T(8,128)(2,1)S(1)}, bf16[1024,128]{1,0:T(8,128)(2,1)}, u32[]{:S(2)}) copy-start(bf16[1024,128]{1,0:T(8,128)(2,1)} %get-tuple-element.34) | copy-start | bytes 786436
  16.4 23.4 %copy-start.8 = (bf16[1024,128]{1,0:T(8,128)(2,1)S(1)}, bf16[1024,128]{1,0:T(8,128)(2,1)}, u32[]{:S(2)}) copy-start(bf16[1024,128]{1,0:T(8,128)(2,1)} %get-tuple-element.46) | copy-start | bytes 786436
  16.4 27.5 %copy-start.15 = (bf16[512,128]{1,0:T(8,128)(2,1)S(1)}, bf16[512,128]{1,0:T(8,128)(2,1)}, u32[]{:S(2)}) copy-start(bf16[512,128]{1,0:T(8,128)(2,1)} %get-tuple-element.47) | copy-start | bytes 393220
  16.4 30.4 %copy-start.14 = (bf16[512,128]{1,0:T(8,128)(2,1)S(1)}, bf16[512,128]{1,0:T(8,128)(2,1)}, u32[]{:S(2)}) copy-start(bf16[512,128]{1,0:T(8,128)(2,1)} %get-tuple-element.48) | copy-start | bytes 393220
  16.4 33.7 %copy-start.13 = (bf16[512,128]{1,0:T(8,128)(2,1)S(1)}, bf16[512,128]{1,0:T(8,128)(2,1)}, u32[]{:S(2)}) copy-start(bf16[512,128]{1,0:T(8,128)(2,1)} %get-tuple-element.49) | copy-start | bytes 393220
  16.4 47.4 %copy-start.12 = (bf16[512,128]{1,0:T(8,128)(2,1)S(1)}, bf16[512,128]{1,0:T(8,128)(2,1)}, u32[]{:S(2)}) copy-start(bf16[512,128]{1,0:T(8,128)(2,1)} %get-tuple-element.50) | copy-start | bytes 393220
  16.4 15.7 %collective-permute-start.4 = (bf16[512,128]{1,0:T(8,128)(2,1)}, bf16[512,128]{1,0:T(8,128)(2,1)S(1)}, u32[]{:S(2)}, u32[]{:S(2)}) collective-permute-start(bf16[512,128]{1,0:T(8,128)(2,1)} %get-tuple-element.36), channel_id=1, source_target_pairs={{0,24},{4,28},{8,16},{12,20},{16,8},{20,12},{24,0},{28,4},{1,25},{... | collective-permute-start | bytes 393224 | tf_op jit(solution)/shard_map/ppermute | solution.py:410
  20.3 17.4 %collective-permute-start.5 = (bf16[512,128]{1,0:T(8,128)(2,1)}, bf16[512,128]{1,0:T(8,128)(2,1)S(1)}, u32[]{:S(2)}, u32[]{:S(2)}) collective-permute-start(bf16[512,128]{1,0:T(8,128)(2,1)} %get-tuple-element.37), channel_id=1, source_target_pairs={{0,20},{4,16},{8,28},{12,24},{16,4},{20,0},{24,12},{28,8},{1,21},{... | collective-permute-start | bytes 393224 | tf_op jit(solution)/shard_map/ppermute | solution.py:410
  22.1 16.6 %collective-permute-start.6 = (bf16[512,128]{1,0:T(8,128)(2,1)}, bf16[512,128]{1,0:T(8,128)(2,1)S(1)}, u32[]{:S(2)}, u32[]{:S(2)}) collective-permute-start(bf16[512,128]{1,0:T(8,128)(2,1)} %get-tuple-element.38), channel_id=1, source_target_pairs={{0,16},{4,20},{8,24},{12,28},{16,0},{20,4},{24,8},{28,12},{1,17},{... | collective-permute-start | bytes 393224 | tf_op jit(solution)/shard_map/ppermute | solution.py:410
  24.3 19.5 %collective-permute-start.11 = (bf16[1024,128]{1,0:T(8,128)(2,1)S(1)}, bf16[1024,128]{1,0:T(8,128)(2,1)S(1)}, u32[]{:S(2)}, u32[]{:S(2)}) collective-permute-start(bf16[1024,128]{1,0:T(8,128)(2,1)S(1)} %copy-done.11), channel_id=1, source_target_pairs={{0,8},{4,12},{8,0},{12,4},{16,24},{20,28},{24,16},{28,20},{1,9},{5... | collective-permute-start | bytes 786440 | tf_op jit(solution)/shard_map/ppermute | solution.py:410
  32.1 14.6 %collective-permute-start = (bf16[1024,128]{1,0:T(8,128)(2,1)}, bf16[1024,128]{1,0:T(8,128)(2,1)S(1)}, u32[]{:S(2)}, u32[]{:S(2)}) collective-permute-start(bf16[1024,128]{1,0:T(8,128)(2,1)} %get-tuple-element.32), channel_id=1, source_target_pairs={{0,4},{4,0},{8,12},{12,8},{16,20},{20,16},{24,28},{28,24},{1,5},{5... | collective-permute-start | bytes 786440 | tf_op jit(solution)/shard_map/ppermute | solution.py:410
  37.7 12.4 %collective-permute-start.1 = (bf16[1024,128]{1,0:T(8,128)(2,1)S(1)}, bf16[1024,128]{1,0:T(8,128)(2,1)S(1)}, u32[]{:S(2)}, u32[]{:S(2)}) collective-permute-start(bf16[1024,128]{1,0:T(8,128)(2,1)S(1)} %copy-done.10), channel_id=1, source_target_pairs={{0,8},{4,12},{8,0},{12,4},{16,24},{20,28},{24,16},{28,20},{1,9},{5... | collective-permute-start | bytes 786440 | tf_op jit(solution)/shard_map/ppermute | solution.py:410
  38.7 25.1 %collective-permute-start.2 = (bf16[1024,128]{1,0:T(8,128)(2,1)S(1)}, bf16[1024,128]{1,0:T(8,128)(2,1)S(1)}, u32[]{:S(2)}, u32[]{:S(2)}) collective-permute-start(bf16[1024,128]{1,0:T(8,128)(2,1)S(1)} %copy-done.9), channel_id=1, source_target_pairs={{0,12},{4,8},{8,4},{12,0},{16,28},{20,24},{24,20},{28,16},{1,13},{... | collective-permute-start | bytes 786440 | tf_op jit(solution)/shard_map/ppermute | solution.py:410
  39.8 62.2 %collective-permute-start.12 = (bf16[1024,128]{1,0:T(8,128)(2,1)S(1)}, bf16[1024,128]{1,0:T(8,128)(2,1)S(1)}, u32[]{:S(2)}, u32[]{:S(2)}) collective-permute-start(bf16[1024,128]{1,0:T(8,128)(2,1)S(1)} %copy-done.8), channel_id=1, source_target_pairs={{0,12},{4,8},{8,4},{12,0},{16,28},{20,24},{24,20},{28,16},{1,13},{... | collective-permute-start | bytes 786440 | tf_op jit(solution)/shard_map/ppermute | solution.py:410
  43.8 63.2 %collective-permute-start.13 = (bf16[512,128]{1,0:T(8,128)(2,1)S(1)}, bf16[512,128]{1,0:T(8,128)(2,1)S(1)}, u32[]{:S(2)}, u32[]{:S(2)}) collective-permute-start(bf16[512,128]{1,0:T(8,128)(2,1)S(1)} %copy-done.15), channel_id=1, source_target_pairs={{0,28},{4,24},{8,20},{12,16},{16,12},{20,8},{24,4},{28,0},{1,29},{... | collective-permute-start | bytes 393224 | tf_op jit(solution)/shard_map/ppermute | solution.py:410
  46.8 63.2 %collective-permute-start.14 = (bf16[512,128]{1,0:T(8,128)(2,1)S(1)}, bf16[512,128]{1,0:T(8,128)(2,1)S(1)}, u32[]{:S(2)}, u32[]{:S(2)}) collective-permute-start(bf16[512,128]{1,0:T(8,128)(2,1)S(1)} %copy-done.14), channel_id=1, source_target_pairs={{0,24},{4,28},{8,16},{12,20},{16,8},{20,12},{24,0},{28,4},{1,25},{... | collective-permute-start | bytes 393224 | tf_op jit(solution)/shard_map/ppermute | solution.py:410
  50.1 62.2 %collective-permute-start.15 = (bf16[512,128]{1,0:T(8,128)(2,1)S(1)}, bf16[512,128]{1,0:T(8,128)(2,1)S(1)}, u32[]{:S(2)}, u32[]{:S(2)}) collective-permute-start(bf16[512,128]{1,0:T(8,128)(2,1)S(1)} %copy-done.13), channel_id=1, source_target_pairs={{0,20},{4,16},{8,28},{12,24},{16,4},{20,0},{24,12},{28,8},{1,21},{... | collective-permute-start | bytes 393224 | tf_op jit(solution)/shard_map/ppermute | solution.py:410
  63.8 48.5 %collective-permute-start.16 = (bf16[512,128]{1,0:T(8,128)(2,1)S(1)}, bf16[512,128]{1,0:T(8,128)(2,1)S(1)}, u32[]{:S(2)}, u32[]{:S(2)}) collective-permute-start(bf16[512,128]{1,0:T(8,128)(2,1)S(1)} %copy-done.12), channel_id=1, source_target_pairs={{0,16},{4,20},{8,24},{12,28},{16,0},{20,4},{24,8},{28,12},{1,17},{... | collective-permute-start | bytes 393224 | tf_op jit(solution)/shard_map/ppermute | solution.py:410
  63.8 1.0 copy-start.2
  64.7 3.4 %copy-start.3 = (bf16[1024,128]{1,0:T(8,128)(2,1)S(1)}, bf16[1024,128]{1,0:T(8,128)(2,1)}, u32[]{:S(2)}) copy-start(bf16[1024,128]{1,0:T(8,128)(2,1)} %get-tuple-element.31.refs_0_.refs_4_) | copy-start | bytes 786436
  68.2 35.4 %copy-start.1 = (bf16[1024,128]{1,0:T(8,128)(2,1)S(1)}, bf16[1024,128]{1,0:T(8,128)(2,1)}, u32[]{:S(2)}) copy-start(bf16[1024,128]{1,0:T(8,128)(2,1)} %get-tuple-element.43.refs_0_.refs_4_) | copy-start | bytes 786436
  102.0 46.7 %collective-permute-start.7 = (bf16[512,128]{1,0:T(8,128)(2,1)S(1)}, bf16[512,128]{1,0:T(8,128)(2,1)S(1)}, u32[]{:S(2)}, u32[]{:S(2)}) collective-permute-start(bf16[512,128]{1,0:T(8,128)(2,1)S(1)} %get-tuple-element.40), channel_id=1, source_target_pairs={{0,4},{4,0},{8,12},{12,8},{16,20},{20,16},{24,28},{28,24},{1,5},{5... | collective-permute-start | bytes 393224 | tf_op jit(solution)/shard_map/ppermute | solution.py:410
  107.0 42.0 %collective-permute-start.8 = (bf16[512,128]{1,0:T(8,128)(2,1)S(1)}, bf16[512,128]{1,0:T(8,128)(2,1)S(1)}, u32[]{:S(2)}, u32[]{:S(2)}) collective-permute-start(bf16[512,128]{1,0:T(8,128)(2,1)S(1)} %get-tuple-element.41), channel_id=1, source_target_pairs={{0,8},{4,12},{8,0},{12,4},{16,24},{20,28},{24,16},{28,20},{1,9},{5... | collective-permute-start | bytes 393224 | tf_op jit(solution)/shard_map/ppermute | solution.py:410
  110.0 39.0 %collective-permute-start.9 = (bf16[512,128]{1,0:T(8,128)(2,1)S(1)}, bf16[512,128]{1,0:T(8,128)(2,1)S(1)}, u32[]{:S(2)}, u32[]{:S(2)}) collective-permute-start(bf16[512,128]{1,0:T(8,128)(2,1)S(1)} %get-tuple-element.42), channel_id=1, source_target_pairs={{0,12},{4,8},{8,4},{12,0},{16,28},{20,24},{24,20},{28,16},{1,13},{... | collective-permute-start | bytes 393224 | tf_op jit(solution)/shard_map/ppermute | solution.py:410
  112.3 36.7 %copy-start.7 = (s32[1,4,1]{1,2,0:T(1,128)S(1)}, s32[1,4,1]{1,2,0:T(1,128)}, u32[]{:S(2)}) copy-start(s32[1,4,1]{1,2,0:T(1,128)} %param.13) | copy-start | bytes 52
  112.3 36.8 %copy-start = (bf16[1024,1024]{1,0:T(8,128)(2,1)S(1)}, bf16[1024,1024]{1,0:T(8,128)(2,1)}, u32[]{:S(2)}) copy-start(bf16[1024,1024]{1,0:T(8,128)(2,1)} %w_out.3) | copy-start | bytes 6291460
  145.4 5.2 %collective-permute-start.17 = (bf16[512,128]{1,0:T(8,128)(2,1)}, bf16[512,128]{1,0:T(8,128)(2,1)S(1)}, u32[]{:S(2)}, u32[]{:S(2)}) collective-permute-start(bf16[512,128]{1,0:T(8,128)(2,1)} %get-tuple-element.52), channel_id=1, source_target_pairs={{0,4},{4,0},{8,12},{12,8},{16,20},{20,16},{24,28},{28,24},{1,5},{5... | collective-permute-start | bytes 393224 | tf_op jit(solution)/shard_map/ppermute | solution.py:410
  146.7 5.2 %collective-permute-start.18 = (bf16[512,128]{1,0:T(8,128)(2,1)}, bf16[512,128]{1,0:T(8,128)(2,1)S(1)}, u32[]{:S(2)}, u32[]{:S(2)}) collective-permute-start(bf16[512,128]{1,0:T(8,128)(2,1)} %get-tuple-element.53), channel_id=1, source_target_pairs={{0,8},{4,12},{8,0},{12,4},{16,24},{20,28},{24,16},{28,20},{1,9},{5... | collective-permute-start | bytes 393224 | tf_op jit(solution)/shard_map/ppermute | solution.py:410
  148.7 5.9 %collective-permute-start.19 = (bf16[512,128]{1,0:T(8,128)(2,1)S(1)}, bf16[512,128]{1,0:T(8,128)(2,1)S(1)}, u32[]{:S(2)}, u32[]{:S(2)}) collective-permute-start(bf16[512,128]{1,0:T(8,128)(2,1)S(1)} %get-tuple-element.54), channel_id=1, source_target_pairs={{0,12},{4,8},{8,4},{12,0},{16,28},{20,24},{24,20},{28,16},{1,13},{... | collective-permute-start | bytes 393224 | tf_op jit(solution)/shard_map/ppermute | solution.py:410
  149.0 5.5 %copy-start.4 = (f32[1024]{0:T(1024)S(1)}, f32[1024]{0:T(1024)}, u32[]{:S(2)}) copy-start(f32[1024]{0:T(1024)} %param.12) | copy-start | bytes 12292
  149.1 5.5 %copy-start.5 = (s32[1,4,128]{2,1,0:T(4,128)S(1)}, s32[1,4,128]{2,1,0:T(4,128)}, u32[]{:S(2)}) copy-start(s32[1,4,128]{2,1,0:T(4,128)} %param.15) | copy-start | bytes 6148
  149.1 5.5 %copy-start.6 = (s32[1,4]{1,0:T(1,128)S(1)}, s32[1,4]{1,0:T(1,128)}, u32[]{:S(2)}) copy-start(s32[1,4]{1,0:T(1,128)} %bases.1) | copy-start | bytes 52
  156.9 1.9 %collective-permute-start.20 = (bf16[32,1152]{1,0:T(8,128)(2,1)S(1)}, bf16[32,1152]{1,0:T(8,128)(2,1)S(1)}, u32[]{:S(2)}, u32[]{:S(2)}) collective-permute-start(bf16[32,1152]{1,0:T(8,128)(2,1)S(1)} %get-tuple-element.57), channel_id=1, source_target_pairs={{0,1},{1,0},{2,3},{3,2},{4,5},{5,4},{6,7},{7,6},{8,9},{9,8},{10,11... | collective-permute-start | bytes 221192 | tf_op jit(solution)/shard_map/ppermute | solution.py:410
  157.0 4.7 %collective-permute-start.21 = (bf16[32,1152]{1,0:T(8,128)(2,1)S(1)}, bf16[32,1152]{1,0:T(8,128)(2,1)S(1)}, u32[]{:S(2)}, u32[]{:S(2)}) collective-permute-start(bf16[32,1152]{1,0:T(8,128)(2,1)S(1)} %get-tuple-element.58), channel_id=1, source_target_pairs={{0,2},{1,3},{2,0},{3,1},{4,6},{5,7},{6,4},{7,5},{8,10},{9,11},{10,... | collective-permute-start | bytes 221192 | tf_op jit(solution)/shard_map/ppermute | solution.py:410
  158.6 4.4 %collective-permute-start.22 = (bf16[32,1152]{1,0:T(8,128)(2,1)S(1)}, bf16[32,1152]{1,0:T(8,128)(2,1)S(1)}, u32[]{:S(2)}, u32[]{:S(2)}) collective-permute-start(bf16[32,1152]{1,0:T(8,128)(2,1)S(1)} %get-tuple-element.59), channel_id=1, source_target_pairs={{0,3},{1,2},{2,1},{3,0},{4,7},{5,6},{6,5},{7,4},{8,11},{9,10},{10,... | collective-permute-start | bytes 221192 | tf_op jit(solution)/shard_map/ppermute | solution.py:410
